TPU v7x, 512 devices: a whole 4x4x16 slice. The times are simulated.
512 devices in a mesh: section: 8 (over z_hi, core), seq: 64 (over z_lo, y, x).
Axes of the slice: x: 4, y: 4, z: 16 (z_hi: 4, z_lo: 4; z = z_hi * 4 + z_lo), core: 2. Of those that a mesh axis runs over, the one named last changes fastest.
Arguments:
- bases: int32 [2, 32768], P(None, 'seq'), may hold values from 0 to 3
- stem_weight: bfloat16 [15, 4, 1536], replicated, may hold values from -1.5 to 1.5
- gains: bfloat16 [8, 1536], P('section'), may hold values from 0.099609375 to 1.8984375
- depth_taps: bfloat16 [8, 5, 1536], P('section'), may hold values from -2.5 to 2.5
- point_weight: bfloat16 [8, 1536, 1536], P('section', 'seq'), may hold values from -0.15625 to 0.15625
Outputs:
- encoded: bfloat16 [2, 128, 1536], P(None, 'seq', 'section')
All inputs are finite; a program needn't handle non-finite values.
Results may differ from a plain program's by a relative error of at most 0.015.
Values may be sent and summed in bfloat16 or wider, within the bound.
No kernel may reach another device: no remote copies, remote signals or barrier semaphores. Data moves between devices by JAX's collectives and lax.ppermute only.
A program may use at most 64 MiB of HBM per device.

v0:
```python
import jax
import jax.numpy as jnp
from jax import lax
from jax.experimental import pallas as pl
from jax.experimental.pallas import tpu as pltpu
from jax.sharding import Mesh
from jax.sharding import PartitionSpec as P


SEQ = ("zl", "y", "x")
SECTION = ("zh", "co")
C = 1536
HALF = C // 2
TAPS = 5
RUN = 1024
EDGE = 12
BLOCK = 96
SHIFTS = (0, 1, -1, 2)


def up16(rows):
    return -(-rows // 16) * 16


def activate(load, par_ref, a_scr, rows, edge, first, last):
    def step(i, carry):
        start = pl.multiple_of(i * 16, 16)
        left, right = load(start)
        squares = jnp.sum(left * left, axis=-1, keepdims=True)
        squares = squares + jnp.sum(right * right, axis=-1, keepdims=True)
        scale = lax.rsqrt(squares * (1.0 / C) + 1e-06)
        index = start + lax.broadcasted_iota(jnp.int32, (16, 1), 0)
        low = jnp.where(first == 1, edge, 0)
        high = jnp.where(last == 1, rows - edge, rows)
        inside = (index >= low) & (index < high)
        for side, part in enumerate((left, right)):
            lanes = pl.ds(side * HALF, HALF)
            value = part * scale * par_ref[0:1, lanes]
            value = jax.nn.gelu(value, approximate=True).astype(jnp.bfloat16)
            a_scr[pl.ds(start + 8, 16), lanes] = jnp.where(inside, value.astype(jnp.float32), 0.0)
        return carry

    lax.fori_loop(0, up16(rows) // 16, step, 0)


def spread(par_ref, a_scr, d_ref, rows):
    width = 384
    for lane in range(0, C, width):
        taps = [par_ref[1 + k : 2 + k, lane : lane + width] for k in range(TAPS)]

        def step(i, carry):
            start = pl.multiple_of(i * 16, 16)
            window = a_scr[pl.ds(start, 32), lane : lane + width]
            total = taps[0] * window[4:20]
            for k in range(1, TAPS):
                total = total + taps[k] * window[4 + 2 * k : 20 + 2 * k]
            d_ref[pl.ds(start, 16), lane : lane + width] = total.astype(jnp.bfloat16)
            return carry

        lax.fori_loop(0, up16(rows) // 16, step, 0)


def weight_copies(meta_ref, pieces, w_scr, sems):
    copies = []
    for p, piece in enumerate(pieces):
        for k in range(4):
            row = pl.multiple_of(meta_ref[3 + 4 * p + k] * BLOCK, 16)
            target = w_scr.at[pl.ds(row, BLOCK)]
            copies.append(pltpu.make_async_copy(piece.at[k], target, sems.at[4 * p + k]))
    return copies


def mix_and_pool(d_ref, w_scr, residual, y_scr, out_ref, rows, count):
    total = up16(rows)
    chunk = next(total // n for n in range(1, 99) if total % (16 * n) == 0 and total // n <= 272)
    for start in range(0, total, chunk):
        product = jnp.dot(
            d_ref[start : start + chunk], w_scr[...], preferred_element_type=jnp.float32
        )
        mixed = residual(start, chunk) + product
        for n in range(HALF // 128):
            y_scr[n, start : start + chunk] = mixed[:, 128 * n : 128 * n + 128]
    part = next(p for p in (128, 104, 64, 40, 16, 8, 4) if count % p == 0)
    for start in range(0, count, part):
        for n in range(HALF // 128):
            even = y_scr[n, pl.ds(4 + 2 * start, part, stride=2)]
            odd = y_scr[n, pl.ds(5 + 2 * start, part, stride=2)]
            pooled = jnp.maximum(even, odd).astype(jnp.bfloat16)
            out_ref[start : start + part, 128 * n : 128 * n + 128] = pooled


def first_half(rows, meta_ref, hot_ref, stem_ref, par_ref, x_ref, d_ref, x_scr, a_scr):
    chunk = 176
    for start in range(0, up16(rows), chunk):
        for side in range(2):
            x_scr[side, start : start + chunk] = jnp.dot(
                hot_ref[start : start + chunk],
                stem_ref[:, side * HALF : (side + 1) * HALF],
                preferred_element_type=jnp.float32,
            ).astype(jnp.bfloat16)

    def load(start):
        return [x_scr[side, pl.ds(start, 16)].astype(jnp.float32) for side in range(2)]

    activate(load, par_ref, a_scr, rows, EDGE, meta_ref[1], meta_ref[2])
    spread(par_ref, a_scr, d_ref, rows)
    x_ref[...] = x_scr[meta_ref[0]]


def second_half(rows, meta_ref, x_ref, d_ref, w0, w1, w2, w3, out_ref, w_scr, y_scr, sems):
    copies = weight_copies(meta_ref, (w0, w1, w2, w3), w_scr, sems)
    for copy in copies:
        copy.start()
    for copy in copies:
        copy.wait()

    def residual(start, chunk):
        return x_ref[start : start + chunk].astype(jnp.float32)

    mix_and_pool(d_ref, w_scr, residual, y_scr, out_ref, rows, (rows - 8) // 2)


def whole_level(
    rows, edge, meta_ref, x_refs, par_ref, w0, w1, w2, w3, out_ref, a_scr, d_scr, w_scr, y_scr, sems
):
    two = len(x_refs) == 2
    copies = weight_copies(meta_ref, (w0, w1, w2, w3), w_scr, sems)
    for copy in copies:
        copy.start()

    def load(start):
        if two:
            return [ref[pl.ds(start, 16)].astype(jnp.float32) for ref in x_refs]
        return [x_refs[0][side, pl.ds(start, 16)].astype(jnp.float32) for side in range(2)]

    activate(load, par_ref, a_scr, rows, edge, meta_ref[1], meta_ref[2])
    spread(par_ref, a_scr, d_scr, rows)
    for copy in copies:
        copy.wait()

    def residual(start, chunk):
        if two:
            return x_refs[0][start : start + chunk].astype(jnp.float32)
        return x_refs[0][meta_ref[0], start : start + chunk].astype(jnp.float32)

    mix_and_pool(d_scr, w_scr, residual, y_scr, out_ref, rows, (rows - 8) // 2)


def spec(memory_space=pltpu.VMEM):
    return pl.BlockSpec(memory_space=memory_space)


def out_rows(rows, last):
    return (rows - 8) // 2 if last else up16((rows - 8) // 2)


def run_first_half(rows, meta, hot, stem, par):
    size = up16(rows)
    return pl.pallas_call(
        lambda *refs: first_half(rows, *refs),
        in_specs=[spec(pltpu.SMEM), spec(), spec(), spec()],
        out_specs=[spec(), spec()],
        out_shape=[
            jax.ShapeDtypeStruct((size, HALF), jnp.bfloat16),
            jax.ShapeDtypeStruct((size, C), jnp.bfloat16),
        ],
        scratch_shapes=[
            pltpu.VMEM((2, size, HALF), jnp.bfloat16),
            pltpu.VMEM((size + 16, C), jnp.float32),
        ],
        name="stem_and_taps",
    )(meta, hot, stem, par)


def run_second_half(rows, meta, x, d, pieces):
    size = up16(rows)
    return pl.pallas_call(
        lambda *refs: second_half(rows, *refs),
        in_specs=[spec(pltpu.SMEM), spec(), spec()] + [spec(pl.ANY)] * 4,
        out_specs=spec(),
        out_shape=jax.ShapeDtypeStruct((out_rows(rows, False), HALF), jnp.bfloat16),
        scratch_shapes=[
            pltpu.VMEM((C, HALF), jnp.bfloat16),
            pltpu.VMEM((HALF // 128, size, 128), jnp.float32),
            pltpu.SemaphoreType.DMA((16,)),
        ],
        name="mix_first",
    )(meta, x, d, *pieces)


def run_level(rows, edge, last, meta, x, par, pieces):
    size = up16(rows)
    n = len(x)
    return pl.pallas_call(
        lambda meta_ref, *refs: whole_level(rows, edge, meta_ref, refs[:n], *refs[n:]),
        in_specs=[spec(pltpu.SMEM)] + [spec()] * (n + 1) + [spec(pl.ANY)] * 4,
        out_specs=spec(),
        out_shape=jax.ShapeDtypeStruct((out_rows(rows, last), HALF), jnp.bfloat16),
        scratch_shapes=[
            pltpu.VMEM((size + 16, C), jnp.float32),
            pltpu.VMEM((size, C), jnp.bfloat16),
            pltpu.VMEM((C, HALF), jnp.bfloat16),
            pltpu.VMEM((HALF // 128, size, 128), jnp.float32),
            pltpu.SemaphoreType.DMA((16,)),
        ],
    )(meta, *x, par, *pieces)


def ring(size, by):
    return [(i, (i + by) % size) for i in range(size)]


def around(array, axes, size):
    out = [array]
    for by in SHIFTS[1:]:
        out.append(lax.ppermute(array, axes, ring(size, by)))
    return out


def by_role(array, j):
    pairs = [
        (zs * 4 + x0, ((x0 - j) % 4) * 4 + zs) for zs in range(4) for x0 in range(4)
    ]
    return lax.ppermute(array, ("zh", "x"), pairs)


def flat(b, g, role):
    zh, zl, y = 2 * b + g % 2, g // 8, (g // 2) % 4
    return ((zh * 4 + zl) * 4 + y) * 4 + role


def gathered_bases(bases, sequence, before, count):
    mine = lax.dynamic_index_in_dim(bases + 1, sequence, 0, keepdims=False)
    parts = []
    for by in (-1, 0, 1, 2):
        pairs = []
        for zh in range(4):
            for row in range(16):
                place = 4 * row + 2 * (zh % 2) + by
                if 0 <= place < 64:
                    pairs.append((zh * 64 + place, zh * 64 + row * 4))
        parts.append(lax.ppermute(mine, ("zh", "zl", "y", "x"), pairs))
    return jnp.concatenate(parts)[mine.shape[0] - before :][:count]


def pass_on(array, role):
    rows = array.shape[0]
    axes = ("zh", "zl", "y", "x")
    up = [(flat(b, g, role), flat(b, g + 1, role + 1)) for b in range(2) for g in range(31)]
    down = [(flat(b, g + 1, role), flat(b, g, role + 1)) for b in range(2) for g in range(31)]
    before = lax.ppermute(array[rows - EDGE :], axes, up)
    after = lax.ppermute(array[:EDGE], axes, down)
    own = lax.ppermute(array, "x", [(role, role + 1)])
    blank = jnp.zeros((8, HALF), array.dtype)
    return jnp.concatenate([before, own, after, blank], axis=0)


def relay(bases, stem_weight, gains, depth_taps, point_weight):
    zh, co, zl, y, x = [lax.axis_index(name) for name in ("zh", "co", "zl", "y", "x")]
    margin = stem_weight.shape[0] // 2
    group = (zl * 4 + y) * 2 + zh % 2
    sequence = zh // 2

    params = jnp.concatenate(
        [gains, depth_taps[0], jnp.zeros((2, C), gains.dtype)], axis=0
    )
    params = by_role(lax.all_gather(params, "co"), 0).astype(jnp.float32)
    own = point_weight[0].reshape(-1, 2, HALF).transpose(1, 0, 2)
    own = lax.all_to_all(own, "co", 0, 0, tiled=True)
    turned = jnp.stack([by_role(own, j) for j in range(4)] * 2, axis=0)
    ordered = lax.dynamic_slice_in_dim(turned, (4 - zh) % 4, 4, 0)
    blocks = [ordered[:, slot].reshape(BLOCK, HALF) for slot in range(2)]
    along_z = around(blocks[0], ("zh", "zl"), 16)
    along_y = around(blocks[1], "y", 4)
    along_z, along_y = lax.optimization_barrier((jnp.stack(along_z), jnp.stack(along_y)))
    weights = [around(along_z, "y", 4), around(along_y, ("zh", "zl"), 16)]
    shift = jnp.array(SHIFTS, jnp.int32)
    z_of, y_of = (zl - shift) % 4, (y - shift) % 4
    places = [
        (z_of[None, :] * 4 + y_of[:, None]).reshape(-1),
        (z_of[:, None] * 4 + y_of[None, :]).reshape(-1),
    ]
    flags = jnp.stack([co, (group == 0).astype(jnp.int32), (group == 31).astype(jnp.int32)])
    metas = [jnp.concatenate([flags.astype(jnp.int32), place]) for place in places]
    own_first = jnp.concatenate([flags.astype(jnp.int32), (places[1] + 8 * co) % 16])
    swapped = jnp.concatenate([params[1][:, HALF:], params[1][:, :HALF]], axis=1)
    swapped = jnp.where(co == 0, params[1], swapped)

    rows = RUN + 2 * EDGE
    size = up16(rows)
    ids = gathered_bases(bases, sequence, EDGE + margin, size + 2 * margin)
    hot = (ids[:, None] == jnp.arange(1, 5, dtype=jnp.int32)[None, :]).astype(jnp.bfloat16)
    windows = [hot[k : k + size] for k in range(2 * margin + 1)]
    windows = jnp.concatenate(windows + [jnp.zeros((size, 4), jnp.bfloat16)], axis=1)
    stem = jnp.pad(stem_weight.reshape(-1, C), ((0, 4), (0, 0)))
    level_rows, taps = run_first_half(rows, metas[0], windows, stem, params[0])
    now = run_second_half(rows, metas[0], level_rows, taps, weights[0])
    other = lax.ppermute(now, "co", [(0, 1), (1, 0)])
    now = run_level(RUN // 2 + 8, 4, True, own_first, [now, other], swapped, weights[1])
    run = RUN // 4
    for role in range(3):
        now = lax.all_gather(pass_on(now, role), "co")
        now = run_level(run + 2 * EDGE, EDGE, False, metas[0], [now], params[0], weights[0])
        now = lax.all_gather(now, "co")
        now = run_level(run // 2 + 8, 4, True, metas[1], [now], params[1], weights[1])
        run = run // 4

    blocks = now.reshape(2, 2, 4, HALF // 4).transpose(2, 0, 1, 3)
    blocks = jnp.broadcast_to(
        blocks[None, :, None], (2, 4, 2, 2, 2, HALF // 4)
    ).reshape(32, 2, HALF // 4)
    got = lax.all_to_all(blocks, ("zh", "co", "x"), 0, 0, tiled=True)
    got = got.reshape(2, 2, 2, 4, 2, HALF // 4)[:, :, :, 3]
    got = lax.dynamic_index_in_dim(got, x // 2, 1, keepdims=False)
    return lax.dynamic_index_in_dim(got, zh // 2, 1, keepdims=False)


def solution(mesh):
    finer = Mesh(mesh.devices.reshape(4, 2, 4, 4, 4), SECTION + SEQ)
    in_specs = (
        P(None, SEQ),
        P(),
        P(SECTION, None),
        P(SECTION, None, None),
        P(SECTION, SEQ, None),
    )
    out_specs = P(None, SEQ, SECTION)
    return jax.shard_map(relay, mesh=finer, in_specs=in_specs, out_specs=out_specs, check_vma=False)
```

profile of v0, /device:TPU:17, one launch (start us, length us, event | category | flops | bytes accessed | tf_op | source)
XLA Modules:
  0.0 329.4 jit_solution(13551919266525104483)
XLA Ops:
  0.0 0.7 dynamic-slice_add_fusion
  0.7 1.3 collective-permute-start
  2.7 1.3 collective-permute-start.2
  4.0 1.3 collective-permute-start.3
  5.3 0.9 reshape_squeeze.9
  6.2 4.1 %all_to_all.10 = bf16[2,24,768]{2,1,0:T(8,128)(2,1)S(1)} all-to-all(bf16[2,24,768]{2,1,0:T(8,128)(2,1)S(1)} %bitcast.67), channel_id=1, replica_groups=mesh['zh'=4,'co'=2,'zl'=4,'y'=4,'x'=4] {'co'}, dimensions={0} | all-to-all | bytes 147456 | tf_op jit(solution)/shard_map/all_to_all | solution.py:269
  12.0 0.8 maximum_maximum_fusion
  14.0 29.9 %collective-permute-start.6 = (bf16[2,24,768]{2,1,0:T(8,128)(2,1)S(1)}, bf16[2,24,768]{2,1,0:T(8,128)(2,1)S(1)}, u32[]{:S(2)}, u32[]{:S(2)}) collective-permute-start(bf16[2,24,768]{2,1,0:T(8,128)(2,1)S(1)} %all_to_all.10), channel_id=1, source_target_pairs={{0,384},{1,0},{2,128},{3,256},{128,385},{129,1},{130,129},{131,257... | collective-permute-start | bytes 221192 | tf_op jit(solution)/shard_map/ppermute | solution.py:224
  44.0 3.8 %collective-permute-done.6 = bf16[2,24,768]{2,1,0:T(8,128)(2,1)S(1)} collective-permute-done((bf16[2,24,768]{2,1,0:T(8,128)(2,1)S(1)}, bf16[2,24,768]{2,1,0:T(8,128)(2,1)S(1)}, u32[]{:S(2)}, u32[]{:S(2)}) %collective-permute-start.6) | collective-permute-done | bytes 73760 | tf_op jit(solution)/shard_map/ppermute | solution.py:224
  47.8 10.3 %collective-permute-start.7 = (bf16[2,24,768]{2,1,0:T(8,128)(2,1)S(1)}, bf16[2,24,768]{2,1,0:T(8,128)(2,1)S(1)}, u32[]{:S(2)}, u32[]{:S(2)}) collective-permute-start(bf16[2,24,768]{2,1,0:T(8,128)(2,1)S(1)} %all_to_all.10), channel_id=1, source_target_pairs={{0,256},{1,384},{2,0},{3,128},{128,257},{129,385},{130,1},{131,129... | collective-permute-start | bytes 221192 | tf_op jit(solution)/shard_map/ppermute | solution.py:224
  58.1 1.4 collective-permute-done.7
  59.4 1.9 collective-permute-start.8
  61.4 4.4 %collective-permute-done.8 = bf16[2,24,768]{2,1,0:T(8,128)(2,1)S(1)} collective-permute-done((bf16[2,24,768]{2,1,0:T(8,128)(2,1)S(1)}, bf16[2,24,768]{2,1,0:T(8,128)(2,1)S(1)}, u32[]{:S(2)}, u32[]{:S(2)}) %collective-permute-start.8) | collective-permute-done | bytes 73760 | tf_op jit(solution)/shard_map/ppermute | solution.py:224
  65.8 3.1 collective-permute-start.12
  69.0 7.0 %all-gather = bf16[16,1536]{1,0:T(8,128)(2,1)S(1)} all-gather(bf16[8,1536]{1,0:T(8,128)(2,1)S(1)} %maximum_maximum_fusion), channel_id=2, replica_groups=mesh['zh'=4,'co'=2,'zl'=4,'y'=4,'x'=4] {'co'}, dimensions={0}, use_global_device_ids=true | all-gather | bytes 73728 | tf_op jit(solution)/shard_map/all_gather | solution.py:267
  76.0 1.0 reshape.36
  77.7 2.1 collective-permute-start.13
  79.8 3.2 collective-permute-start.14
  83.1 3.9 %collective-permute-start.9 = (bf16[96,768]{1,0:T(8,128)(2,1)S(1)}, bf16[96,768]{1,0:T(8,128)(2,1)S(1)}, u32[]{:S(2)}, u32[]{:S(2)}) collective-permute-start(bf16[96,768]{1,0:T(8,128)(2,1)S(1)} %bitcast.59), channel_id=1, source_target_pairs={{0,16},{16,32},{32,48},{48,128},{128,144},{144,160},{160,176},{176... | collective-permute-start | bytes 442376 | tf_op jit(solution)/shard_map/ppermute | solution.py:216
  87.0 8.5 %collective-permute-start.10 = (bf16[96,768]{1,0:T(8,128)(2,1)S(1)}, bf16[96,768]{1,0:T(8,128)(2,1)S(1)}, u32[]{:S(2)}, u32[]{:S(2)}) collective-permute-start(bf16[96,768]{1,0:T(8,128)(2,1)S(1)} %bitcast.60), channel_id=1, source_target_pairs={{0,432},{16,0},{32,16},{48,32},{128,48},{144,128},{160,144},{176,1... | collective-permute-start | bytes 442376 | tf_op jit(solution)/shard_map/ppermute | solution.py:216
  95.5 1.9 collective-permute-start.11
  97.7 1.3 collective-permute-start.4
  99.1 9.4 %collective-permute-done.11 = bf16[96,768]{1,0:T(8,128)(2,1)S(1)} collective-permute-done((bf16[96,768]{1,0:T(8,128)(2,1)S(1)}, bf16[96,768]{1,0:T(8,128)(2,1)S(1)}, u32[]{:S(2)}, u32[]{:S(2)}) %collective-permute-start.11) | collective-permute-done | bytes 147488 | tf_op jit(solution)/shard_map/ppermute | solution.py:216
  108.6 1.9 collective-permute-start.15
  110.5 3.4 %collective-permute-start.16 = (bf16[4,96,768]{2,1,0:T(8,128)(2,1)S(1)}, bf16[4,96,768]{2,1,0:T(8,128)(2,1)S(1)}, u32[]{:S(2)}, u32[]{:S(2)}) collective-permute-start(bf16[4,96,768]{2,1,0:T(8,128)(2,1)S(1)} %pad_maximum_fusion.refs_3_.refs_2_), channel_id=1, source_target_pairs={{0,12},{4,0},{8,4},{12,8},{1,13},{5,1},{9,5},{13,9},{2,14},{6,2},{... | collective-permute-start | bytes 1769480 | tf_op jit(solution)/shard_map/ppermute | solution.py:216
  113.9 3.8 %collective-permute-start.17 = (bf16[4,96,768]{2,1,0:T(8,128)(2,1)S(1)}, bf16[4,96,768]{2,1,0:T(8,128)(2,1)S(1)}, u32[]{:S(2)}, u32[]{:S(2)}) collective-permute-start(bf16[4,96,768]{2,1,0:T(8,128)(2,1)S(1)} %pad_maximum_fusion.refs_3_.refs_2_), channel_id=1, source_target_pairs={{0,8},{4,12},{8,0},{12,4},{1,9},{5,13},{9,1},{13,5},{2,10},{6,14},... | collective-permute-start | bytes 1769480 | tf_op jit(solution)/shard_map/ppermute | solution.py:216
  117.7 2.0 fusion.5
  119.8 4.9 %concatenate.37.refs_1_ = bf16[1056,64]{1,0:T(8,128)(2,1)} concatenate(bf16[1056,4]{1,0:T(8,128)(2,1)} %get-tuple-element.33, bf16[1056,4]{1,0:T(8,128)(2,1)} %get-tuple-element.32, bf16[1056,4]{1,0:T(8,128)(2,1)} %get-tuple-element.31, bf16[1056,4]{1,0:T(8,128)(2,1)} %get-tuple-element.30, bf16[1056,4]{1,0:T(8,128)(2,1)} %get-tuple-element.29, ...), dimensions={1} | concatenate | bytes 270336 | tf_op jit(solution)/shard_map/concatenate | solution.py:294
  124.7 0.8 convert_element_type.11
  126.2 21.0 %stem_and_taps.1 = (bf16[1056,768]{1,0:T(8,128)(2,1)}, bf16[1056,1536]{1,0:T(8,128)(2,1)}) custom-call(s32[19]{0:T(128)} %get-tuple-element.44.refs_0_.meta_ref, bf16[1056,64]{1,0:T(8,128)(2,1)} %concatenate.37.refs_1_, bf16[64,1536]{1,0:T(8,128)(2,1)} %pad.4.refs_2_, f32[8,1536]{1,0:T(8,128)} %get-tuple-element.37.refs_3_.refs_1_), custom_call_target="tpu_custom_call" | custom-call | tf_op jit(solution)/shard_map/stem_and_taps/pallas_call | solution.py:159
  147.2 0.8 copy-done.2
  148.5 8.0 %mix_first.1.refs_0_ = bf16[528,768]{1,0:T(8,128)(2,1)} custom-call(s32[19]{0:T(128)} %get-tuple-element.44.refs_0_.meta_ref, bf16[1056,768]{1,0:T(8,128)(2,1)} %get-tuple-element.9.refs_1_, bf16[1056,1536]{1,0:T(8,128)(2,1)} %get-tuple-element.10.refs_2_, bf16[4,96,768]{2,1,0:T(8,128)(2,1)} %copy-done.1, bf16[4,96,768]{2,1,0:T(8,128)(2,1)} %copy-done.2, ...), custom_call_target="tpu_custom_call" | custom-call | tf_op jit(solution)/shard_map/mix_first/pallas_call | solution.py:177
  156.5 4.4 %collective-permute-start.18 = (bf16[528,768]{1,0:T(8,128)(2,1)}, bf16[528,768]{1,0:T(8,128)(2,1)}, u32[]{:S(2)}, u32[]{:S(2)}) collective-permute-start(bf16[528,768]{1,0:T(8,128)(2,1)} %mix_first.1.refs_0_), channel_id=1, source_target_pairs={{0,64},{64,0},{1,65},{65,1},{2,66},{66,2},{3,67},{67,3},{4,68},{68... | collective-permute-start | bytes 2433032 | tf_op jit(solution)/shard_map/ppermute | solution.py:298
  160.9 1.9 collective-permute-start.19
  162.8 7.9 %collective-permute-start.20 = (bf16[4,96,768]{2,1,0:T(8,128)(2,1)S(1)}, bf16[4,96,768]{2,1,0:T(8,128)(2,1)S(1)}, u32[]{:S(2)}, u32[]{:S(2)}) collective-permute-start(bf16[4,96,768]{2,1,0:T(8,128)(2,1)S(1)} %pad_maximum_fusion.1.refs_3_.refs_2_), channel_id=1, source_target_pairs={{0,432},{16,0},{32,16},{48,32},{128,48},{144,128},{160,144},{176,1... | collective-permute-start | bytes 1769480 | tf_op jit(solution)/shard_map/ppermute | solution.py:216
  170.8 1.9 collective-permute-start.21
  173.3 9.2 %collective-permute-done.19.refs_4_.refs_3_ = bf16[4,96,768]{2,1,0:T(8,128)(2,1)S(1)} collective-permute-done((bf16[4,96,768]{2,1,0:T(8,128)(2,1)S(1)}, bf16[4,96,768]{2,1,0:T(8,128)(2,1)S(1)}, u32[]{:S(2)}, u32[]{:S(2)}) %collective-permute-start.19) | collective-permute-done | bytes 589856 | tf_op jit(solution)/shard_map/ppermute | solution.py:216
  182.5 0.9 collective-permute-done.20.refs_5_.refs_4_
  183.4 17.1 %collective-permute-done.21.refs_6_.refs_5_ = bf16[4,96,768]{2,1,0:T(8,128)(2,1)S(1)} collective-permute-done((bf16[4,96,768]{2,1,0:T(8,128)(2,1)S(1)}, bf16[4,96,768]{2,1,0:T(8,128)(2,1)S(1)}, u32[]{:S(2)}, u32[]{:S(2)}) %collective-permute-start.21) | collective-permute-done | bytes 589856 | tf_op jit(solution)/shard_map/ppermute | solution.py:216
  200.6 0.8 copy-done.7
  201.4 12.2 %shard_map.64 = bf16[256,768]{1,0:T(8,128)(2,1)} custom-call(s32[19]{0:T(128)} %get-tuple-element.13.meta_ref, bf16[528,768]{1,0:T(8,128)(2,1)} %mix_first.1.refs_0_, bf16[528,768]{1,0:T(8,128)(2,1)} %collective-permute-done.18.refs_1_, f32[8,1536]{1,0:T(8,128)} %maximum_select_fusion.refs_2_, bf16[4,96,768]{2,1,0:T(8,128)(2,1)} %copy-done, ...), custom_call_target="tpu_custom_call" | custom-call | tf_op jit(solution)/shard_map/pallas_call | solution.py:194
  213.6 1.6 collective-permute-start.23
  215.1 0.8 fusion.4
  215.9 3.6 %collective-permute-start.22 = (bf16[12,768]{1,0:T(8,128)(2,1)S(1)}, bf16[12,768]{1,0:T(8,128)(2,1)S(1)}, u32[]{:S(2)}, u32[]{:S(2)}) collective-permute-start(bf16[12,768]{1,0:T(8,128)(2,1)S(1)} %get-tuple-element.17), channel_id=1, source_target_pairs={{0,129},{128,5},{4,133},{132,9},{8,137},{136,13},{12,141},{140,17}... | collective-permute-start | bytes 55304 | tf_op jit(solution)/shard_map/ppermute | solution.py:251
  219.5 1.3 collective-permute-start.24
  220.8 0.9 collective-permute-done.24
  221.8 12.8 %all-gather.1 = bf16[576,768]{1,0:T(8,128)(2,1)} all-gather(bf16[288,768]{1,0:T(8,128)(2,1)S(1)} %pad_maximum_fusion.2), channel_id=3, replica_groups=mesh['zh'=4,'co'=2,'zl'=4,'y'=4,'x'=4] {'co'}, dimensions={0}, use_global_device_ids=true | all-gather | bytes 1327104 | tf_op jit(solution)/shard_map/all_gather | solution.py:302
  234.7 7.5 %shard_map.65 = bf16[144,768]{1,0:T(8,128)(2,1)} custom-call(s32[19]{0:T(128)} %get-tuple-element.44.refs_0_.meta_ref, bf16[2,288,768]{2,1,0:T(8,128)(2,1)} %bitcast.54, f32[8,1536]{1,0:T(8,128)} %get-tuple-element.37.refs_3_.refs_1_, bf16[4,96,768]{2,1,0:T(8,128)(2,1)} %copy-done.1, bf16[4,96,768]{2,1,0:T(8,128)(2,1)} %copy-done.2, ...), custom_call_target="tpu_custom_call" | custom-call | tf_op jit(solution)/shard_map/pallas_call | solution.py:194
  242.2 4.0 %all-gather.2 = bf16[288,768]{1,0:T(8,128)(2,1)} all-gather(bf16[144,768]{1,0:T(8,128)(2,1)} %shard_map.65), channel_id=4, replica_groups=mesh['zh'=4,'co'=2,'zl'=4,'y'=4,'x'=4] {'co'}, dimensions={0}, use_global_device_ids=true | all-gather | bytes 663552 | tf_op jit(solution)/shard_map/all_gather | solution.py:304
  246.2 4.7 %shard_map.66 = bf16[64,768]{1,0:T(8,128)(2,1)} custom-call(s32[19]{0:T(128)} %get-tuple-element.45.meta_ref, bf16[2,144,768]{2,1,0:T(8,128)(2,1)} %bitcast.55, f32[8,1536]{1,0:T(8,128)} %copy-done.8, bf16[4,96,768]{2,1,0:T(8,128)(2,1)} %copy-done, bf16[4,96,768]{2,1,0:T(8,128)(2,1)} %copy-done.5, bf16[4,96,768]{2,1,0:T(8,128)(2,1)} %copy-done.6, ...), custom_call_target="tpu_custom_call" | custom-call | tf_op jit(solution)/shard_map/pallas_call | solution.py:194
  251.5 0.8 fusion.6
  253.0 0.8 collective-permute-start.27
  253.9 2.1 all-gather.3
  256.1 4.0 %shard_map.67 = bf16[48,768]{1,0:T(8,128)(2,1)} custom-call(s32[19]{0:T(128)} %get-tuple-element.44.refs_0_.meta_ref, bf16[2,96,768]{2,1,0:T(8,128)(2,1)} %bitcast.56, f32[8,1536]{1,0:T(8,128)} %get-tuple-element.37.refs_3_.refs_1_, bf16[4,96,768]{2,1,0:T(8,128)(2,1)} %copy-done.1, bf16[4,96,768]{2,1,0:T(8,128)(2,1)} %copy-done.2, ...), custom_call_target="tpu_custom_call" | custom-call | tf_op jit(solution)/shard_map/pallas_call | solution.py:194
  260.0 3.4 %all-gather.4 = bf16[96,768]{1,0:T(8,128)(2,1)} all-gather(bf16[48,768]{1,0:T(8,128)(2,1)} %shard_map.67), channel_id=6, replica_groups=mesh['zh'=4,'co'=2,'zl'=4,'y'=4,'x'=4] {'co'}, dimensions={0}, use_global_device_ids=true | all-gather | bytes 221184 | tf_op jit(solution)/shard_map/all_gather | solution.py:304
  263.5 3.9 %shard_map.68 = bf16[16,768]{1,0:T(8,128)(2,1)} custom-call(s32[19]{0:T(128)} %get-tuple-element.45.meta_ref, bf16[2,48,768]{2,1,0:T(8,128)(2,1)} %bitcast.58, f32[8,1536]{1,0:T(8,128)} %copy-done.8, bf16[4,96,768]{2,1,0:T(8,128)(2,1)} %copy-done, bf16[4,96,768]{2,1,0:T(8,128)(2,1)} %copy-done.5, bf16[4,96,768]{2,1,0:T(8,128)(2,1)} %copy-done.6, ...), custom_call_target="tpu_custom_call" | custom-call | tf_op jit(solution)/shard_map/pallas_call | solution.py:194
  268.0 0.8 fusion.8
  270.3 2.0 all-gather.5
  272.3 3.9 %shard_map.69 = bf16[16,768]{1,0:T(8,128)(2,1)} custom-call(s32[19]{0:T(128)} %get-tuple-element.44.refs_0_.meta_ref, bf16[2,48,768]{2,1,0:T(8,128)(2,1)} %bitcast.57, f32[8,1536]{1,0:T(8,128)} %get-tuple-element.37.refs_3_.refs_1_, bf16[4,96,768]{2,1,0:T(8,128)(2,1)} %copy-done.1, bf16[4,96,768]{2,1,0:T(8,128)(2,1)} %copy-done.2, ...), custom_call_target="tpu_custom_call" | custom-call | tf_op jit(solution)/shard_map/pallas_call | solution.py:194
  276.2 3.4 %all-gather.6 = bf16[32,768]{1,0:T(8,128)(2,1)} all-gather(bf16[16,768]{1,0:T(8,128)(2,1)} %shard_map.69), channel_id=8, replica_groups=mesh['zh'=4,'co'=2,'zl'=4,'y'=4,'x'=4] {'co'}, dimensions={0}, use_global_device_ids=true | all-gather | bytes 73728 | tf_op jit(solution)/shard_map/all_gather | solution.py:304
  279.6 3.7 %shard_map.70 = bf16[4,768]{1,0:T(4,128)(2,1)} custom-call(s32[19]{0:T(128)} %get-tuple-element.45.meta_ref, bf16[2,16,768]{2,1,0:T(8,128)(2,1)} %bitcast.68, f32[8,1536]{1,0:T(8,128)} %copy-done.8, bf16[4,96,768]{2,1,0:T(8,128)(2,1)} %copy-done, bf16[4,96,768]{2,1,0:T(8,128)(2,1)} %copy-done.5, bf16[4,96,768]{2,1,0:T(8,128)(2,1)} %copy-done.6, ...), custom_call_target="tpu_custom_call" | custom-call | tf_op jit(solution)/shard_map/pallas_call | solution.py:194
  283.3 0.8 reshape.37
  284.7 29.6 %all-to-all-start.1 = ((bf16[32,2,192]{2,1,0:T(2,128)(2,1)}), bf16[32,2,192]{2,1,0:T(2,128)(2,1)S(1)}, u32[]{:S(2)}, u32[]{:S(2)}) async-start(bf16[32,2,192]{2,1,0:T(2,128)(2,1)} %bitcast.33), calls=%async_computation.1 | async-start | bytes 65536 | tf_op jit(solution)/shard_map/all_to_all | solution.py:312
  314.4 14.4 %all-to-all-done.1 = bf16[32,2,192]{2,1,0:T(2,128)(2,1)S(1)} async-done(((bf16[32,2,192]{2,1,0:T(2,128)(2,1)}), bf16[32,2,192]{2,1,0:T(2,128)(2,1)S(1)}, u32[]{:S(2)}, u32[]{:S(2)}) %all-to-all-start.1) | async-done | bytes 24608 | tf_op jit(solution)/shard_map/all_to_all | solution.py:312
  (83 shorter events, 11.3 us)
Async XLA Ops:
  0.7 76.9 %collective-permute-start = (s32[512]{0:T(512)S(1)}, s32[512]{0:T(512)S(1)}, u32[]{:S(2)}, u32[]{:S(2)}) collective-permute-start(s32[512]{0:T(512)S(1)} %bitcast.79), channel_id=1, source_target_pairs={{3,4},{7,8},{11,12},{15,16},{19,20},{23,24},{27,28},{31,32},{35,36... | collective-permute-start | bytes 6152 | tf_op jit(solution)/shard_map/ppermute | solution.py:242
  2.0 75.7 %collective-permute-start.1 = (s32[512]{0:T(512)S(1)}, s32[512]{0:T(512)S(1)}, u32[]{:S(2)}, u32[]{:S(2)}) collective-permute-start(s32[512]{0:T(512)S(1)} %bitcast.80), channel_id=1, source_target_pairs={{0,0},{4,4},{8,8},{12,12},{16,16},{20,20},{24,24},{28,28},{32,32},... | collective-permute-start | bytes 6152 | tf_op jit(solution)/shard_map/ppermute | solution.py:242
  2.7 75.0 %collective-permute-start.2 = (s32[512]{0:T(512)S(1)}, s32[512]{0:T(512)S(1)}, u32[]{:S(2)}, u32[]{:S(2)}) collective-permute-start(s32[512]{0:T(512)S(1)} %bitcast.81), channel_id=1, source_target_pairs={{1,0},{5,4},{9,8},{13,12},{17,16},{21,20},{25,24},{29,28},{33,32},... | collective-permute-start | bytes 6152 | tf_op jit(solution)/shard_map/ppermute | solution.py:242
  4.0 73.7 %collective-permute-start.3 = (s32[512]{0:T(512)S(1)}, s32[512]{0:T(512)S(1)}, u32[]{:S(2)}, u32[]{:S(2)}) collective-permute-start(s32[512]{0:T(512)S(1)} %bitcast.82), channel_id=1, source_target_pairs={{2,0},{6,4},{10,8},{14,12},{18,16},{22,20},{26,24},{30,28},{34,32}... | collective-permute-start | bytes 6152 | tf_op jit(solution)/shard_map/ppermute | solution.py:242
  10.3 3.8 %collective-permute-start.5 = (bf16[2,24,768]{2,1,0:T(8,128)(2,1)S(1)}, bf16[2,24,768]{2,1,0:T(8,128)(2,1)S(1)}, u32[]{:S(2)}, u32[]{:S(2)}) collective-permute-start(bf16[2,24,768]{2,1,0:T(8,128)(2,1)S(1)} %all_to_all.10), channel_id=1, source_target_pairs={{0,0},{1,128},{2,256},{3,384},{128,1},{129,129},{130,257},{131,385... | collective-permute-start | bytes 221192 | tf_op jit(solution)/shard_map/ppermute | solution.py:224
  14.0 33.7 %collective-permute-start.6 = (bf16[2,24,768]{2,1,0:T(8,128)(2,1)S(1)}, bf16[2,24,768]{2,1,0:T(8,128)(2,1)S(1)}, u32[]{:S(2)}, u32[]{:S(2)}) collective-permute-start(bf16[2,24,768]{2,1,0:T(8,128)(2,1)S(1)} %all_to_all.10), channel_id=1, source_target_pairs={{0,384},{1,0},{2,128},{3,256},{128,385},{129,1},{130,129},{131,257... | collective-permute-start | bytes 221192 | tf_op jit(solution)/shard_map/ppermute | solution.py:224
  47.8 11.7 %collective-permute-start.7 = (bf16[2,24,768]{2,1,0:T(8,128)(2,1)S(1)}, bf16[2,24,768]{2,1,0:T(8,128)(2,1)S(1)}, u32[]{:S(2)}, u32[]{:S(2)}) collective-permute-start(bf16[2,24,768]{2,1,0:T(8,128)(2,1)S(1)} %all_to_all.10), channel_id=1, source_target_pairs={{0,256},{1,384},{2,0},{3,128},{128,257},{129,385},{130,1},{131,129... | collective-permute-start | bytes 221192 | tf_op jit(solution)/shard_map/ppermute | solution.py:224
  59.4 6.3 %collective-permute-start.8 = (bf16[2,24,768]{2,1,0:T(8,128)(2,1)S(1)}, bf16[2,24,768]{2,1,0:T(8,128)(2,1)S(1)}, u32[]{:S(2)}, u32[]{:S(2)}) collective-permute-start(bf16[2,24,768]{2,1,0:T(8,128)(2,1)S(1)} %all_to_all.10), channel_id=1, source_target_pairs={{0,128},{1,256},{2,384},{3,0},{128,129},{129,257},{130,385},{131,1... | collective-permute-start | bytes 221192 | tf_op jit(solution)/shard_map/ppermute | solution.py:224
  65.8 29.7 %collective-permute-start.12 = (bf16[96,768]{1,0:T(8,128)(2,1)S(1)}, bf16[96,768]{1,0:T(8,128)(2,1)S(1)}, u32[]{:S(2)}, u32[]{:S(2)}) collective-permute-start(bf16[96,768]{1,0:T(8,128)(2,1)S(1)} %bitcast.63), channel_id=1, source_target_pairs={{0,4},{4,8},{8,12},{12,0},{1,5},{5,9},{9,13},{13,1},{2,6},{6,10},{... | collective-permute-start | bytes 442376 | tf_op jit(solution)/shard_map/ppermute | solution.py:216
  77.7 20.0 %collective-permute-start.13 = (bf16[96,768]{1,0:T(8,128)(2,1)S(1)}, bf16[96,768]{1,0:T(8,128)(2,1)S(1)}, u32[]{:S(2)}, u32[]{:S(2)}) collective-permute-start(bf16[96,768]{1,0:T(8,128)(2,1)S(1)} %bitcast.64), channel_id=1, source_target_pairs={{0,12},{4,0},{8,4},{12,8},{1,13},{5,1},{9,5},{13,9},{2,14},{6,2},{... | collective-permute-start | bytes 442376 | tf_op jit(solution)/shard_map/ppermute | solution.py:216
  79.8 19.1 %collective-permute-start.14 = (bf16[96,768]{1,0:T(8,128)(2,1)S(1)}, bf16[96,768]{1,0:T(8,128)(2,1)S(1)}, u32[]{:S(2)}, u32[]{:S(2)}) collective-permute-start(bf16[96,768]{1,0:T(8,128)(2,1)S(1)} %bitcast.65), channel_id=1, source_target_pairs={{0,8},{4,12},{8,0},{12,4},{1,9},{5,13},{9,1},{13,5},{2,10},{6,14},... | collective-permute-start | bytes 442376 | tf_op jit(solution)/shard_map/ppermute | solution.py:216
  83.1 16.0 %collective-permute-start.9 = (bf16[96,768]{1,0:T(8,128)(2,1)S(1)}, bf16[96,768]{1,0:T(8,128)(2,1)S(1)}, u32[]{:S(2)}, u32[]{:S(2)}) collective-permute-start(bf16[96,768]{1,0:T(8,128)(2,1)S(1)} %bitcast.59), channel_id=1, source_target_pairs={{0,16},{16,32},{32,48},{48,128},{128,144},{144,160},{160,176},{176... | collective-permute-start | bytes 442376 | tf_op jit(solution)/shard_map/ppermute | solution.py:216
  87.0 12.1 %collective-permute-start.10 = (bf16[96,768]{1,0:T(8,128)(2,1)S(1)}, bf16[96,768]{1,0:T(8,128)(2,1)S(1)}, u32[]{:S(2)}, u32[]{:S(2)}) collective-permute-start(bf16[96,768]{1,0:T(8,128)(2,1)S(1)} %bitcast.60), channel_id=1, source_target_pairs={{0,432},{16,0},{32,16},{48,32},{128,48},{144,128},{160,144},{176,1... | collective-permute-start | bytes 442376 | tf_op jit(solution)/shard_map/ppermute | solution.py:216
  95.5 12.9 %collective-permute-start.11 = (bf16[96,768]{1,0:T(8,128)(2,1)S(1)}, bf16[96,768]{1,0:T(8,128)(2,1)S(1)}, u32[]{:S(2)}, u32[]{:S(2)}) collective-permute-start(bf16[96,768]{1,0:T(8,128)(2,1)S(1)} %bitcast.61), channel_id=1, source_target_pairs={{0,32},{16,48},{32,128},{48,144},{128,160},{144,176},{160,256},{17... | collective-permute-start | bytes 442376 | tf_op jit(solution)/shard_map/ppermute | solution.py:216
  97.7 27.0 %collective-permute-start.4 = (bf16[2,8,1536]{2,1,0:T(8,128)(2,1)S(1)}, bf16[2,8,1536]{2,1,0:T(8,128)(2,1)}, u32[]{:S(2)}, u32[]{:S(2)}) collective-permute-start(bf16[2,8,1536]{2,1,0:T(8,128)(2,1)S(1)} %bitcast.76), channel_id=1, source_target_pairs={{0,0},{1,128},{2,256},{3,384},{128,1},{129,129},{130,257},{131,385... | collective-permute-start | bytes 147464 | tf_op jit(solution)/shard_map/ppermute | solution.py:224
  99.0 71.7 %copy-start = (bf16[4,96,768]{2,1,0:T(8,128)(2,1)}, bf16[4,96,768]{2,1,0:T(8,128)(2,1)S(1)}, u32[]{:S(2)}) copy-start(bf16[4,96,768]{2,1,0:T(8,128)(2,1)S(1)} %pad_maximum_fusion.1.refs_3_.refs_2_) | copy-start | bytes 1769476
  108.6 11.2 %copy-start.1 = (bf16[4,96,768]{2,1,0:T(8,128)(2,1)}, bf16[4,96,768]{2,1,0:T(8,128)(2,1)S(1)}, u32[]{:S(2)}) copy-start(bf16[4,96,768]{2,1,0:T(8,128)(2,1)S(1)} %pad_maximum_fusion.refs_3_.refs_2_) | copy-start | bytes 1769476
  108.6 38.6 %collective-permute-start.15 = (bf16[4,96,768]{2,1,0:T(8,128)(2,1)S(1)}, bf16[4,96,768]{2,1,0:T(8,128)(2,1)S(1)}, u32[]{:S(2)}, u32[]{:S(2)}) collective-permute-start(bf16[4,96,768]{2,1,0:T(8,128)(2,1)S(1)} %pad_maximum_fusion.refs_3_.refs_2_), channel_id=1, source_target_pairs={{0,4},{4,8},{8,12},{12,0},{1,5},{5,9},{9,13},{13,1},{2,6},{6,10},{... | collective-permute-start | bytes 1769480 | tf_op jit(solution)/shard_map/ppermute | solution.py:216
  110.5 36.7 %collective-permute-start.16 = (bf16[4,96,768]{2,1,0:T(8,128)(2,1)S(1)}, bf16[4,96,768]{2,1,0:T(8,128)(2,1)S(1)}, u32[]{:S(2)}, u32[]{:S(2)}) collective-permute-start(bf16[4,96,768]{2,1,0:T(8,128)(2,1)S(1)} %pad_maximum_fusion.refs_3_.refs_2_), channel_id=1, source_target_pairs={{0,12},{4,0},{8,4},{12,8},{1,13},{5,1},{9,5},{13,9},{2,14},{6,2},{... | collective-permute-start | bytes 1769480 | tf_op jit(solution)/shard_map/ppermute | solution.py:216
  113.9 33.4 %collective-permute-start.17 = (bf16[4,96,768]{2,1,0:T(8,128)(2,1)S(1)}, bf16[4,96,768]{2,1,0:T(8,128)(2,1)S(1)}, u32[]{:S(2)}, u32[]{:S(2)}) collective-permute-start(bf16[4,96,768]{2,1,0:T(8,128)(2,1)S(1)} %pad_maximum_fusion.refs_3_.refs_2_), channel_id=1, source_target_pairs={{0,8},{4,12},{8,0},{12,4},{1,9},{5,13},{9,1},{13,5},{2,10},{6,14},... | collective-permute-start | bytes 1769480 | tf_op jit(solution)/shard_map/ppermute | solution.py:216
  126.2 46.5 %copy-start.8 = (f32[8,1536]{1,0:T(8,128)}, f32[8,1536]{1,0:T(8,128)S(1)}, u32[]{:S(2)}) copy-start(f32[8,1536]{1,0:T(8,128)S(1)} %get-tuple-element.36.refs_1_) | copy-start | bytes 147460
  147.2 0.8 copy-start.2
  147.2 1.1 copy-start.3
  147.2 1.2 copy-start.4
  156.5 44.1 %collective-permute-start.18 = (bf16[528,768]{1,0:T(8,128)(2,1)}, bf16[528,768]{1,0:T(8,128)(2,1)}, u32[]{:S(2)}, u32[]{:S(2)}) collective-permute-start(bf16[528,768]{1,0:T(8,128)(2,1)} %mix_first.1.refs_0_), channel_id=1, source_target_pairs={{0,64},{64,0},{1,65},{65,1},{2,66},{66,2},{3,67},{67,3},{4,68},{68... | collective-permute-start | bytes 2433032 | tf_op jit(solution)/shard_map/ppermute | solution.py:298
  160.9 21.6 %collective-permute-start.19 = (bf16[4,96,768]{2,1,0:T(8,128)(2,1)S(1)}, bf16[4,96,768]{2,1,0:T(8,128)(2,1)S(1)}, u32[]{:S(2)}, u32[]{:S(2)}) collective-permute-start(bf16[4,96,768]{2,1,0:T(8,128)(2,1)S(1)} %pad_maximum_fusion.1.refs_3_.refs_2_), channel_id=1, source_target_pairs={{0,16},{16,32},{32,48},{48,128},{128,144},{144,160},{160,176},{176... | collective-permute-start | bytes 1769480 | tf_op jit(solution)/shard_map/ppermute | solution.py:216
  162.8 20.6 %collective-permute-start.20 = (bf16[4,96,768]{2,1,0:T(8,128)(2,1)S(1)}, bf16[4,96,768]{2,1,0:T(8,128)(2,1)S(1)}, u32[]{:S(2)}, u32[]{:S(2)}) collective-permute-start(bf16[4,96,768]{2,1,0:T(8,128)(2,1)S(1)} %pad_maximum_fusion.1.refs_3_.refs_2_), channel_id=1, source_target_pairs={{0,432},{16,0},{32,16},{48,32},{128,48},{144,128},{160,144},{176,1... | collective-permute-start | bytes 1769480 | tf_op jit(solution)/shard_map/ppermute | solution.py:216
  170.8 29.8 %collective-permute-start.21 = (bf16[4,96,768]{2,1,0:T(8,128)(2,1)S(1)}, bf16[4,96,768]{2,1,0:T(8,128)(2,1)S(1)}, u32[]{:S(2)}, u32[]{:S(2)}) collective-permute-start(bf16[4,96,768]{2,1,0:T(8,128)(2,1)S(1)} %pad_maximum_fusion.1.refs_3_.refs_2_), channel_id=1, source_target_pairs={{0,32},{16,48},{32,128},{48,144},{128,160},{144,176},{160,256},{17... | collective-permute-start | bytes 1769480 | tf_op jit(solution)/shard_map/ppermute | solution.py:216
  182.5 18.1 %copy-start.5 = (bf16[4,96,768]{2,1,0:T(8,128)(2,1)}, bf16[4,96,768]{2,1,0:T(8,128)(2,1)S(1)}, u32[]{:S(2)}) copy-start(bf16[4,96,768]{2,1,0:T(8,128)(2,1)S(1)} %collective-permute-done.19.refs_4_.refs_3_) | copy-start | bytes 1769476
  183.4 17.2 %copy-start.6 = (bf16[4,96,768]{2,1,0:T(8,128)(2,1)}, bf16[4,96,768]{2,1,0:T(8,128)(2,1)S(1)}, u32[]{:S(2)}) copy-start(bf16[4,96,768]{2,1,0:T(8,128)(2,1)S(1)} %collective-permute-done.20.refs_5_.refs_4_) | copy-start | bytes 1769476
  200.5 0.8 copy-start.7
  213.6 8.2 %collective-permute-start.23 = (bf16[256,768]{1,0:T(8,128)(2,1)}, bf16[256,768]{1,0:T(8,128)(2,1)S(1)}, u32[]{:S(2)}, u32[]{:S(2)}) collective-permute-start(bf16[256,768]{1,0:T(8,128)(2,1)} %shard_map.64), channel_id=1, source_target_pairs={{0,1},{4,5},{8,9},{12,13},{16,17},{20,21},{24,25},{28,29},{32,33},... | collective-permute-start | bytes 1179656 | tf_op jit(solution)/shard_map/ppermute | solution.py:253
  215.9 4.9 %collective-permute-start.22 = (bf16[12,768]{1,0:T(8,128)(2,1)S(1)}, bf16[12,768]{1,0:T(8,128)(2,1)S(1)}, u32[]{:S(2)}, u32[]{:S(2)}) collective-permute-start(bf16[12,768]{1,0:T(8,128)(2,1)S(1)} %get-tuple-element.17), channel_id=1, source_target_pairs={{0,129},{128,5},{4,133},{132,9},{8,137},{136,13},{12,141},{140,17}... | collective-permute-start | bytes 55304 | tf_op jit(solution)/shard_map/ppermute | solution.py:251
  219.5 2.2 collective-permute-start.24
  250.9 3.0 collective-permute-start.26
  252.3 1.5 collective-permute-start.25
  253.0 0.9 collective-permute-start.27
  267.4 2.9 collective-permute-start.29
  268.9 1.3 collective-permute-start.28
  269.5 0.7 collective-permute-start.30
  284.7 44.0 %all-to-all-start.1 = ((bf16[32,2,192]{2,1,0:T(2,128)(2,1)}), bf16[32,2,192]{2,1,0:T(2,128)(2,1)S(1)}, u32[]{:S(2)}, u32[]{:S(2)}) async-start(bf16[32,2,192]{2,1,0:T(2,128)(2,1)} %bitcast.33), calls=%async_computation.1 | async-start | bytes 65536 | tf_op jit(solution)/shard_map/all_to_all | solution.py:312
where the time goes:
time: 332 us; the launch traced here: 329 us
  starting transfers between devices  137 us (41%)
  Pallas kernels  68.9 us (21%)
  waiting for transfers between devices  61.5 us (19%)
  blocking collectives  38.9 us (12%)
  local copies, waits for them, and re-layouts  17 us (5%)
  other arithmetic  5.57 us (2%)
    ppermute x5, starting transfers between devices, by_role(): return lax.ppermute(array, ('zh', 'x'), pairs)  44 us
    ppermute x12, starting transfers between devices, around(): out.append(lax.ppermute(array, axes, ring(size, by)))  43.7 us
    pallas_call x7, Pallas kernels, run_level(): pl.pallas_call(lambda meta_ref, *refs: whole_level(rows, edge, meta_ref,...  39.9 us
    ppermute x12, waiting for transfers between devices, around(): out.append(lax.ppermute(array, axes, ring(size, by)))  36.6 us
    all_to_all x1, starting transfers between devices, relay(): got = lax.all_to_all(blocks, ('zh', 'co', 'x'), 0, 0, tiled=True)  29.6 us
    pallas_call x1, Pallas kernels, run_first_half(): pl.pallas_call(lambda *refs: first_half(rows, *refs), in_specs=[spec(pltp...  21 us
    all_gather x3, blocking collectives, relay(): now = lax.all_gather(pass_on(now, role), 'co')  17 us
    all_to_all x1, waiting for transfers between devices, relay(): got = lax.all_to_all(blocks, ('zh', 'co', 'x'), 0, 0, tiled=True)  14.4 us
  transfers between devices with their start and end apart: 32, of which 9 were waited for; matrix products, arithmetic and copies ran while one was open for 5% of the time, Pallas kernels for 6%

commit v1 on v0

v1 whole, which is shorter than its diff:
```python
import jax
import jax.numpy as jnp
from jax import lax
from jax.experimental import pallas as pl
from jax.experimental.pallas import tpu as pltpu
from jax.sharding import Mesh
from jax.sharding import PartitionSpec as P


SEQ = ("zl", "y", "x")
SECTION = ("zh", "co")
C = 1536
HALF = C // 2
TAPS = 5
RUN = 1024
EDGE = 12
BLOCK = 96
SHIFTS = (0, 1, -1, 2)
TILES = HALF // 128
GELU = 0.7978845608028654


def up16(rows):
    return -(-rows // 16) * 16


def even_chunk(rows, most):
    total = up16(rows)
    return next(total // n for n in range(1, 99) if total % (16 * n) == 0 and total // n <= most)


def activate(load, par_ref, a_scr, rows, edge, meta_ref):
    def step(i, carry):
        start = pl.multiple_of(i * 16, 16)
        parts = load(start)
        squares = jnp.sum(parts[0] * parts[0] + parts[1] * parts[1], axis=-1, keepdims=True)
        scale = lax.rsqrt(squares * (1.0 / C) + 1e-06)
        for side, part in enumerate(parts):
            value = part * scale * par_ref[0:1, side * HALF : (side + 1) * HALF]
            bent = jnp.tanh(value * (GELU + (GELU * 0.044715) * (value * value)))
            half = 0.5 * value
            value = (half + half * bent).astype(jnp.bfloat16).astype(jnp.float32)
            for t in range(TILES):
                tile = value[:, 128 * t : 128 * t + 128]
                a_scr[side * TILES + t, pl.ds(start + 8, 16)] = tile
        return carry

    lax.fori_loop(0, up16(rows) // 16, step, 0)

    @pl.when(meta_ref[1] == 1)
    def _():
        for t in range(2 * TILES):
            a_scr[t, 8 : 8 + edge] = jnp.zeros((edge, 128), jnp.float32)

    @pl.when(meta_ref[2] == 1)
    def _():
        for t in range(2 * TILES):
            a_scr[t, 8 + rows - edge : 8 + rows] = jnp.zeros((edge, 128), jnp.float32)


def spread(par_ref, a_scr, d_ref, rows):
    chunk = even_chunk(rows, 176)
    for t in range(2 * TILES):
        lanes = slice(128 * t, 128 * t + 128)
        taps = [par_ref[1 + k : 2 + k, lanes] for k in range(TAPS)]

        def step(i, carry):
            start = pl.multiple_of(i * chunk, 16)
            total = taps[0] * a_scr[t, pl.ds(start + 4, chunk)]
            for k in range(1, TAPS):
                total = total + taps[k] * a_scr[t, pl.ds(start + 4 + 2 * k, chunk)]
            d_ref[pl.ds(start, chunk), lanes] = total.astype(jnp.bfloat16)
            return carry

        lax.fori_loop(0, up16(rows) // chunk, step, 0)


def weight_copies(meta_ref, pieces, w_ref, sems):
    copies = []
    for piece in pieces:
        for k in range(piece.shape[0]):
            n = len(copies)
            row = pl.multiple_of(meta_ref[3 + n] * BLOCK, 16)
            copies.append(
                pltpu.make_async_copy(piece.at[k], w_ref.at[pl.ds(row, BLOCK)], sems.at[n])
            )
    return copies


def mix_and_pool(d_ref, w_ref, residual, y_scr, out_ref, rows):
    count = (rows - 8) // 2
    total = up16(rows)
    chunk = even_chunk(rows, 272)
    for start in range(0, total, chunk):
        product = jnp.dot(
            d_ref[start : start + chunk], w_ref[...], preferred_element_type=jnp.float32
        )
        mixed = residual(start, chunk) + product
        for n in range(TILES):
            y_scr[n, start : start + chunk] = mixed[:, 128 * n : 128 * n + 128]
    part = next(p for p in (128, 104, 64, 40, 16, 8, 4) if count % p == 0)
    for start in range(0, count, part):
        for n in range(TILES):
            even = y_scr[n, pl.ds(4 + 2 * start, part, stride=2)]
            odd = y_scr[n, pl.ds(5 + 2 * start, part, stride=2)]
            pooled = jnp.maximum(even, odd).astype(jnp.bfloat16)
            out_ref[start : start + part, 128 * n : 128 * n + 128] = pooled


def first_half(rows, meta_ref, hot_ref, stem_ref, par_ref, x_ref, d_ref, x_scr, a_scr):
    chunk = 176
    for start in range(0, up16(rows), chunk):
        for side, target in enumerate((x_ref, x_scr)):
            target[start : start + chunk] = jnp.dot(
                hot_ref[start : start + chunk],
                stem_ref[:, side * HALF : (side + 1) * HALF],
                preferred_element_type=jnp.float32,
            ).astype(jnp.bfloat16)

    def load(start):
        return [ref[pl.ds(start, 16)].astype(jnp.float32) for ref in (x_ref, x_scr)]

    activate(load, par_ref, a_scr, rows, EDGE, meta_ref)
    spread(par_ref, a_scr, d_ref, rows)


def second_half(rows, meta_ref, x_ref, d_ref, *refs):
    *pieces, out_ref, w_ref, y_scr, sems = refs
    copies = weight_copies(meta_ref, pieces, w_ref, sems)
    for copy in copies:
        copy.start()
    for copy in copies:
        copy.wait()

    def residual(start, chunk):
        return x_ref[start : start + chunk].astype(jnp.float32)

    mix_and_pool(d_ref, w_ref, residual, y_scr, out_ref, rows)


def swapped_level(rows, edge, meta_ref, own_ref, other_ref, par_ref, *refs):
    *pieces, out_ref, w_ref, a_scr, d_scr, y_scr, sems = refs
    copies = weight_copies(meta_ref, pieces, w_ref, sems)
    for copy in copies:
        copy.start()

    def load(start):
        return [ref[pl.ds(start, 16)].astype(jnp.float32) for ref in (own_ref, other_ref)]

    activate(load, par_ref, a_scr, rows, edge, meta_ref)
    spread(par_ref, a_scr, d_scr, rows)
    for copy in copies:
        copy.wait()

    def residual(start, chunk):
        return own_ref[start : start + chunk].astype(jnp.float32)

    mix_and_pool(d_scr, w_ref, residual, y_scr, out_ref, rows)


def paired_level(rows, edge, meta_ref, x_ref, par_ref, w_ref, out_ref, a_scr, d_scr, y_scr):
    own = meta_ref[0]

    def load(start):
        return [x_ref[side, pl.ds(start, 16)].astype(jnp.float32) for side in (own, 1 - own)]

    activate(load, par_ref, a_scr, rows, edge, meta_ref)
    spread(par_ref, a_scr, d_scr, rows)

    def residual(start, chunk):
        return x_ref[own, start : start + chunk].astype(jnp.float32)

    mix_and_pool(d_scr, w_ref, residual, y_scr, out_ref, rows)


def spec(memory_space=pltpu.VMEM):
    return pl.BlockSpec(memory_space=memory_space)


def out_rows(rows, last):
    return (rows - 8) // 2 if last else up16((rows - 8) // 2)


def scratch(rows, names):
    size = up16(rows)
    shapes = {
        "a": pltpu.VMEM((2 * TILES, size + 16, 128), jnp.float32),
        "d": pltpu.VMEM((size, C), jnp.bfloat16),
        "x": pltpu.VMEM((size, HALF), jnp.bfloat16),
        "y": pltpu.VMEM((TILES, size, 128), jnp.float32),
        "s": pltpu.SemaphoreType.DMA((16,)),
    }
    return [shapes[name] for name in names]


def half_rows(size, width=HALF):
    return jax.ShapeDtypeStruct((size, width), jnp.bfloat16)


def run_first_half(rows, meta, hot, stem, par):
    size = up16(rows)
    return pl.pallas_call(
        lambda *refs: first_half(rows, *refs),
        in_specs=[spec(pltpu.SMEM), spec(), spec(), spec()],
        out_specs=[spec(), spec()],
        out_shape=[half_rows(size), half_rows(size, C)],
        scratch_shapes=scratch(rows, "xa"),
        name="stem_and_taps",
    )(meta, hot, stem, par)


def run_second_half(rows, meta, x, d, pieces):
    return pl.pallas_call(
        lambda *refs: second_half(rows, *refs),
        in_specs=[spec(pltpu.SMEM), spec(), spec()] + [spec(pl.ANY)] * len(pieces),
        out_specs=[spec(), spec()],
        out_shape=[half_rows(out_rows(rows, False)), half_rows(C)],
        scratch_shapes=scratch(rows, "ys"),
        name="mix_first",
    )(meta, x, d, *pieces)


def run_swapped_level(rows, edge, meta, own, other, par, pieces):
    return pl.pallas_call(
        lambda *refs: swapped_level(rows, edge, *refs),
        in_specs=[spec(pltpu.SMEM)] + [spec()] * 3 + [spec(pl.ANY)] * len(pieces),
        out_specs=[spec(), spec()],
        out_shape=[half_rows(out_rows(rows, True)), half_rows(C)],
        scratch_shapes=scratch(rows, "adys"),
    )(meta, own, other, par, *pieces)


def run_level(rows, edge, last, meta, x, par, weights):
    return pl.pallas_call(
        lambda *refs: paired_level(rows, edge, *refs),
        in_specs=[spec(pltpu.SMEM)] + [spec()] * 3,
        out_specs=spec(),
        out_shape=half_rows(out_rows(rows, last)),
        scratch_shapes=scratch(rows, "ady"),
    )(meta, x, par, weights)


def ring(size, by):
    return [(i, (i + by) % size) for i in range(size)]


def around(array, axes, size):
    out = [array]
    for by in SHIFTS[1:]:
        out.append(lax.ppermute(array, axes, ring(size, by)))
    return out


def around_y(array):
    copies = lax.optimization_barrier(jnp.broadcast_to(array[None], (4, *array.shape)))
    return lax.all_to_all(copies, "y", 0, 0, tiled=True)


def own_first(array, co):
    turned = jnp.concatenate([array[..., HALF:], array[..., :HALF]], axis=-1)
    return jnp.where(co == 0, array, turned)


def flat(b, g, role):
    zh, zl, y = 2 * b + g % 2, g // 8, (g // 2) % 4
    return ((zh * 4 + zl) * 4 + y) * 4 + role


def gathered_bases(bases, sequence, before, count):
    mine = lax.dynamic_index_in_dim(bases + 1, sequence, 0, keepdims=False)
    parts = []
    for by in (-1, 0, 1, 2):
        pairs = []
        for zh in range(4):
            for row in range(16):
                place = 4 * row + 2 * (zh % 2) + by
                if 0 <= place < 64:
                    pairs.append((zh * 64 + place, zh * 64 + row * 4))
        parts.append(lax.ppermute(mine, ("zh", "zl", "y", "x"), pairs))
    return jnp.concatenate(parts)[mine.shape[0] - before :][:count]


def pass_on(array, role):
    rows = array.shape[0]
    axes = ("zh", "zl", "y", "x")
    up = [(flat(b, g, role), flat(b, g + 1, role + 1)) for b in range(2) for g in range(31)]
    down = [(flat(b, g + 1, role), flat(b, g, role + 1)) for b in range(2) for g in range(31)]
    before = lax.ppermute(array[rows - EDGE :], axes, up)
    after = lax.ppermute(array[:EDGE], axes, down)
    own = lax.ppermute(array, "x", [(role, role + 1)])
    blank = jnp.zeros((8, HALF), array.dtype)
    return jnp.concatenate([before, own, after, blank], axis=0)


def relay(bases, stem_weight, gains, depth_taps, point_weight):
    zh, co, zl, y, x = [lax.axis_index(name) for name in ("zh", "co", "zl", "y", "x")]
    margin = stem_weight.shape[0] // 2
    group = (zl * 4 + y) * 2 + zh % 2
    sequence = zh // 2

    held = [point_weight[0], gains, depth_taps[0], jnp.zeros((2, C), gains.dtype)]
    held = jnp.concatenate(held, axis=0).reshape(-1, 2, HALF).transpose(1, 0, 2)
    held = lax.all_to_all(held, "co", 0, 0, tiled=True)
    held = lax.all_to_all(lax.all_gather(held, "zh"), "x", 0, 0, tiled=True)
    params = lax.all_gather(held[0, :, 24:], "co").transpose(1, 2, 0, 3).reshape(2, 8, C)
    params = own_first(params, co).astype(jnp.float32)
    blocks = [held[:, slot, :24].reshape(BLOCK, HALF) for slot in range(2)]
    along_z = jnp.stack(around(blocks[0], ("zh", "zl"), 16))
    along_y = around_y(blocks[1])
    along_z, along_y = lax.optimization_barrier((along_z, along_y))
    pieces = [[around_y(along_z).reshape(16, BLOCK, HALF)], around(along_y, ("zh", "zl"), 16)]
    z_of = (zl - jnp.array(SHIFTS, jnp.int32)) % 4
    y_of = jnp.arange(4, dtype=jnp.int32)
    places = [z_of[None, :] * 4 + y_of[:, None], z_of[:, None] * 4 + y_of[None, :]]
    flags = jnp.stack([co, (group == 0).astype(jnp.int32), (group == 31).astype(jnp.int32)])
    metas = [
        jnp.concatenate([flags.astype(jnp.int32), (place.reshape(-1) + 8 * co) % 16])
        for place in places
    ]

    rows = RUN + 2 * EDGE
    size = up16(rows)
    ids = gathered_bases(bases, sequence, EDGE + margin, size + 2 * margin)
    windows = jnp.stack([ids[k : k + size] for k in range(2 * margin + 1)])
    kinds = jnp.arange(1, 5, dtype=jnp.int32)[None, :, None]
    hot = (windows[:, None, :] == kinds).astype(jnp.bfloat16).reshape(-1, size)
    hot = jnp.pad(hot, ((0, 4), (0, 0))).T
    stem = own_first(jnp.pad(stem_weight.reshape(-1, C), ((0, 4), (0, 0))), co)
    level_rows, taps = run_first_half(rows, metas[0], hot, stem, params[0])
    now, even_weights = run_second_half(rows, metas[0], level_rows, taps, pieces[0])
    other = lax.ppermute(now, "co", [(0, 1), (1, 0)])
    now, odd_weights = run_swapped_level(
        RUN // 2 + 8, 4, metas[1], now, other, params[1], pieces[1]
    )
    run = RUN // 4
    for role in range(3):
        now = lax.all_gather(pass_on(now, role), "co")
        now = run_level(run + 2 * EDGE, EDGE, False, metas[0], now, params[0], even_weights)
        now = lax.all_gather(now, "co")
        now = run_level(run // 2 + 8, 4, True, metas[1], now, params[1], odd_weights)
        run = run // 4

    blocks = now.reshape(2, 2, 4, HALF // 4).transpose(2, 0, 1, 3)
    blocks = jnp.broadcast_to(
        blocks[None, :, None], (2, 4, 2, 2, 2, HALF // 4)
    ).reshape(32, 2, HALF // 4)
    got = lax.all_to_all(blocks, ("zh", "co", "x"), 0, 0, tiled=True)
    got = got.reshape(2, 2, 2, 4, 2, HALF // 4)[:, :, :, 3]
    got = lax.dynamic_index_in_dim(got, x // 2, 1, keepdims=False)
    return lax.dynamic_index_in_dim(got, zh // 2, 1, keepdims=False)


def solution(mesh):
    finer = Mesh(mesh.devices.reshape(4, 2, 4, 4, 4), SECTION + SEQ)
    in_specs = (
        P(None, SEQ),
        P(),
        P(SECTION, None),
        P(SECTION, None, None),
        P(SECTION, SEQ, None),
    )
    out_specs = P(None, SEQ, SECTION)
    return jax.shard_map(relay, mesh=finer, in_specs=in_specs, out_specs=out_specs, check_vma=False)
```

time: 332 us -> 282 us (0.85)
  the two profiles are of different devices: /device:TPU:17 before, /device:TPU:1 now
where the time goes in v1:
time: 282 us; the launch traced here: 280 us
  starting transfers between devices  77.6 us (28%)
  blocking collectives  63.7 us (23%)
  waiting for transfers between devices  59.6 us (21%)
  Pallas kernels  58.3 us (21%)
  local copies, waits for them, and re-layouts  14.8 us (5%)
  other arithmetic  5.4 us (2%)
    ppermute x6, waiting for transfers between devices, around(): out.append(lax.ppermute(array, axes, ring(size, by)))  39.2 us
    all_to_all x1, starting transfers between devices, relay(): got = lax.all_to_all(blocks, ('zh', 'co', 'x'), 0, 0, tiled=True)  27.2 us
    pallas_call x6, Pallas kernels, run_level(): pl.pallas_call(lambda *refs: paired_level(rows, edge, *refs), in_specs=[s...  24.9 us
    all_gather x1, blocking collectives, relay(): held = lax.all_to_all(lax.all_gather(held, 'zh'), 'x', 0, 0, tiled=True)  23.8 us
    ppermute x6, starting transfers between devices, around(): out.append(lax.ppermute(array, axes, ring(size, by)))  17.2 us
    pallas_call x1, Pallas kernels, run_first_half(): pl.pallas_call(lambda *refs: first_half(rows, *refs), in_specs=[spec(pltp...  15.7 us
    all_to_all x1, waiting for transfers between devices, relay(): got = lax.all_to_all(blocks, ('zh', 'co', 'x'), 0, 0, tiled=True)  14.4 us
    all_to_all x2, starting transfers between devices, around_y(): return lax.all_to_all(copies, 'y', 0, 0, tiled=True)  11.1 us
  transfers between devices with their start and end apart: 24, of which 7 were waited for; matrix products, arithmetic and copies ran while one was open for 5% of the time, Pallas kernels for 6%

profile of v1, /device:TPU:1, one launch (start us, length us, event | category | flops | bytes accessed | tf_op | source)
XLA Modules:
  0.0 280.0 jit_solution(2372615339462644754)
XLA Ops:
  0.0 0.7 dynamic-slice_add_fusion
  1.4 0.7 collective-permute-start.1
  2.0 1.3 collective-permute-start.2
  3.3 1.3 collective-permute-start.3
  4.6 0.9 concatenate.40
  5.5 0.8 concatenate.42
  6.3 0.7 reduce
  7.3 10.3 %all_to_all.25 = bf16[2,32,768]{2,1,0:T(8,128)(2,1)S(1)} all-to-all(bf16[2,32,768]{2,1,0:T(8,128)(2,1)S(1)} %copy.21), channel_id=1, replica_groups=mesh['zh'=4,'co'=2,'zl'=4,'y'=4,'x'=4] {'co'}, dimensions={0} | all-to-all | bytes 196608 | tf_op jit(solution)/shard_map/all_to_all | solution.py:303
  17.6 23.8 %all-gather = bf16[8,32,768]{2,1,0:T(8,128)(2,1)} all-gather(bf16[2,32,768]{2,1,0:T(8,128)(2,1)S(1)} %all_to_all.25), channel_id=2, replica_groups=mesh['zh'=4,'co'=2,'zl'=4,'y'=4,'x'=4] {'zh'}, dimensions={0}, use_global_device_ids=true | all-gather | bytes 491520 | tf_op jit(solution)/shard_map/all_gather | solution.py:304
  41.4 4.2 %all-to-all-start.1 = ((bf16[4,2,32,768]{3,2,1,0:T(8,128)(2,1)}), bf16[4,2,32,768]{3,2,1,0:T(8,128)(2,1)S(1)}, u32[]{:S(2)}, u32[]{:S(2)}) async-start(bf16[4,2,32,768]{3,2,1,0:T(8,128)(2,1)} %bitcast.6), calls=%async_computation.1 | async-start | bytes 786432 | tf_op jit(solution)/shard_map/all_to_all | solution.py:304
  45.6 0.7 fusion.3
  46.5 1.0 reshape.56
  47.5 0.7 maximum_select_fusion.refs_2_
  49.0 2.9 %all-to-all-done.1 = bf16[4,2,32,768]{3,2,1,0:T(8,128)(2,1)S(1)} async-done(((bf16[4,2,32,768]{3,2,1,0:T(8,128)(2,1)}), bf16[4,2,32,768]{3,2,1,0:T(8,128)(2,1)S(1)}, u32[]{:S(2)}, u32[]{:S(2)}) %all-to-all-start.1) | async-done | bytes 393248 | tf_op jit(solution)/shard_map/all_to_all | solution.py:304
  51.9 0.9 broadcast_in_dim.12
  52.8 7.0 %all-to-all-start.2 = ((bf16[4,96,768]{2,1,0:T(8,128)(2,1)}), bf16[4,96,768]{2,1,0:T(8,128)(2,1)S(1)}, u32[]{:S(2)}, u32[]{:S(2)}) async-start(bf16[4,96,768]{2,1,0:T(8,128)(2,1)} %broadcast_in_dim.12), calls=%async_computation.2 | async-start | bytes 1179648 | tf_op jit(solution)/shard_map/all_to_all | solution.py:256
  59.9 2.6 collective-permute-start.4
  62.5 3.9 %collective-permute-start.5 = (bf16[96,768]{1,0:T(8,128)(2,1)S(1)}, bf16[96,768]{1,0:T(8,128)(2,1)S(1)}, u32[]{:S(2)}, u32[]{:S(2)}) collective-permute-start(bf16[96,768]{1,0:T(8,128)(2,1)S(1)} %bitcast.40), channel_id=1, source_target_pairs={{0,432},{16,0},{32,16},{48,32},{128,48},{144,128},{160,144},{176,1... | collective-permute-start | bytes 442376 | tf_op jit(solution)/shard_map/ppermute | solution.py:250
  66.4 2.3 collective-permute-start.6
  69.6 6.2 %collective-permute-done.6 = bf16[96,768]{1,0:T(8,128)(2,1)S(1)} collective-permute-done((bf16[96,768]{1,0:T(8,128)(2,1)S(1)}, bf16[96,768]{1,0:T(8,128)(2,1)S(1)}, u32[]{:S(2)}, u32[]{:S(2)}) %collective-permute-start.6) | collective-permute-done | bytes 147488 | tf_op jit(solution)/shard_map/ppermute | solution.py:250
  75.9 1.6 broadcast_in_dim.13
  77.5 4.0 %all-to-all-start.3 = ((bf16[4,4,96,768]{3,2,1,0:T(8,128)(2,1)}), bf16[4,4,96,768]{3,2,1,0:T(8,128)(2,1)S(1)}, u32[]{:S(2)}, u32[]{:S(2)}) async-start(bf16[4,4,96,768]{3,2,1,0:T(8,128)(2,1)} %broadcast_in_dim.13), calls=%async_computation.3 | async-start | bytes 4718592 | tf_op jit(solution)/shard_map/all_to_all | solution.py:256
  81.7 0.8 fusion.refs_1_
  82.4 0.7 slice.163
  83.2 10.1 %all_gather.47 = bf16[2,2,8,768]{3,2,1,0:T(8,128)(2,1)S(1)} all-gather(bf16[1,2,8,768]{3,2,1,0:T(8,128)(2,1)S(1)} %slice.163), channel_id=1, replica_groups=mesh['zh'=4,'co'=2,'zl'=4,'y'=4,'x'=4] {'co'}, dimensions={0}, use_global_device_ids=true | all-gather | bytes 73728 | tf_op jit(solution)/shard_map/all_gather | solution.py:305
  94.0 15.7 %stem_and_taps.1 = (bf16[1056,768]{1,0:T(8,128)(2,1)}, bf16[1056,1536]{1,0:T(8,128)(2,1)}) custom-call(s32[19]{0:T(128)} %get-tuple-element.21.refs_0_, bf16[1056,64]{1,0:T(8,128)(2,1)} %fusion.refs_1_, bf16[64,1536]{1,0:T(8,128)(2,1)} %maximum_select_fusion.refs_2_, f32[8,1536]{1,0:T(8,128)} %get-tuple-element.32.refs_3_.refs_2_), custom_call_target="tpu_custom_call" | custom-call | tf_op jit(solution)/shard_map/stem_and_taps/pallas_call | solution.py:202
  109.7 1.4 copy-done
  111.1 8.0 %mix_first.1 = (bf16[528,768]{1,0:T(8,128)(2,1)}, bf16[1536,768]{1,0:T(8,128)(2,1)}) custom-call(s32[19]{0:T(128)} %get-tuple-element.21.refs_0_, bf16[1056,768]{1,0:T(8,128)(2,1)} %get-tuple-element.13.refs_1_, bf16[1056,1536]{1,0:T(8,128)(2,1)} %get-tuple-element.14.refs_2_, bf16[16,96,768]{2,1,0:T(8,128)(2,1)} %bitcast.33), custom_call_target="tpu_custom_call" | custom-call | tf_op jit(solution)/shard_map/mix_first/pallas_call | solution.py:213
  119.2 3.9 %collective-permute-start.7 = (bf16[528,768]{1,0:T(8,128)(2,1)}, bf16[528,768]{1,0:T(8,128)(2,1)S(1)}, u32[]{:S(2)}, u32[]{:S(2)}) collective-permute-start(bf16[528,768]{1,0:T(8,128)(2,1)} %get-tuple-element.16.refs_1_), channel_id=1, source_target_pairs={{0,64},{64,0},{1,65},{65,1},{2,66},{66,2},{3,67},{67,3},{4,68},{68... | collective-permute-start | bytes 2433032 | tf_op jit(solution)/shard_map/ppermute | solution.py:331
  123.1 1.9 collective-permute-start.10
  125.0 2.7 collective-permute-start.8
  127.7 3.8 %collective-permute-start.9 = (bf16[4,96,768]{2,1,0:T(8,128)(2,1)S(1)}, bf16[4,96,768]{2,1,0:T(8,128)(2,1)S(1)}, u32[]{:S(2)}, u32[]{:S(2)}) collective-permute-start(bf16[4,96,768]{2,1,0:T(8,128)(2,1)S(1)} %all-to-all-done.2.refs_4_), channel_id=1, source_target_pairs={{0,432},{16,0},{32,16},{48,32},{128,48},{144,128},{160,144},{176,1... | collective-permute-start | bytes 1769480 | tf_op jit(solution)/shard_map/ppermute | solution.py:250
  132.2 20.1 %collective-permute-done.10.refs_7_ = bf16[4,96,768]{2,1,0:T(8,128)(2,1)S(1)} collective-permute-done((bf16[4,96,768]{2,1,0:T(8,128)(2,1)S(1)}, bf16[4,96,768]{2,1,0:T(8,128)(2,1)S(1)}, u32[]{:S(2)}, u32[]{:S(2)}) %collective-permute-start.10) | collective-permute-done | bytes 589856 | tf_op jit(solution)/shard_map/ppermute | solution.py:250
  152.3 12.8 %collective-permute-done.8.refs_5_ = bf16[4,96,768]{2,1,0:T(8,128)(2,1)S(1)} collective-permute-done((bf16[4,96,768]{2,1,0:T(8,128)(2,1)S(1)}, bf16[4,96,768]{2,1,0:T(8,128)(2,1)S(1)}, u32[]{:S(2)}, u32[]{:S(2)}) %collective-permute-start.8) | collective-permute-done | bytes 589856 | tf_op jit(solution)/shard_map/ppermute | solution.py:250
  165.2 0.8 copy-done.5
  166.5 9.7 %shard_map.64 = (bf16[256,768]{1,0:T(8,128)(2,1)}, bf16[1536,768]{1,0:T(8,128)(2,1)}) custom-call(s32[19]{0:T(128)} %pad_add_fusion.refs_0_, bf16[528,768]{1,0:T(8,128)(2,1)} %get-tuple-element.16.refs_1_, bf16[528,768]{1,0:T(8,128)(2,1)} %copy-done.3, f32[8,1536]{1,0:T(8,128)} %get-tuple-element.31.refs_3_.refs_2_, bf16[4,96,768]{2,1,0:T(8,128)(2,1)} %copy-done.1, ...), custom_call_target="tpu_custom_call" | custom-call | tf_op jit(solution)/shard_map/pallas_call | solution.py:224
  176.2 2.2 collective-permute-start.12
  178.3 0.8 fusion.6
  179.1 3.3 %collective-permute-start.11 = (bf16[12,768]{1,0:T(8,128)(2,1)S(1)}, bf16[12,768]{1,0:T(8,128)(2,1)S(1)}, u32[]{:S(2)}, u32[]{:S(2)}) collective-permute-start(bf16[12,768]{1,0:T(8,128)(2,1)S(1)} %get-tuple-element.23), channel_id=1, source_target_pairs={{0,129},{128,5},{4,133},{132,9},{8,137},{136,13},{12,141},{140,17}... | collective-permute-start | bytes 55304 | tf_op jit(solution)/shard_map/ppermute | solution.py:288
  182.4 0.7 collective-permute-start.13
  183.4 2.7 collective-permute-done.12
  186.2 4.4 %all-gather.1 = bf16[576,768]{1,0:T(8,128)(2,1)} all-gather(bf16[288,768]{1,0:T(8,128)(2,1)S(1)} %pad_maximum_fusion.1), channel_id=3, replica_groups=mesh['zh'=4,'co'=2,'zl'=4,'y'=4,'x'=4] {'co'}, dimensions={0}, use_global_device_ids=true | all-gather | bytes 1327104 | tf_op jit(solution)/shard_map/all_gather | solution.py:337
  190.6 6.8 %shard_map.65 = bf16[144,768]{1,0:T(8,128)(2,1)} custom-call(s32[19]{0:T(128)} %get-tuple-element.21.refs_0_, bf16[2,288,768]{2,1,0:T(8,128)(2,1)} %bitcast.34, f32[8,1536]{1,0:T(8,128)} %get-tuple-element.32.refs_3_.refs_2_, bf16[1536,768]{1,0:T(8,128)(2,1)} %get-tuple-element.19.refs_3_), custom_call_target="tpu_custom_call" | custom-call | tf_op jit(solution)/shard_map/pallas_call | solution.py:234
  197.4 3.9 %all-gather.2 = bf16[288,768]{1,0:T(8,128)(2,1)} all-gather(bf16[144,768]{1,0:T(8,128)(2,1)} %shard_map.65), channel_id=4, replica_groups=mesh['zh'=4,'co'=2,'zl'=4,'y'=4,'x'=4] {'co'}, dimensions={0}, use_global_device_ids=true | all-gather | bytes 663552 | tf_op jit(solution)/shard_map/all_gather | solution.py:339
  201.4 4.5 %shard_map.66 = bf16[64,768]{1,0:T(8,128)(2,1)} custom-call(s32[19]{0:T(128)} %pad_add_fusion.refs_0_, bf16[2,144,768]{2,1,0:T(8,128)(2,1)} %bitcast.35, f32[8,1536]{1,0:T(8,128)} %get-tuple-element.31.refs_3_.refs_2_, bf16[1536,768]{1,0:T(8,128)(2,1)} %get-tuple-element.20.refs_3_), custom_call_target="tpu_custom_call" | custom-call | tf_op jit(solution)/shard_map/pallas_call | solution.py:234
  205.9 0.7 collective-permute-start.15
  206.6 0.8 fusion.8
  207.3 0.7 collective-permute-start.14
  208.0 0.7 collective-permute-start.16
  208.7 2.3 all-gather.3
  211.1 3.9 %shard_map.67 = bf16[48,768]{1,0:T(8,128)(2,1)} custom-call(s32[19]{0:T(128)} %get-tuple-element.21.refs_0_, bf16[2,96,768]{2,1,0:T(8,128)(2,1)} %bitcast.36, f32[8,1536]{1,0:T(8,128)} %get-tuple-element.32.refs_3_.refs_2_, bf16[1536,768]{1,0:T(8,128)(2,1)} %get-tuple-element.19.refs_3_), custom_call_target="tpu_custom_call" | custom-call | tf_op jit(solution)/shard_map/pallas_call | solution.py:234
  215.0 3.4 %all-gather.4 = bf16[96,768]{1,0:T(8,128)(2,1)} all-gather(bf16[48,768]{1,0:T(8,128)(2,1)} %shard_map.67), channel_id=6, replica_groups=mesh['zh'=4,'co'=2,'zl'=4,'y'=4,'x'=4] {'co'}, dimensions={0}, use_global_device_ids=true | all-gather | bytes 221184 | tf_op jit(solution)/shard_map/all_gather | solution.py:339
  218.4 3.4 %shard_map.68 = bf16[16,768]{1,0:T(8,128)(2,1)} custom-call(s32[19]{0:T(128)} %pad_add_fusion.refs_0_, bf16[2,48,768]{2,1,0:T(8,128)(2,1)} %bitcast.38, f32[8,1536]{1,0:T(8,128)} %get-tuple-element.31.refs_3_.refs_2_, bf16[1536,768]{1,0:T(8,128)(2,1)} %get-tuple-element.20.refs_3_), custom_call_target="tpu_custom_call" | custom-call | tf_op jit(solution)/shard_map/pallas_call | solution.py:234
  221.8 0.7 collective-permute-start.18
  222.4 0.8 fusion.10
  223.3 0.7 collective-permute-start.17
  223.9 0.7 collective-permute-start.19
  224.7 2.0 all-gather.5
  226.7 3.4 %shard_map.69 = bf16[16,768]{1,0:T(8,128)(2,1)} custom-call(s32[19]{0:T(128)} %get-tuple-element.21.refs_0_, bf16[2,48,768]{2,1,0:T(8,128)(2,1)} %bitcast.37, f32[8,1536]{1,0:T(8,128)} %get-tuple-element.32.refs_3_.refs_2_, bf16[1536,768]{1,0:T(8,128)(2,1)} %get-tuple-element.19.refs_3_), custom_call_target="tpu_custom_call" | custom-call | tf_op jit(solution)/shard_map/pallas_call | solution.py:234
  230.1 3.3 %all-gather.6 = bf16[32,768]{1,0:T(8,128)(2,1)} all-gather(bf16[16,768]{1,0:T(8,128)(2,1)} %shard_map.69), channel_id=8, replica_groups=mesh['zh'=4,'co'=2,'zl'=4,'y'=4,'x'=4] {'co'}, dimensions={0}, use_global_device_ids=true | all-gather | bytes 73728 | tf_op jit(solution)/shard_map/all_gather | solution.py:339
  233.4 2.9 %shard_map.70 = bf16[4,768]{1,0:T(4,128)(2,1)} custom-call(s32[19]{0:T(128)} %pad_add_fusion.refs_0_, bf16[2,16,768]{2,1,0:T(8,128)(2,1)} %bitcast.47, f32[8,1536]{1,0:T(8,128)} %get-tuple-element.31.refs_3_.refs_2_, bf16[1536,768]{1,0:T(8,128)(2,1)} %get-tuple-element.20.refs_3_), custom_call_target="tpu_custom_call" | custom-call | tf_op jit(solution)/shard_map/pallas_call | solution.py:234
  236.4 0.8 reshape.59
  237.8 27.2 %all-to-all-start.4 = ((bf16[32,2,192]{2,1,0:T(2,128)(2,1)}), bf16[32,2,192]{2,1,0:T(2,128)(2,1)S(1)}, u32[]{:S(2)}, u32[]{:S(2)}) async-start(bf16[32,2,192]{2,1,0:T(2,128)(2,1)} %bitcast.25), calls=%async_computation.4 | async-start | bytes 65536 | tf_op jit(solution)/shard_map/all_to_all | solution.py:347
  265.0 14.4 %all-to-all-done.4 = bf16[32,2,192]{2,1,0:T(2,128)(2,1)S(1)} async-done(((bf16[32,2,192]{2,1,0:T(2,128)(2,1)}), bf16[32,2,192]{2,1,0:T(2,128)(2,1)S(1)}, u32[]{:S(2)}, u32[]{:S(2)}) %all-to-all-start.4) | async-done | bytes 24608 | tf_op jit(solution)/shard_map/all_to_all | solution.py:347
  (87 shorter events, 6.2 us)
Async XLA Ops:
  0.7 48.2 %collective-permute-start = (s32[512]{0:T(512)S(1)}, s32[512]{0:T(512)S(1)}, u32[]{:S(2)}, u32[]{:S(2)}) collective-permute-start(s32[512]{0:T(512)S(1)} %bitcast.53), channel_id=1, source_target_pairs={{3,4},{7,8},{11,12},{15,16},{19,20},{23,24},{27,28},{31,32},{35,36... | collective-permute-start | bytes 6152 | tf_op jit(solution)/shard_map/ppermute | solution.py:279
  1.4 47.6 %collective-permute-start.1 = (s32[512]{0:T(512)S(1)}, s32[512]{0:T(512)S(1)}, u32[]{:S(2)}, u32[]{:S(2)}) collective-permute-start(s32[512]{0:T(512)S(1)} %bitcast.54), channel_id=1, source_target_pairs={{0,0},{4,4},{8,8},{12,12},{16,16},{20,20},{24,24},{28,28},{32,32},... | collective-permute-start | bytes 6152 | tf_op jit(solution)/shard_map/ppermute | solution.py:279
  2.0 46.9 %collective-permute-start.2 = (s32[512]{0:T(512)S(1)}, s32[512]{0:T(512)S(1)}, u32[]{:S(2)}, u32[]{:S(2)}) collective-permute-start(s32[512]{0:T(512)S(1)} %bitcast.55), channel_id=1, source_target_pairs={{1,0},{5,4},{9,8},{13,12},{17,16},{21,20},{25,24},{29,28},{33,32},... | collective-permute-start | bytes 6152 | tf_op jit(solution)/shard_map/ppermute | solution.py:279
  3.3 56.6 %collective-permute-start.3 = (s32[512]{0:T(512)S(1)}, s32[512]{0:T(512)S(1)}, u32[]{:S(2)}, u32[]{:S(2)}) collective-permute-start(s32[512]{0:T(512)S(1)} %bitcast.56), channel_id=1, source_target_pairs={{2,0},{6,4},{10,8},{14,12},{18,16},{22,20},{26,24},{30,28},{34,32}... | collective-permute-start | bytes 6152 | tf_op jit(solution)/shard_map/ppermute | solution.py:279
  41.4 10.5 %all-to-all-start.1 = ((bf16[4,2,32,768]{3,2,1,0:T(8,128)(2,1)}), bf16[4,2,32,768]{3,2,1,0:T(8,128)(2,1)S(1)}, u32[]{:S(2)}, u32[]{:S(2)}) async-start(bf16[4,2,32,768]{3,2,1,0:T(8,128)(2,1)} %bitcast.6), calls=%async_computation.1 | async-start | bytes 786432 | tf_op jit(solution)/shard_map/all_to_all | solution.py:304
  51.9 0.9 copy-start.2
  52.8 23.1 %all-to-all-start.2 = ((bf16[4,96,768]{2,1,0:T(8,128)(2,1)}), bf16[4,96,768]{2,1,0:T(8,128)(2,1)S(1)}, u32[]{:S(2)}, u32[]{:S(2)}) async-start(bf16[4,96,768]{2,1,0:T(8,128)(2,1)} %broadcast_in_dim.12), calls=%async_computation.2 | async-start | bytes 1179648 | tf_op jit(solution)/shard_map/all_to_all | solution.py:256
  59.9 9.7 %collective-permute-start.4 = (bf16[96,768]{1,0:T(8,128)(2,1)S(1)}, bf16[96,768]{1,0:T(8,128)(2,1)S(1)}, u32[]{:S(2)}, u32[]{:S(2)}) collective-permute-start(bf16[96,768]{1,0:T(8,128)(2,1)S(1)} %bitcast.39), channel_id=1, source_target_pairs={{0,16},{16,32},{32,48},{48,128},{128,144},{144,160},{160,176},{176... | collective-permute-start | bytes 442376 | tf_op jit(solution)/shard_map/ppermute | solution.py:250
  62.5 7.1 %collective-permute-start.5 = (bf16[96,768]{1,0:T(8,128)(2,1)S(1)}, bf16[96,768]{1,0:T(8,128)(2,1)S(1)}, u32[]{:S(2)}, u32[]{:S(2)}) collective-permute-start(bf16[96,768]{1,0:T(8,128)(2,1)S(1)} %bitcast.40), channel_id=1, source_target_pairs={{0,432},{16,0},{32,16},{48,32},{128,48},{144,128},{160,144},{176,1... | collective-permute-start | bytes 442376 | tf_op jit(solution)/shard_map/ppermute | solution.py:250
  66.4 9.4 %collective-permute-start.6 = (bf16[96,768]{1,0:T(8,128)(2,1)S(1)}, bf16[96,768]{1,0:T(8,128)(2,1)S(1)}, u32[]{:S(2)}, u32[]{:S(2)}) collective-permute-start(bf16[96,768]{1,0:T(8,128)(2,1)S(1)} %bitcast.41), channel_id=1, source_target_pairs={{0,32},{16,48},{32,128},{48,144},{128,160},{144,176},{160,256},{17... | collective-permute-start | bytes 442376 | tf_op jit(solution)/shard_map/ppermute | solution.py:250
  75.9 51.8 %copy-start.1 = (bf16[4,96,768]{2,1,0:T(8,128)(2,1)}, bf16[4,96,768]{2,1,0:T(8,128)(2,1)S(1)}, u32[]{:S(2)}) copy-start(bf16[4,96,768]{2,1,0:T(8,128)(2,1)S(1)} %all-to-all-done.2.refs_4_) | copy-start | bytes 1769476
  77.5 32.1 %all-to-all-start.3 = ((bf16[4,4,96,768]{3,2,1,0:T(8,128)(2,1)}), bf16[4,4,96,768]{3,2,1,0:T(8,128)(2,1)S(1)}, u32[]{:S(2)}, u32[]{:S(2)}) async-start(bf16[4,4,96,768]{3,2,1,0:T(8,128)(2,1)} %broadcast_in_dim.13), calls=%async_computation.3 | async-start | bytes 4718592 | tf_op jit(solution)/shard_map/all_to_all | solution.py:256
  109.7 1.4 copy-start
  119.2 46.0 %collective-permute-start.7 = (bf16[528,768]{1,0:T(8,128)(2,1)}, bf16[528,768]{1,0:T(8,128)(2,1)S(1)}, u32[]{:S(2)}, u32[]{:S(2)}) collective-permute-start(bf16[528,768]{1,0:T(8,128)(2,1)} %get-tuple-element.16.refs_1_), channel_id=1, source_target_pairs={{0,64},{64,0},{1,65},{65,1},{2,66},{66,2},{3,67},{67,3},{4,68},{68... | collective-permute-start | bytes 2433032 | tf_op jit(solution)/shard_map/ppermute | solution.py:331
  123.1 29.3 %collective-permute-start.10 = (bf16[4,96,768]{2,1,0:T(8,128)(2,1)S(1)}, bf16[4,96,768]{2,1,0:T(8,128)(2,1)S(1)}, u32[]{:S(2)}, u32[]{:S(2)}) collective-permute-start(bf16[4,96,768]{2,1,0:T(8,128)(2,1)S(1)} %all-to-all-done.2.refs_4_), channel_id=1, source_target_pairs={{0,32},{16,48},{32,128},{48,144},{128,160},{144,176},{160,256},{17... | collective-permute-start | bytes 1769480 | tf_op jit(solution)/shard_map/ppermute | solution.py:250
  125.0 40.2 %collective-permute-start.8 = (bf16[4,96,768]{2,1,0:T(8,128)(2,1)S(1)}, bf16[4,96,768]{2,1,0:T(8,128)(2,1)S(1)}, u32[]{:S(2)}, u32[]{:S(2)}) collective-permute-start(bf16[4,96,768]{2,1,0:T(8,128)(2,1)S(1)} %all-to-all-done.2.refs_4_), channel_id=1, source_target_pairs={{0,16},{16,32},{32,48},{48,128},{128,144},{144,160},{160,176},{176... | collective-permute-start | bytes 1769480 | tf_op jit(solution)/shard_map/ppermute | solution.py:250
  127.7 37.5 %collective-permute-start.9 = (bf16[4,96,768]{2,1,0:T(8,128)(2,1)S(1)}, bf16[4,96,768]{2,1,0:T(8,128)(2,1)S(1)}, u32[]{:S(2)}, u32[]{:S(2)}) collective-permute-start(bf16[4,96,768]{2,1,0:T(8,128)(2,1)S(1)} %all-to-all-done.2.refs_4_), channel_id=1, source_target_pairs={{0,432},{16,0},{32,16},{48,32},{128,48},{144,128},{160,144},{176,1... | collective-permute-start | bytes 1769480 | tf_op jit(solution)/shard_map/ppermute | solution.py:250
  152.3 12.9 %copy-start.4 = (bf16[4,96,768]{2,1,0:T(8,128)(2,1)}, bf16[4,96,768]{2,1,0:T(8,128)(2,1)S(1)}, u32[]{:S(2)}) copy-start(bf16[4,96,768]{2,1,0:T(8,128)(2,1)S(1)} %collective-permute-done.10.refs_7_) | copy-start | bytes 1769476
  165.2 0.8 copy-start.5
  165.2 1.0 copy-start.6
  165.2 1.3 copy-start.3
  176.2 9.9 %collective-permute-start.12 = (bf16[256,768]{1,0:T(8,128)(2,1)}, bf16[256,768]{1,0:T(8,128)(2,1)S(1)}, u32[]{:S(2)}, u32[]{:S(2)}) collective-permute-start(bf16[256,768]{1,0:T(8,128)(2,1)} %get-tuple-element.18), channel_id=1, source_target_pairs={{0,1},{4,5},{8,9},{12,13},{16,17},{20,21},{24,25},{28,29},{32,33},... | collective-permute-start | bytes 1179656 | tf_op jit(solution)/shard_map/ppermute | solution.py:290
  179.1 4.3 %collective-permute-start.11 = (bf16[12,768]{1,0:T(8,128)(2,1)S(1)}, bf16[12,768]{1,0:T(8,128)(2,1)S(1)}, u32[]{:S(2)}, u32[]{:S(2)}) collective-permute-start(bf16[12,768]{1,0:T(8,128)(2,1)S(1)} %get-tuple-element.23), channel_id=1, source_target_pairs={{0,129},{128,5},{4,133},{132,9},{8,137},{136,13},{12,141},{140,17}... | collective-permute-start | bytes 55304 | tf_op jit(solution)/shard_map/ppermute | solution.py:288
  182.4 0.9 collective-permute-start.13
  205.9 2.8 collective-permute-start.15
  207.3 1.3 collective-permute-start.14
  208.0 0.7 collective-permute-start.16
  221.8 2.8 %collective-permute-start.18 = (bf16[16,768]{1,0:T(8,128)(2,1)}, bf16[16,768]{1,0:T(8,128)(2,1)S(1)}, u32[]{:S(2)}, u32[]{:S(2)}) collective-permute-start(bf16[16,768]{1,0:T(8,128)(2,1)} %shard_map.68), channel_id=1, source_target_pairs={{2,3},{6,7},{10,11},{14,15},{18,19},{22,23},{26,27},{30,31},{34,35... | collective-permute-start | bytes 73736 | tf_op jit(solution)/shard_map/ppermute | solution.py:290
  223.3 1.3 collective-permute-start.17
  223.9 0.7 collective-permute-start.19
  237.8 41.7 %all-to-all-start.4 = ((bf16[32,2,192]{2,1,0:T(2,128)(2,1)}), bf16[32,2,192]{2,1,0:T(2,128)(2,1)S(1)}, u32[]{:S(2)}, u32[]{:S(2)}) async-start(bf16[32,2,192]{2,1,0:T(2,128)(2,1)} %bitcast.25), calls=%async_computation.4 | async-start | bytes 65536 | tf_op jit(solution)/shard_map/all_to_all | solution.py:347

commit v2 on v1

--- a/solution.py
+++ b/solution.py
@@ -212,7 +212,7 @@
 def run_second_half(rows, meta, x, d, pieces):
     return pl.pallas_call(
         lambda *refs: second_half(rows, *refs),
-        in_specs=[spec(pltpu.SMEM), spec(), spec()] + [spec(pl.ANY)] * len(pieces),
+        in_specs=[spec(pltpu.SMEM), spec(), spec()] + [spec()] * len(pieces),
         out_specs=[spec(), spec()],
         out_shape=[half_rows(out_rows(rows, False)), half_rows(C)],
         scratch_shapes=scratch(rows, "ys"),
@@ -223,7 +223,7 @@
 def run_swapped_level(rows, edge, meta, own, other, par, pieces):
     return pl.pallas_call(
         lambda *refs: swapped_level(rows, edge, *refs),
-        in_specs=[spec(pltpu.SMEM)] + [spec()] * 3 + [spec(pl.ANY)] * len(pieces),
+        in_specs=[spec(pltpu.SMEM)] + [spec()] * 3 + [spec()] * len(pieces),
         out_specs=[spec(), spec()],
         out_shape=[half_rows(out_rows(rows, True)), half_rows(C)],
         scratch_shapes=scratch(rows, "adys"),
@@ -244,11 +244,19 @@
     return [(i, (i + by) % size) for i in range(size)]
 
 
-def around(array, axes, size):
+def around_z(array):
+    sends = [(array, 1), (array, -1), (array[:2], 2), (array[2:], -2)]
     out = [array]
-    for by in SHIFTS[1:]:
-        out.append(lax.ppermute(array, axes, ring(size, by)))
+    for part, by in sends:
+        out.append(lax.ppermute(part, ("zh", "zl"), ring(16, by)))
     return out
+
+
+def to_roles(array, axis):
+    copies = jnp.broadcast_to(array[None], (4, *array.shape)).reshape(16, *array.shape[1:])
+    copies = lax.optimization_barrier(copies)
+    got = lax.all_to_all(copies, (axis, "x"), 0, 0, tiled=True)
+    return got.reshape(4, BLOCK, HALF)
 
 
 def around_y(array):
@@ -301,17 +309,18 @@
     held = [point_weight[0], gains, depth_taps[0], jnp.zeros((2, C), gains.dtype)]
     held = jnp.concatenate(held, axis=0).reshape(-1, 2, HALF).transpose(1, 0, 2)
     held = lax.all_to_all(held, "co", 0, 0, tiled=True)
-    held = lax.all_to_all(lax.all_gather(held, "zh"), "x", 0, 0, tiled=True)
-    params = lax.all_gather(held[0, :, 24:], "co").transpose(1, 2, 0, 3).reshape(2, 8, C)
+    held, bases = lax.optimization_barrier((lax.all_gather(held, "zh"), bases))
+    along_z = to_roles(held[:, 0, :24], "zl")
+    along_y = to_roles(held[:, 1, :24], "y")
+    along_z, along_y = lax.optimization_barrier((along_z, along_y))
+    pieces = [[around_y(along_z).reshape(16, BLOCK, HALF)], around_z(along_y)]
+    params = lax.dynamic_index_in_dim(held, x, 0, keepdims=False)[:, 24:]
+    params = lax.all_gather(params, "co")
+    params = params.transpose(1, 2, 0, 3).reshape(2, 8, C)
     params = own_first(params, co).astype(jnp.float32)
-    blocks = [held[:, slot, :24].reshape(BLOCK, HALF) for slot in range(2)]
-    along_z = jnp.stack(around(blocks[0], ("zh", "zl"), 16))
-    along_y = around_y(blocks[1])
-    along_z, along_y = lax.optimization_barrier((along_z, along_y))
-    pieces = [[around_y(along_z).reshape(16, BLOCK, HALF)], around(along_y, ("zh", "zl"), 16)]
+    four = jnp.arange(4, dtype=jnp.int32)
     z_of = (zl - jnp.array(SHIFTS, jnp.int32)) % 4
-    y_of = jnp.arange(4, dtype=jnp.int32)
-    places = [z_of[None, :] * 4 + y_of[:, None], z_of[:, None] * 4 + y_of[None, :]]
+    places = [four[None, :] * 4 + four[:, None], z_of[:, None] * 4 + four[None, :]]
     flags = jnp.stack([co, (group == 0).astype(jnp.int32), (group == 31).astype(jnp.int32)])
     metas = [
         jnp.concatenate([flags.astype(jnp.int32), (place.reshape(-1) + 8 * co) % 16])

time: 282 us -> 275 us (0.975)
  blocking collectives: 63.7 us -> 56.6 us
  Pallas kernels: 58.3 us -> 64.2 us
  starting transfers between devices: 77.6 us -> 74.7 us
    ppermute x6 -> x4, waiting for transfers between devices: 39.2 us -> 20.9 us  [around_z(): out.append(lax.ppermute(part, ('zh', 'zl'), ring(16, by)))]
    all_to_all x1 -> x2, waiting for transfers between devices: 2.9 us -> 13.6 us  [to_roles(): got = lax.all_to_all(copies, (axis, 'x'), 0, 0, tiled=True)]
    all_to_all x2 -> x1, starting transfers between devices: 11.1 us -> 3.63 us  [around_y(): return lax.all_to_all(copies, 'y', 0, 0, tiled=True)]
    all_gather x2, blocking collectives: 33.9 us -> 26.9 us  [the longest x1 22.6 us: relay(): held, bases = lax.optimization_barrier((lax.all_gather(held, 'zh'), bases))]
    all_to_all x1 -> x2, starting transfers between devices: 4.22 us -> 10.3 us  [to_roles(): got = lax.all_to_all(copies, (axis, 'x'), 0, 0, tiled=True)]
    all_to_all x2 -> x1, waiting for transfers between devices: 0.01 us -> 4.02 us  [around_y(): return lax.all_to_all(copies, 'y', 0, 0, tiled=True)]
    pallas_call x1, Pallas kernels: 9.69 us -> 13.4 us  [run_swapped_level(): pl.pallas_call(lambda *refs: swapped_level(rows, edge, *refs), in_specs=[...]
    ppermute x1, starting transfers between devices: 3.9 us -> 7.4 us  [relay(): other = lax.ppermute(now, 'co', [(0, 1), (1, 0)])]
  transfers between devices with their start and end apart: 24 -> 22, of which waited for: 7 -> 8; matrix products, arithmetic and copies ran while one was open for 5% -> 4% of each run, Pallas kernels for 6% -> 6%
where the time goes in v2:
time: 275 us; the launch traced here: 274 us
  starting transfers between devices  74.7 us (27%)
  Pallas kernels  64.2 us (23%)
  waiting for transfers between devices  57.8 us (21%)
  blocking collectives  56.6 us (21%)
  local copies, waits for them, and re-layouts  15.7 us (6%)
  other arithmetic  3.96 us (1%)
    all_to_all x1, starting transfers between devices, relay(): got = lax.all_to_all(blocks, ('zh', 'co', 'x'), 0, 0, tiled=True)  27.3 us
    pallas_call x6, Pallas kernels, run_level(): pl.pallas_call(lambda *refs: paired_level(rows, edge, *refs), in_specs=[s...  24.9 us
    all_gather x1, blocking collectives, relay(): held, bases = lax.optimization_barrier((lax.all_gather(held, 'zh'), bases))  22.6 us
    ppermute x4, waiting for transfers between devices, around_z(): out.append(lax.ppermute(part, ('zh', 'zl'), ring(16, by)))  20.9 us
    pallas_call x1, Pallas kernels, run_first_half(): pl.pallas_call(lambda *refs: first_half(rows, *refs), in_specs=[spec(pltp...  15.7 us
    all_to_all x1, waiting for transfers between devices, relay(): got = lax.all_to_all(blocks, ('zh', 'co', 'x'), 0, 0, tiled=True)  14.4 us
    ppermute x4, starting transfers between devices, around_z(): out.append(lax.ppermute(part, ('zh', 'zl'), ring(16, by)))  13.9 us
    all_to_all x2, waiting for transfers between devices, to_roles(): got = lax.all_to_all(copies, (axis, 'x'), 0, 0, tiled=True)  13.6 us
  transfers between devices with their start and end apart: 22, of which 8 were waited for; matrix products, arithmetic and copies ran while one was open for 4% of the time, Pallas kernels for 6%

profile of v2, /device:TPU:1, one launch (start us, length us, event | category | flops | bytes accessed | tf_op | source)
XLA Modules:
  0.0 273.7 jit_solution(13261764605726028126)
XLA Ops:
  0.0 0.9 concatenate.38
  0.9 0.8 concatenate.40
  1.7 0.7 reduce
  2.7 10.3 %all_to_all.25 = bf16[2,32,768]{2,1,0:T(8,128)(2,1)S(1)} all-to-all(bf16[2,32,768]{2,1,0:T(8,128)(2,1)S(1)} %copy.24), channel_id=1, replica_groups=mesh['zh'=4,'co'=2,'zl'=4,'y'=4,'x'=4] {'co'}, dimensions={0} | all-to-all | bytes 196608 | tf_op jit(solution)/shard_map/all_to_all | solution.py:311
  13.0 22.6 %all-gather = bf16[8,32,768]{2,1,0:T(8,128)(2,1)S(1)} all-gather(bf16[2,32,768]{2,1,0:T(8,128)(2,1)S(1)} %all_to_all.25), channel_id=2, replica_groups=mesh['zh'=4,'co'=2,'zl'=4,'y'=4,'x'=4] {'zh'}, dimensions={0}, use_global_device_ids=true | all-gather | bytes 491520 | tf_op jit(solution)/shard_map/all_gather | solution.py:312
  35.6 0.9 broadcast_in_dim.18
  36.5 6.8 %all-to-all-start.2 = ((bf16[16,24,768]{2,1,0:T(8,128)(2,1)}), bf16[16,24,768]{2,1,0:T(8,128)(2,1)S(1)}, u32[]{:S(2)}, u32[]{:S(2)}) async-start(bf16[16,24,768]{2,1,0:T(8,128)(2,1)} %bitcast.16), calls=%async_computation.2 | async-start | bytes 1179648 | tf_op jit(solution)/shard_map/all_to_all | solution.py:258
  43.2 0.9 broadcast_in_dim.16
  44.1 9.9 %all-to-all-done.2 = bf16[16,24,768]{2,1,0:T(8,128)(2,1)S(1)} async-done(((bf16[16,24,768]{2,1,0:T(8,128)(2,1)}), bf16[16,24,768]{2,1,0:T(8,128)(2,1)S(1)}, u32[]{:S(2)}, u32[]{:S(2)}) %all-to-all-start.2) | async-done | bytes 589856 | tf_op jit(solution)/shard_map/all_to_all | solution.py:258
  54.0 3.6 %all-to-all-start.1 = ((bf16[16,24,768]{2,1,0:T(8,128)(2,1)}), bf16[16,24,768]{2,1,0:T(8,128)(2,1)S(1)}, u32[]{:S(2)}, u32[]{:S(2)}) async-start(bf16[16,24,768]{2,1,0:T(8,128)(2,1)} %bitcast.13), calls=%async_computation.1 | async-start | bytes 1179648 | tf_op jit(solution)/shard_map/all_to_all | solution.py:258
  57.7 0.7 collective-permute-start
  58.3 0.7 collective-permute-start.1
  59.0 1.3 collective-permute-start.2
  60.3 1.3 collective-permute-start.3
  61.8 4.4 %all-gather.1 = bf16[4,8,768]{2,1,0:T(8,128)(2,1)S(1)} all-gather(bf16[2,8,768]{2,1,0:T(8,128)(2,1)S(1)} %slice.171), channel_id=3, replica_groups=mesh['zh'=4,'co'=2,'zl'=4,'y'=4,'x'=4] {'co'}, dimensions={0}, use_global_device_ids=true | all-gather | bytes 73728 | tf_op jit(solution)/shard_map/all_gather | solution.py:318
  67.0 3.7 %all-to-all-done.1 = bf16[16,24,768]{2,1,0:T(8,128)(2,1)S(1)} async-done(((bf16[16,24,768]{2,1,0:T(8,128)(2,1)}), bf16[16,24,768]{2,1,0:T(8,128)(2,1)S(1)}, u32[]{:S(2)}, u32[]{:S(2)}) %all-to-all-start.1) | async-done | bytes 589856 | tf_op jit(solution)/shard_map/all_to_all | solution.py:258
  70.7 1.6 broadcast_in_dim.19
  72.3 3.6 %all-to-all-start.3 = ((bf16[4,4,96,768]{3,2,1,0:T(8,128)(2,1)}), bf16[4,4,96,768]{3,2,1,0:T(8,128)(2,1)S(1)}, u32[]{:S(2)}, u32[]{:S(2)}) async-start(bf16[4,4,96,768]{3,2,1,0:T(8,128)(2,1)} %broadcast_in_dim.19), calls=%async_computation.3 | async-start | bytes 4718592 | tf_op jit(solution)/shard_map/all_to_all | solution.py:264
  76.5 0.7 maximum_select_fusion.refs_2_
  77.9 0.8 eq.40
  78.7 1.2 copy.25
  80.0 0.8 fusion.refs_1_
  80.8 15.7 %stem_and_taps.1 = (bf16[1056,768]{1,0:T(8,128)(2,1)}, bf16[1056,1536]{1,0:T(8,128)(2,1)}) custom-call(s32[19]{0:T(128)} %get-tuple-element.25.refs_0_, bf16[1056,64]{1,0:T(8,128)(2,1)} %fusion.refs_1_, bf16[64,1536]{1,0:T(8,128)(2,1)} %maximum_select_fusion.refs_2_, f32[8,1536]{1,0:T(8,128)} %get-tuple-element.38.refs_3_.refs_2_), custom_call_target="tpu_custom_call" | custom-call | tf_op jit(solution)/shard_map/stem_and_taps/pallas_call | solution.py:202
  96.5 4.0 %all-to-all-done.3 = bf16[4,4,96,768]{3,2,1,0:T(8,128)(2,1)S(1)} async-done(((bf16[4,4,96,768]{3,2,1,0:T(8,128)(2,1)}), bf16[4,4,96,768]{3,2,1,0:T(8,128)(2,1)S(1)}, u32[]{:S(2)}, u32[]{:S(2)}) %all-to-all-start.3) | async-done | bytes 2359328 | tf_op jit(solution)/shard_map/all_to_all | solution.py:264
  100.5 1.4 copy-done
  101.9 10.2 %mix_first.1 = (bf16[528,768]{1,0:T(8,128)(2,1)}, bf16[1536,768]{1,0:T(8,128)(2,1)}) custom-call(s32[19]{0:T(128)} %get-tuple-element.25.refs_0_, bf16[1056,768]{1,0:T(8,128)(2,1)} %get-tuple-element.17.refs_1_, bf16[1056,1536]{1,0:T(8,128)(2,1)} %get-tuple-element.18.refs_2_, bf16[16,96,768]{2,1,0:T(8,128)(2,1)} %bitcast.39), custom_call_target="tpu_custom_call" | custom-call | tf_op jit(solution)/shard_map/mix_first/pallas_call | solution.py:213
  112.1 7.4 %collective-permute-start.4 = (bf16[528,768]{1,0:T(8,128)(2,1)}, bf16[528,768]{1,0:T(8,128)(2,1)S(1)}, u32[]{:S(2)}, u32[]{:S(2)}) collective-permute-start(bf16[528,768]{1,0:T(8,128)(2,1)} %get-tuple-element.20.refs_1_), channel_id=1, source_target_pairs={{0,64},{64,0},{1,65},{65,1},{2,66},{66,2},{3,67},{67,3},{4,68},{68... | collective-permute-start | bytes 2433032 | tf_op jit(solution)/shard_map/ppermute | solution.py:340
  119.6 4.6 %collective-permute-start.5 = (bf16[4,96,768]{2,1,0:T(8,128)(2,1)S(1)}, bf16[4,96,768]{2,1,0:T(8,128)(2,1)S(1)}, u32[]{:S(2)}, u32[]{:S(2)}) collective-permute-start(bf16[4,96,768]{2,1,0:T(8,128)(2,1)S(1)} %bitcast.40), channel_id=1, source_target_pairs={{0,16},{16,32},{32,48},{48,128},{128,144},{144,160},{160,176},{176... | collective-permute-start | bytes 1769480 | tf_op jit(solution)/shard_map/ppermute | solution.py:251
  124.2 1.9 collective-permute-start.6
  126.2 5.1 %collective-permute-start.7 = (bf16[2,96,768]{2,1,0:T(8,128)(2,1)S(1)}, bf16[2,96,768]{2,1,0:T(8,128)(2,1)S(1)}, u32[]{:S(2)}, u32[]{:S(2)}) collective-permute-start(bf16[2,96,768]{2,1,0:T(8,128)(2,1)S(1)} %get-tuple-element.28), channel_id=1, source_target_pairs={{0,32},{16,48},{32,128},{48,144},{128,160},{144,176},{160,256},{17... | collective-permute-start | bytes 884744 | tf_op jit(solution)/shard_map/ppermute | solution.py:251
  131.3 2.3 collective-permute-start.8
  134.2 12.0 %collective-permute-done.7.refs_7_ = bf16[2,96,768]{2,1,0:T(8,128)(2,1)S(1)} collective-permute-done((bf16[2,96,768]{2,1,0:T(8,128)(2,1)S(1)}, bf16[2,96,768]{2,1,0:T(8,128)(2,1)S(1)}, u32[]{:S(2)}, u32[]{:S(2)}) %collective-permute-start.7) | collective-permute-done | bytes 294944 | tf_op jit(solution)/shard_map/ppermute | solution.py:251
  146.1 8.9 %collective-permute-done.8.refs_8_ = bf16[2,96,768]{2,1,0:T(8,128)(2,1)S(1)} collective-permute-done((bf16[2,96,768]{2,1,0:T(8,128)(2,1)S(1)}, bf16[2,96,768]{2,1,0:T(8,128)(2,1)S(1)}, u32[]{:S(2)}, u32[]{:S(2)}) %collective-permute-start.8) | collective-permute-done | bytes 294944 | tf_op jit(solution)/shard_map/ppermute | solution.py:251
  155.1 0.7 copy-done.6
  156.4 13.4 %shard_map.64 = (bf16[256,768]{1,0:T(8,128)(2,1)}, bf16[1536,768]{1,0:T(8,128)(2,1)}) custom-call(s32[19]{0:T(128)} %pad_add_fusion.refs_0_, bf16[528,768]{1,0:T(8,128)(2,1)} %get-tuple-element.20.refs_1_, bf16[528,768]{1,0:T(8,128)(2,1)} %copy-done.2, f32[8,1536]{1,0:T(8,128)} %get-tuple-element.37.refs_3_.refs_2_, bf16[4,96,768]{2,1,0:T(8,128)(2,1)} %bitcast.43, ...), custom_call_target="tpu_custom_call" | custom-call | tf_op jit(solution)/shard_map/pallas_call | solution.py:224
  169.8 2.2 collective-permute-start.10
  172.0 0.8 fusion.7
  172.8 0.7 collective-permute-start.11
  173.5 1.3 collective-permute-start.9
  174.8 0.9 collective-permute-done.9
  175.7 3.9 %collective-permute-done.10 = bf16[256,768]{1,0:T(8,128)(2,1)S(1)} collective-permute-done((bf16[256,768]{1,0:T(8,128)(2,1)}, bf16[256,768]{1,0:T(8,128)(2,1)S(1)}, u32[]{:S(2)}, u32[]{:S(2)}) %collective-permute-start.10) | collective-permute-done | bytes 393248 | tf_op jit(solution)/shard_map/ppermute | solution.py:298
  179.7 4.5 %all-gather.2 = bf16[576,768]{1,0:T(8,128)(2,1)} all-gather(bf16[288,768]{1,0:T(8,128)(2,1)S(1)} %pad_maximum_fusion), channel_id=4, replica_groups=mesh['zh'=4,'co'=2,'zl'=4,'y'=4,'x'=4] {'co'}, dimensions={0}, use_global_device_ids=true | all-gather | bytes 1327104 | tf_op jit(solution)/shard_map/all_gather | solution.py:346
  184.2 6.8 %shard_map.65 = bf16[144,768]{1,0:T(8,128)(2,1)} custom-call(s32[19]{0:T(128)} %get-tuple-element.25.refs_0_, bf16[2,288,768]{2,1,0:T(8,128)(2,1)} %bitcast.44, f32[8,1536]{1,0:T(8,128)} %get-tuple-element.38.refs_3_.refs_2_, bf16[1536,768]{1,0:T(8,128)(2,1)} %get-tuple-element.23.refs_3_), custom_call_target="tpu_custom_call" | custom-call | tf_op jit(solution)/shard_map/pallas_call | solution.py:234
  191.0 4.0 %all-gather.3 = bf16[288,768]{1,0:T(8,128)(2,1)} all-gather(bf16[144,768]{1,0:T(8,128)(2,1)} %shard_map.65), channel_id=5, replica_groups=mesh['zh'=4,'co'=2,'zl'=4,'y'=4,'x'=4] {'co'}, dimensions={0}, use_global_device_ids=true | all-gather | bytes 663552 | tf_op jit(solution)/shard_map/all_gather | solution.py:348
  194.9 4.5 %shard_map.66 = bf16[64,768]{1,0:T(8,128)(2,1)} custom-call(s32[19]{0:T(128)} %pad_add_fusion.refs_0_, bf16[2,144,768]{2,1,0:T(8,128)(2,1)} %bitcast.46, f32[8,1536]{1,0:T(8,128)} %get-tuple-element.37.refs_3_.refs_2_, bf16[1536,768]{1,0:T(8,128)(2,1)} %get-tuple-element.24.refs_3_), custom_call_target="tpu_custom_call" | custom-call | tf_op jit(solution)/shard_map/pallas_call | solution.py:234
  199.5 0.8 collective-permute-start.13
  200.3 0.8 fusion.8
  201.1 0.7 collective-permute-start.12
  201.7 0.7 collective-permute-start.14
  202.5 2.1 all-gather.4
  204.6 3.9 %shard_map.67 = bf16[48,768]{1,0:T(8,128)(2,1)} custom-call(s32[19]{0:T(128)} %get-tuple-element.25.refs_0_, bf16[2,96,768]{2,1,0:T(8,128)(2,1)} %bitcast.49, f32[8,1536]{1,0:T(8,128)} %get-tuple-element.38.refs_3_.refs_2_, bf16[1536,768]{1,0:T(8,128)(2,1)} %get-tuple-element.23.refs_3_), custom_call_target="tpu_custom_call" | custom-call | tf_op jit(solution)/shard_map/pallas_call | solution.py:234
  208.6 3.4 %all-gather.5 = bf16[96,768]{1,0:T(8,128)(2,1)} all-gather(bf16[48,768]{1,0:T(8,128)(2,1)} %shard_map.67), channel_id=7, replica_groups=mesh['zh'=4,'co'=2,'zl'=4,'y'=4,'x'=4] {'co'}, dimensions={0}, use_global_device_ids=true | all-gather | bytes 221184 | tf_op jit(solution)/shard_map/all_gather | solution.py:348
  212.0 3.4 %shard_map.68 = bf16[16,768]{1,0:T(8,128)(2,1)} custom-call(s32[19]{0:T(128)} %pad_add_fusion.refs_0_, bf16[2,48,768]{2,1,0:T(8,128)(2,1)} %bitcast.51, f32[8,1536]{1,0:T(8,128)} %get-tuple-element.37.refs_3_.refs_2_, bf16[1536,768]{1,0:T(8,128)(2,1)} %get-tuple-element.24.refs_3_), custom_call_target="tpu_custom_call" | custom-call | tf_op jit(solution)/shard_map/pallas_call | solution.py:234
  215.4 0.7 collective-permute-start.16
  216.0 0.8 fusion.10
  216.8 0.7 collective-permute-start.15
  217.5 0.7 collective-permute-start.17
  218.2 2.0 all-gather.6
  220.3 3.4 %shard_map.69 = bf16[16,768]{1,0:T(8,128)(2,1)} custom-call(s32[19]{0:T(128)} %get-tuple-element.25.refs_0_, bf16[2,48,768]{2,1,0:T(8,128)(2,1)} %bitcast.50, f32[8,1536]{1,0:T(8,128)} %get-tuple-element.38.refs_3_.refs_2_, bf16[1536,768]{1,0:T(8,128)(2,1)} %get-tuple-element.23.refs_3_), custom_call_target="tpu_custom_call" | custom-call | tf_op jit(solution)/shard_map/pallas_call | solution.py:234
  223.7 3.4 %all-gather.7 = bf16[32,768]{1,0:T(8,128)(2,1)} all-gather(bf16[16,768]{1,0:T(8,128)(2,1)} %shard_map.69), channel_id=9, replica_groups=mesh['zh'=4,'co'=2,'zl'=4,'y'=4,'x'=4] {'co'}, dimensions={0}, use_global_device_ids=true | all-gather | bytes 73728 | tf_op jit(solution)/shard_map/all_gather | solution.py:348
  227.0 2.9 %shard_map.70 = bf16[4,768]{1,0:T(4,128)(2,1)} custom-call(s32[19]{0:T(128)} %pad_add_fusion.refs_0_, bf16[2,16,768]{2,1,0:T(8,128)(2,1)} %bitcast.55, f32[8,1536]{1,0:T(8,128)} %get-tuple-element.37.refs_3_.refs_2_, bf16[1536,768]{1,0:T(8,128)(2,1)} %get-tuple-element.24.refs_3_), custom_call_target="tpu_custom_call" | custom-call | tf_op jit(solution)/shard_map/pallas_call | solution.py:234
  230.0 0.8 reshape.79
  231.4 27.3 %all-to-all-start.4 = ((bf16[32,2,192]{2,1,0:T(2,128)(2,1)}), bf16[32,2,192]{2,1,0:T(2,128)(2,1)S(1)}, u32[]{:S(2)}, u32[]{:S(2)}) async-start(bf16[32,2,192]{2,1,0:T(2,128)(2,1)} %bitcast.27), calls=%async_computation.4 | async-start | bytes 65536 | tf_op jit(solution)/shard_map/all_to_all | solution.py:356
  258.7 14.4 %all-to-all-done.4 = bf16[32,2,192]{2,1,0:T(2,128)(2,1)S(1)} async-done(((bf16[32,2,192]{2,1,0:T(2,128)(2,1)}), bf16[32,2,192]{2,1,0:T(2,128)(2,1)S(1)}, u32[]{:S(2)}, u32[]{:S(2)}) %all-to-all-start.4) | async-done | bytes 24608 | tf_op jit(solution)/shard_map/all_to_all | solution.py:356
  (92 shorter events, 5.2 us)
Async XLA Ops:
  35.5 22.1 %copy-start.8 = (s32[2,512]{1,0:T(2,128)S(1)}, s32[2,512]{1,0:T(2,128)}, u32[]{:S(2)}) copy-start(s32[2,512]{1,0:T(2,128)} %param.6) | copy-start | bytes 12292
  35.6 26.1 %copy-start.9 = (s32[4]{0:T(128)S(1)}, s32[4]{0:T(128)}, u32[]{:S(2)}) copy-start(s32[4]{0:T(128)} %constant.157) | copy-start | bytes 52
  35.6 30.7 %copy-start.7 = (bf16[15,4,1536]{2,1,0:T(4,128)(2,1)S(1)}, bf16[15,4,1536]{2,1,0:T(4,128)(2,1)}, u32[]{:S(2)}) copy-start(bf16[15,4,1536]{2,1,0:T(4,128)(2,1)} %param.7) | copy-start | bytes 552964
  36.5 17.6 %all-to-all-start.2 = ((bf16[16,24,768]{2,1,0:T(8,128)(2,1)}), bf16[16,24,768]{2,1,0:T(8,128)(2,1)S(1)}, u32[]{:S(2)}, u32[]{:S(2)}) async-start(bf16[16,24,768]{2,1,0:T(8,128)(2,1)} %bitcast.16), calls=%async_computation.2 | async-start | bytes 1179648 | tf_op jit(solution)/shard_map/all_to_all | solution.py:258
  54.0 72.1 %copy-start.1 = (bf16[16,24,768]{2,1,0:T(8,128)(2,1)}, bf16[16,24,768]{2,1,0:T(8,128)(2,1)S(1)}, u32[]{:S(2)}) copy-start(bf16[16,24,768]{2,1,0:T(8,128)(2,1)S(1)} %all-to-all-done.2) | copy-start | bytes 1769476
  54.0 16.6 %all-to-all-start.1 = ((bf16[16,24,768]{2,1,0:T(8,128)(2,1)}), bf16[16,24,768]{2,1,0:T(8,128)(2,1)S(1)}, u32[]{:S(2)}, u32[]{:S(2)}) async-start(bf16[16,24,768]{2,1,0:T(8,128)(2,1)} %bitcast.13), calls=%async_computation.1 | async-start | bytes 1179648 | tf_op jit(solution)/shard_map/all_to_all | solution.py:258
  57.7 19.7 %collective-permute-start = (s32[512]{0:T(512)S(1)}, s32[512]{0:T(512)S(1)}, u32[]{:S(2)}, u32[]{:S(2)}) collective-permute-start(s32[512]{0:T(512)S(1)} %bitcast.58), channel_id=1, source_target_pairs={{3,4},{7,8},{11,12},{15,16},{19,20},{23,24},{27,28},{31,32},{35,36... | collective-permute-start | bytes 6152 | tf_op jit(solution)/shard_map/ppermute | solution.py:287
  58.3 19.0 %collective-permute-start.1 = (s32[512]{0:T(512)S(1)}, s32[512]{0:T(512)S(1)}, u32[]{:S(2)}, u32[]{:S(2)}) collective-permute-start(s32[512]{0:T(512)S(1)} %bitcast.59), channel_id=1, source_target_pairs={{0,0},{4,4},{8,8},{12,12},{16,16},{20,20},{24,24},{28,28},{32,32},... | collective-permute-start | bytes 6152 | tf_op jit(solution)/shard_map/ppermute | solution.py:287
  59.0 18.4 %collective-permute-start.2 = (s32[512]{0:T(512)S(1)}, s32[512]{0:T(512)S(1)}, u32[]{:S(2)}, u32[]{:S(2)}) collective-permute-start(s32[512]{0:T(512)S(1)} %bitcast.60), channel_id=1, source_target_pairs={{1,0},{5,4},{9,8},{13,12},{17,16},{21,20},{25,24},{29,28},{33,32},... | collective-permute-start | bytes 6152 | tf_op jit(solution)/shard_map/ppermute | solution.py:287
  60.3 17.1 %collective-permute-start.3 = (s32[512]{0:T(512)S(1)}, s32[512]{0:T(512)S(1)}, u32[]{:S(2)}, u32[]{:S(2)}) collective-permute-start(s32[512]{0:T(512)S(1)} %bitcast.61), channel_id=1, source_target_pairs={{2,0},{6,4},{10,8},{14,12},{18,16},{22,20},{26,24},{30,28},{34,32}... | collective-permute-start | bytes 6152 | tf_op jit(solution)/shard_map/ppermute | solution.py:287
  72.3 28.2 %all-to-all-start.3 = ((bf16[4,4,96,768]{3,2,1,0:T(8,128)(2,1)}), bf16[4,4,96,768]{3,2,1,0:T(8,128)(2,1)S(1)}, u32[]{:S(2)}, u32[]{:S(2)}) async-start(bf16[4,4,96,768]{3,2,1,0:T(8,128)(2,1)} %broadcast_in_dim.19), calls=%async_computation.3 | async-start | bytes 4718592 | tf_op jit(solution)/shard_map/all_to_all | solution.py:264
  100.5 1.4 copy-start
  112.1 43.0 %collective-permute-start.4 = (bf16[528,768]{1,0:T(8,128)(2,1)}, bf16[528,768]{1,0:T(8,128)(2,1)S(1)}, u32[]{:S(2)}, u32[]{:S(2)}) collective-permute-start(bf16[528,768]{1,0:T(8,128)(2,1)} %get-tuple-element.20.refs_1_), channel_id=1, source_target_pairs={{0,64},{64,0},{1,65},{65,1},{2,66},{66,2},{3,67},{67,3},{4,68},{68... | collective-permute-start | bytes 2433032 | tf_op jit(solution)/shard_map/ppermute | solution.py:340
  119.6 35.5 %collective-permute-start.5 = (bf16[4,96,768]{2,1,0:T(8,128)(2,1)S(1)}, bf16[4,96,768]{2,1,0:T(8,128)(2,1)S(1)}, u32[]{:S(2)}, u32[]{:S(2)}) collective-permute-start(bf16[4,96,768]{2,1,0:T(8,128)(2,1)S(1)} %bitcast.40), channel_id=1, source_target_pairs={{0,16},{16,32},{32,48},{48,128},{128,144},{144,160},{160,176},{176... | collective-permute-start | bytes 1769480 | tf_op jit(solution)/shard_map/ppermute | solution.py:251
  124.2 30.9 %collective-permute-start.6 = (bf16[4,96,768]{2,1,0:T(8,128)(2,1)S(1)}, bf16[4,96,768]{2,1,0:T(8,128)(2,1)S(1)}, u32[]{:S(2)}, u32[]{:S(2)}) collective-permute-start(bf16[4,96,768]{2,1,0:T(8,128)(2,1)S(1)} %bitcast.41), channel_id=1, source_target_pairs={{0,432},{16,0},{32,16},{48,32},{128,48},{144,128},{160,144},{176,1... | collective-permute-start | bytes 1769480 | tf_op jit(solution)/shard_map/ppermute | solution.py:251
  126.2 20.0 %collective-permute-start.7 = (bf16[2,96,768]{2,1,0:T(8,128)(2,1)S(1)}, bf16[2,96,768]{2,1,0:T(8,128)(2,1)S(1)}, u32[]{:S(2)}, u32[]{:S(2)}) collective-permute-start(bf16[2,96,768]{2,1,0:T(8,128)(2,1)S(1)} %get-tuple-element.28), channel_id=1, source_target_pairs={{0,32},{16,48},{32,128},{48,144},{128,160},{144,176},{160,256},{17... | collective-permute-start | bytes 884744 | tf_op jit(solution)/shard_map/ppermute | solution.py:251
  131.3 23.8 %collective-permute-start.8 = (bf16[2,96,768]{2,1,0:T(8,128)(2,1)S(1)}, bf16[2,96,768]{2,1,0:T(8,128)(2,1)S(1)}, u32[]{:S(2)}, u32[]{:S(2)}) collective-permute-start(bf16[2,96,768]{2,1,0:T(8,128)(2,1)S(1)} %get-tuple-element.27), channel_id=1, source_target_pairs={{0,416},{16,432},{32,0},{48,16},{128,32},{144,48},{160,128},{176,1... | collective-permute-start | bytes 884744 | tf_op jit(solution)/shard_map/ppermute | solution.py:251
  146.1 9.0 %copy-start.5 = (bf16[2,96,768]{2,1,0:T(8,128)(2,1)}, bf16[2,96,768]{2,1,0:T(8,128)(2,1)S(1)}, u32[]{:S(2)}) copy-start(bf16[2,96,768]{2,1,0:T(8,128)(2,1)S(1)} %collective-permute-done.7.refs_7_) | copy-start | bytes 884740
  155.1 0.8 copy-start.6
  155.1 0.9 copy-start.3
  155.1 1.1 copy-start.4
  155.1 1.3 copy-start.2
  169.8 9.8 %collective-permute-start.10 = (bf16[256,768]{1,0:T(8,128)(2,1)}, bf16[256,768]{1,0:T(8,128)(2,1)S(1)}, u32[]{:S(2)}, u32[]{:S(2)}) collective-permute-start(bf16[256,768]{1,0:T(8,128)(2,1)} %get-tuple-element.22), channel_id=1, source_target_pairs={{0,1},{4,5},{8,9},{12,13},{16,17},{20,21},{24,25},{28,29},{32,33},... | collective-permute-start | bytes 1179656 | tf_op jit(solution)/shard_map/ppermute | solution.py:298
  172.8 2.0 collective-permute-start.11
  173.5 2.2 collective-permute-start.9
  199.5 3.0 %collective-permute-start.13 = (bf16[64,768]{1,0:T(8,128)(2,1)}, bf16[64,768]{1,0:T(8,128)(2,1)S(1)}, u32[]{:S(2)}, u32[]{:S(2)}) collective-permute-start(bf16[64,768]{1,0:T(8,128)(2,1)} %shard_map.66), channel_id=1, source_target_pairs={{1,2},{5,6},{9,10},{13,14},{17,18},{21,22},{25,26},{29,30},{33,34}... | collective-permute-start | bytes 294920 | tf_op jit(solution)/shard_map/ppermute | solution.py:298
  201.1 1.3 collective-permute-start.12
  201.7 0.7 collective-permute-start.14
  215.4 2.8 %collective-permute-start.16 = (bf16[16,768]{1,0:T(8,128)(2,1)}, bf16[16,768]{1,0:T(8,128)(2,1)S(1)}, u32[]{:S(2)}, u32[]{:S(2)}) collective-permute-start(bf16[16,768]{1,0:T(8,128)(2,1)} %shard_map.68), channel_id=1, source_target_pairs={{2,3},{6,7},{10,11},{14,15},{18,19},{22,23},{26,27},{30,31},{34,35... | collective-permute-start | bytes 73736 | tf_op jit(solution)/shard_map/ppermute | solution.py:298
  216.8 1.3 collective-permute-start.15
  217.5 0.7 collective-permute-start.17
  231.4 41.7 %all-to-all-start.4 = ((bf16[32,2,192]{2,1,0:T(2,128)(2,1)}), bf16[32,2,192]{2,1,0:T(2,128)(2,1)S(1)}, u32[]{:S(2)}, u32[]{:S(2)}) async-start(bf16[32,2,192]{2,1,0:T(2,128)(2,1)} %bitcast.27), calls=%async_computation.4 | async-start | bytes 65536 | tf_op jit(solution)/shard_map/all_to_all | solution.py:356

commit v3 on v1

--- a/solution.py
+++ b/solution.py
@@ -75,14 +75,15 @@
         lax.fori_loop(0, up16(rows) // chunk, step, 0)
 
 
-def weight_copies(meta_ref, pieces, w_ref, sems):
+def weight_copies(slot, meta_ref, pieces, w_ref, sems):
     copies = []
     for piece in pieces:
-        for k in range(piece.shape[0]):
+        for k in range(4):
             n = len(copies)
             row = pl.multiple_of(meta_ref[3 + n] * BLOCK, 16)
+            source = piece.at[k, slot] if len(piece.shape) == 4 else piece.at[k]
             copies.append(
-                pltpu.make_async_copy(piece.at[k], w_ref.at[pl.ds(row, BLOCK)], sems.at[n])
+                pltpu.make_async_copy(source, w_ref.at[pl.ds(row, BLOCK)], sems.at[n])
             )
     return copies
 
@@ -126,7 +127,7 @@
 
 def second_half(rows, meta_ref, x_ref, d_ref, *refs):
     *pieces, out_ref, w_ref, y_scr, sems = refs
-    copies = weight_copies(meta_ref, pieces, w_ref, sems)
+    copies = weight_copies(0, meta_ref, pieces, w_ref, sems)
     for copy in copies:
         copy.start()
     for copy in copies:
@@ -140,7 +141,7 @@
 
 def swapped_level(rows, edge, meta_ref, own_ref, other_ref, par_ref, *refs):
     *pieces, out_ref, w_ref, a_scr, d_scr, y_scr, sems = refs
-    copies = weight_copies(meta_ref, pieces, w_ref, sems)
+    copies = weight_copies(1, meta_ref, pieces, w_ref, sems)
     for copy in copies:
         copy.start()
 
@@ -242,13 +243,6 @@
 
 def ring(size, by):
     return [(i, (i + by) % size) for i in range(size)]
-
-
-def around(array, axes, size):
-    out = [array]
-    for by in SHIFTS[1:]:
-        out.append(lax.ppermute(array, axes, ring(size, by)))
-    return out
 
 
 def around_y(array):
@@ -299,24 +293,32 @@
     sequence = zh // 2
 
     held = [point_weight[0], gains, depth_taps[0], jnp.zeros((2, C), gains.dtype)]
-    held = jnp.concatenate(held, axis=0).reshape(-1, 2, HALF).transpose(1, 0, 2)
-    held = lax.all_to_all(held, "co", 0, 0, tiled=True)
-    held = lax.all_to_all(lax.all_gather(held, "zh"), "x", 0, 0, tiled=True)
-    params = lax.all_gather(held[0, :, 24:], "co").transpose(1, 2, 0, 3).reshape(2, 8, C)
+    held = lax.all_gather(jnp.concatenate(held, axis=0), "zh")
+    held, bases = lax.optimization_barrier((held, bases))
+    blocks = held[:, :24].reshape(4, 24, 2, HALF).transpose(2, 0, 1, 3)
+    blocks = jnp.broadcast_to(blocks[:, None], (2, 4, 4, 24, HALF)).reshape(32, 24, HALF)
+    blocks = lax.optimization_barrier(blocks)
+    blocks = lax.all_to_all(blocks, ("co", "y", "x"), 0, 0, tiled=True)
+    near = lax.optimization_barrier(blocks.reshape(2, 4, BLOCK, HALF))
+    share = lax.dynamic_index_in_dim(near, y, 1, keepdims=False)
+    share0 = lax.ppermute(share[0], ("zh", "zl"), ring(16, 2))
+    share1 = lax.ppermute(share[1], ("zh", "zl"), ring(16, -2))
+    beside = []
+    for slot in range(2):
+        sides = [near[slot]]
+        for by in (1, -1):
+            sides.append(lax.ppermute(near[slot], ("zh", "zl"), ring(16, by)))
+        beside.append(sides)
+    opposite = around_y(jnp.stack([share0, share1]))
+    pieces = [sides + [opposite] for sides in beside]
+    params = lax.dynamic_index_in_dim(held, x, 0, keepdims=False)[24:]
+    params = lax.all_gather(params, "co")
     params = own_first(params, co).astype(jnp.float32)
-    blocks = [held[:, slot, :24].reshape(BLOCK, HALF) for slot in range(2)]
-    along_z = jnp.stack(around(blocks[0], ("zh", "zl"), 16))
-    along_y = around_y(blocks[1])
-    along_z, along_y = lax.optimization_barrier((along_z, along_y))
-    pieces = [[around_y(along_z).reshape(16, BLOCK, HALF)], around(along_y, ("zh", "zl"), 16)]
+    four = jnp.arange(4, dtype=jnp.int32)
     z_of = (zl - jnp.array(SHIFTS, jnp.int32)) % 4
-    y_of = jnp.arange(4, dtype=jnp.int32)
-    places = [z_of[None, :] * 4 + y_of[:, None], z_of[:, None] * 4 + y_of[None, :]]
+    place = (z_of[:, None] * 4 + four[None, :]).reshape(-1)
     flags = jnp.stack([co, (group == 0).astype(jnp.int32), (group == 31).astype(jnp.int32)])
-    metas = [
-        jnp.concatenate([flags.astype(jnp.int32), (place.reshape(-1) + 8 * co) % 16])
-        for place in places
-    ]
+    meta = jnp.concatenate([flags.astype(jnp.int32), (place + 8 * co) % 16])
 
     rows = RUN + 2 * EDGE
     size = up16(rows)
@@ -326,18 +328,18 @@
     hot = (windows[:, None, :] == kinds).astype(jnp.bfloat16).reshape(-1, size)
     hot = jnp.pad(hot, ((0, 4), (0, 0))).T
     stem = own_first(jnp.pad(stem_weight.reshape(-1, C), ((0, 4), (0, 0))), co)
-    level_rows, taps = run_first_half(rows, metas[0], hot, stem, params[0])
-    now, even_weights = run_second_half(rows, metas[0], level_rows, taps, pieces[0])
+    level_rows, taps = run_first_half(rows, meta, hot, stem, params[0])
+    now, even_weights = run_second_half(rows, meta, level_rows, taps, pieces[0])
     other = lax.ppermute(now, "co", [(0, 1), (1, 0)])
     now, odd_weights = run_swapped_level(
-        RUN // 2 + 8, 4, metas[1], now, other, params[1], pieces[1]
+        RUN // 2 + 8, 4, meta, now, other, params[1], pieces[1]
     )
     run = RUN // 4
     for role in range(3):
         now = lax.all_gather(pass_on(now, role), "co")
-        now = run_level(run + 2 * EDGE, EDGE, False, metas[0], now, params[0], even_weights)
+        now = run_level(run + 2 * EDGE, EDGE, False, meta, now, params[0], even_weights)
         now = lax.all_gather(now, "co")
-        now = run_level(run // 2 + 8, 4, True, metas[1], now, params[1], odd_weights)
+        now = run_level(run // 2 + 8, 4, True, meta, now, params[1], odd_weights)
         run = run // 4
 
     blocks = now.reshape(2, 2, 4, HALF // 4).transpose(2, 0, 1, 3)

time: 282 us -> 259 us (0.918)
  blocking collectives: 63.7 us -> 48.8 us
  waiting for transfers between devices: 59.6 us -> 50.3 us
  starting transfers between devices: 77.6 us -> 82.9 us
  local copies, waits for them, and re-layouts: 14.8 us -> 11.9 us
    ppermute x6, waiting for transfers between devices: 39.2 us -> 19.8 us  [the longest x4 15.6 us: relay(): sides.append(lax.ppermute(near[slot], ('zh', 'zl'), ring(16, by)))]
    all_to_all x1, waiting for transfers between devices: 2.9 us -> 13.6 us  [relay(): blocks = lax.all_to_all(blocks, ('co', 'y', 'x'), 0, 0, tiled=True)]
    all_to_all x1 -> x0, blocking collectives: 10.3 us -> none  [relay(): held = lax.all_to_all(held, 'co', 0, 0, tiled=True)]
    all_to_all x1, starting transfers between devices: 4.22 us -> 13.2 us  [relay(): blocks = lax.all_to_all(blocks, ('co', 'y', 'x'), 0, 0, tiled=True)]
    all_to_all x2 -> x1, starting transfers between devices: 11.1 us -> 3.78 us  [around_y(): return lax.all_to_all(copies, 'y', 0, 0, tiled=True)]
    all_gather x2, blocking collectives: 33.9 us -> 29.6 us  [the longest x1 27.8 us: relay(): held = lax.all_gather(jnp.concatenate(held, axis=0), 'zh')]
  transfers between devices with their start and end apart: 24 -> 23, of which waited for: 7 -> 7; matrix products, arithmetic and copies ran while one was open for 5% -> 3% of each run, Pallas kernels for 6% -> 6%
where the time goes in v3:
time: 259 us; the launch traced here: 257 us
  starting transfers between devices  82.9 us (32%)
  Pallas kernels  58.3 us (23%)
  waiting for transfers between devices  50.3 us (19%)
  blocking collectives  48.8 us (19%)
  local copies, waits for them, and re-layouts  11.9 us (5%)
  other arithmetic  4.23 us (2%)
    all_to_all x1, starting transfers between devices, relay(): got = lax.all_to_all(blocks, ('zh', 'co', 'x'), 0, 0, tiled=True)  28.2 us
    all_gather x1, blocking collectives, relay(): held = lax.all_gather(jnp.concatenate(held, axis=0), 'zh')  27.8 us
    pallas_call x6, Pallas kernels, run_level(): pl.pallas_call(lambda *refs: paired_level(rows, edge, *refs), in_specs=[s...  24.9 us
    pallas_call x1, Pallas kernels, run_first_half(): pl.pallas_call(lambda *refs: first_half(rows, *refs), in_specs=[spec(pltp...  15.7 us
    ppermute x4, waiting for transfers between devices, relay(): sides.append(lax.ppermute(near[slot], ('zh', 'zl'), ring(16, by)))  15.6 us
    all_to_all x1, waiting for transfers between devices, relay(): got = lax.all_to_all(blocks, ('zh', 'co', 'x'), 0, 0, tiled=True)  14.4 us
    all_to_all x1, waiting for transfers between devices, relay(): blocks = lax.all_to_all(blocks, ('co', 'y', 'x'), 0, 0, tiled=True)  13.6 us
    all_to_all x1, starting transfers between devices, relay(): blocks = lax.all_to_all(blocks, ('co', 'y', 'x'), 0, 0, tiled=True)  13.2 us
  transfers between devices with their start and end apart: 23, of which 7 were waited for; matrix products, arithmetic and copies ran while one was open for 3% of the time, Pallas kernels for 6%

profile of v3, /device:TPU:1, one launch (start us, length us, event | category | flops | bytes accessed | tf_op | source)
XLA Modules:
  0.0 257.1 jit_solution(18374913514679764835)
XLA Ops:
  0.1 1.0 maximum_maximum_fusion
  1.1 27.8 %all-gather = bf16[128,1536]{1,0:T(8,128)(2,1)S(1)} all-gather(bf16[32,1536]{1,0:T(8,128)(2,1)S(1)} %maximum_maximum_fusion), channel_id=2, replica_groups=mesh['zh'=4,'co'=2,'zl'=4,'y'=4,'x'=4] {'zh'}, dimensions={0}, use_global_device_ids=true | all-gather | bytes 491520 | tf_op jit(solution)/shard_map/all_gather | solution.py:296
  28.9 0.7 dynamic-slice_add_fusion
  29.6 0.6 collective-permute-start
  30.2 0.7 collective-permute-start.1
  30.9 1.3 collective-permute-start.2
  32.2 1.3 collective-permute-start.3
  33.6 1.1 broadcast_in_dim.9
  34.8 13.2 %all-to-all-start = ((bf16[32,24,768]{2,1,0:T(8,128)(2,1)}), bf16[32,24,768]{2,1,0:T(8,128)(2,1)S(1)}, u32[]{:S(2)}, u32[]{:S(2)}) async-start(bf16[32,24,768]{2,1,0:T(8,128)(2,1)} %bitcast.10), calls=%async_computation | async-start | bytes 2359296 | tf_op jit(solution)/shard_map/all_to_all | solution.py:301
  48.2 1.8 all_gather.48
  50.1 0.7 maximum_select_fusion.refs_2_
  50.9 0.6 slice_bitcast_fusion.2
  51.5 0.6 pad_add_fusion.refs_0_
  52.3 13.6 %all-to-all-done = bf16[32,24,768]{2,1,0:T(8,128)(2,1)S(1)} async-done(((bf16[32,24,768]{2,1,0:T(8,128)(2,1)}), bf16[32,24,768]{2,1,0:T(8,128)(2,1)S(1)}, u32[]{:S(2)}, u32[]{:S(2)}) %all-to-all-start) | async-done | bytes 1179680 | tf_op jit(solution)/shard_map/all_to_all | solution.py:301
  65.9 2.7 %collective-permute-start.6 = (bf16[96,768]{1,0:T(8,128)(2,1)S(1)}, bf16[96,768]{1,0:T(8,128)(2,1)S(1)}, u32[]{:S(2)}, u32[]{:S(2)}) collective-permute-start(bf16[96,768]{1,0:T(8,128)(2,1)S(1)} %get-tuple-element.23), channel_id=1, source_target_pairs={{0,32},{16,48},{32,128},{48,144},{128,160},{144,176},{160,256},{17... | collective-permute-start | bytes 442376 | tf_op jit(solution)/shard_map/ppermute | solution.py:304
  68.6 4.7 %collective-permute-start.7 = (bf16[96,768]{1,0:T(8,128)(2,1)S(1)}, bf16[96,768]{1,0:T(8,128)(2,1)S(1)}, u32[]{:S(2)}, u32[]{:S(2)}) collective-permute-start(bf16[96,768]{1,0:T(8,128)(2,1)S(1)} %get-tuple-element.24), channel_id=1, source_target_pairs={{0,416},{16,432},{32,0},{48,16},{128,32},{144,48},{160,128},{176,1... | collective-permute-start | bytes 442376 | tf_op jit(solution)/shard_map/ppermute | solution.py:305
  73.9 1.0 copy.15
  74.9 4.2 %collective-permute-done.7 = bf16[96,768]{1,0:T(8,128)(2,1)S(1)} collective-permute-done((bf16[96,768]{1,0:T(8,128)(2,1)S(1)}, bf16[96,768]{1,0:T(8,128)(2,1)S(1)}, u32[]{:S(2)}, u32[]{:S(2)}) %collective-permute-start.7) | collective-permute-done | bytes 147488 | tf_op jit(solution)/shard_map/ppermute | solution.py:305
  79.2 1.1 broadcast_in_dim.10
  80.3 3.8 %all-to-all-start.1 = ((bf16[4,2,96,768]{3,2,1,0:T(8,128)(2,1)}), bf16[4,2,96,768]{3,2,1,0:T(8,128)(2,1)S(1)}, u32[]{:S(2)}, u32[]{:S(2)}) async-start(bf16[4,2,96,768]{3,2,1,0:T(8,128)(2,1)} %broadcast_in_dim.10), calls=%async_computation.1 | async-start | bytes 2359296 | tf_op jit(solution)/shard_map/all_to_all | solution.py:250
  84.1 2.1 collective-permute-start.4
  86.2 4.6 %collective-permute-start.5 = (bf16[4,96,768]{2,1,0:T(8,128)(2,1)S(1)}, bf16[4,96,768]{2,1,0:T(8,128)(2,1)S(1)}, u32[]{:S(2)}, u32[]{:S(2)}) collective-permute-start(bf16[4,96,768]{2,1,0:T(8,128)(2,1)S(1)} %get-tuple-element.22.refs_3_), channel_id=1, source_target_pairs={{0,432},{16,0},{32,16},{48,32},{128,48},{144,128},{160,144},{176,1... | collective-permute-start | bytes 1769480 | tf_op jit(solution)/shard_map/ppermute | solution.py:310
  90.9 0.8 fusion.refs_1_
  91.7 15.7 %stem_and_taps.1 = (bf16[1056,768]{1,0:T(8,128)(2,1)}, bf16[1056,1536]{1,0:T(8,128)(2,1)}) custom-call(s32[19]{0:T(128)} %pad_add_fusion.refs_0_, bf16[1056,64]{1,0:T(8,128)(2,1)} %fusion.refs_1_, bf16[64,1536]{1,0:T(8,128)(2,1)} %maximum_select_fusion.refs_2_, f32[8,1536]{1,0:T(8,128)} %get-tuple-element.32.refs_3_.refs_2_), custom_call_target="tpu_custom_call" | custom-call | tf_op jit(solution)/shard_map/stem_and_taps/pallas_call | solution.py:203
  107.4 0.8 copy-done.7
  108.4 0.5 copy-done
  108.9 8.0 %mix_first.1 = (bf16[528,768]{1,0:T(8,128)(2,1)}, bf16[1536,768]{1,0:T(8,128)(2,1)}) custom-call(s32[19]{0:T(128)} %pad_add_fusion.refs_0_, bf16[1056,768]{1,0:T(8,128)(2,1)} %get-tuple-element.15.refs_1_, bf16[1056,1536]{1,0:T(8,128)(2,1)} %get-tuple-element.16.refs_2_, bf16[4,96,768]{2,1,0:T(8,128)(2,1)} %copy-done.2, bf16[4,96,768]{2,1,0:T(8,128)(2,1)} %copy-done.7, ...), custom_call_target="tpu_custom_call" | custom-call | tf_op jit(solution)/shard_map/mix_first/pallas_call | solution.py:214
  116.9 4.0 %collective-permute-start.8 = (bf16[528,768]{1,0:T(8,128)(2,1)}, bf16[528,768]{1,0:T(8,128)(2,1)S(1)}, u32[]{:S(2)}, u32[]{:S(2)}) collective-permute-start(bf16[528,768]{1,0:T(8,128)(2,1)} %get-tuple-element.17.refs_1_), channel_id=1, source_target_pairs={{0,64},{64,0},{1,65},{65,1},{2,66},{66,2},{3,67},{67,3},{4,68},{68... | collective-permute-start | bytes 2433032 | tf_op jit(solution)/shard_map/ppermute | solution.py:333
  120.9 3.2 %collective-permute-start.10 = (bf16[4,96,768]{2,1,0:T(8,128)(2,1)S(1)}, bf16[4,96,768]{2,1,0:T(8,128)(2,1)S(1)}, u32[]{:S(2)}, u32[]{:S(2)}) collective-permute-start(bf16[4,96,768]{2,1,0:T(8,128)(2,1)S(1)} %get-tuple-element.21.refs_4_), channel_id=1, source_target_pairs={{0,432},{16,0},{32,16},{48,32},{128,48},{144,128},{160,144},{176,1... | collective-permute-start | bytes 1769480 | tf_op jit(solution)/shard_map/ppermute | solution.py:310
  124.1 2.1 collective-permute-start.9
  126.2 11.5 %collective-permute-done.10.refs_6_ = bf16[4,96,768]{2,1,0:T(8,128)(2,1)S(1)} collective-permute-done((bf16[4,96,768]{2,1,0:T(8,128)(2,1)S(1)}, bf16[4,96,768]{2,1,0:T(8,128)(2,1)S(1)}, u32[]{:S(2)}, u32[]{:S(2)}) %collective-permute-start.10) | collective-permute-done | bytes 589856 | tf_op jit(solution)/shard_map/ppermute | solution.py:310
  137.7 4.1 %collective-permute-done.9.refs_5_ = bf16[4,96,768]{2,1,0:T(8,128)(2,1)S(1)} collective-permute-done((bf16[4,96,768]{2,1,0:T(8,128)(2,1)S(1)}, bf16[4,96,768]{2,1,0:T(8,128)(2,1)S(1)}, u32[]{:S(2)}, u32[]{:S(2)}) %collective-permute-start.9) | collective-permute-done | bytes 589856 | tf_op jit(solution)/shard_map/ppermute | solution.py:310
  141.8 0.8 copy-done.6
  142.9 9.6 %shard_map.64 = (bf16[256,768]{1,0:T(8,128)(2,1)}, bf16[1536,768]{1,0:T(8,128)(2,1)}) custom-call(s32[19]{0:T(128)} %pad_add_fusion.refs_0_, bf16[528,768]{1,0:T(8,128)(2,1)} %get-tuple-element.17.refs_1_, bf16[528,768]{1,0:T(8,128)(2,1)} %copy-done.4, f32[8,1536]{1,0:T(8,128)} %get-tuple-element.31.refs_3_.refs_2_, bf16[4,96,768]{2,1,0:T(8,128)(2,1)} %copy-done.1, ...), custom_call_target="tpu_custom_call" | custom-call | tf_op jit(solution)/shard_map/pallas_call | solution.py:225
  152.6 2.1 collective-permute-start.12
  154.7 0.8 fusion.5
  155.5 3.6 %collective-permute-start.11 = (bf16[12,768]{1,0:T(8,128)(2,1)S(1)}, bf16[12,768]{1,0:T(8,128)(2,1)S(1)}, u32[]{:S(2)}, u32[]{:S(2)}) collective-permute-start(bf16[12,768]{1,0:T(8,128)(2,1)S(1)} %get-tuple-element.25), channel_id=1, source_target_pairs={{0,129},{128,5},{4,133},{132,9},{8,137},{136,13},{12,141},{140,17}... | collective-permute-start | bytes 55304 | tf_op jit(solution)/shard_map/ppermute | solution.py:282
  159.2 0.7 collective-permute-start.13
  160.1 2.2 collective-permute-done.12
  162.4 4.3 %all-gather.1 = bf16[576,768]{1,0:T(8,128)(2,1)} all-gather(bf16[288,768]{1,0:T(8,128)(2,1)S(1)} %pad_maximum_fusion), channel_id=3, replica_groups=mesh['zh'=4,'co'=2,'zl'=4,'y'=4,'x'=4] {'co'}, dimensions={0}, use_global_device_ids=true | all-gather | bytes 1327104 | tf_op jit(solution)/shard_map/all_gather | solution.py:339
  166.7 6.8 %shard_map.65 = bf16[144,768]{1,0:T(8,128)(2,1)} custom-call(s32[19]{0:T(128)} %pad_add_fusion.refs_0_, bf16[2,288,768]{2,1,0:T(8,128)(2,1)} %bitcast.39, f32[8,1536]{1,0:T(8,128)} %get-tuple-element.32.refs_3_.refs_2_, bf16[1536,768]{1,0:T(8,128)(2,1)} %get-tuple-element.19.refs_3_), custom_call_target="tpu_custom_call" | custom-call | tf_op jit(solution)/shard_map/pallas_call | solution.py:235
  173.5 4.0 %all-gather.2 = bf16[288,768]{1,0:T(8,128)(2,1)} all-gather(bf16[144,768]{1,0:T(8,128)(2,1)} %shard_map.65), channel_id=4, replica_groups=mesh['zh'=4,'co'=2,'zl'=4,'y'=4,'x'=4] {'co'}, dimensions={0}, use_global_device_ids=true | all-gather | bytes 663552 | tf_op jit(solution)/shard_map/all_gather | solution.py:341
  177.4 4.5 %shard_map.66 = bf16[64,768]{1,0:T(8,128)(2,1)} custom-call(s32[19]{0:T(128)} %pad_add_fusion.refs_0_, bf16[2,144,768]{2,1,0:T(8,128)(2,1)} %bitcast.40, f32[8,1536]{1,0:T(8,128)} %get-tuple-element.31.refs_3_.refs_2_, bf16[1536,768]{1,0:T(8,128)(2,1)} %get-tuple-element.20.refs_3_), custom_call_target="tpu_custom_call" | custom-call | tf_op jit(solution)/shard_map/pallas_call | solution.py:235
  181.9 0.7 collective-permute-start.15
  182.6 0.8 fusion.6
  183.4 0.7 collective-permute-start.14
  184.0 0.8 collective-permute-start.16
  185.0 2.1 all-gather.3
  187.1 3.9 %shard_map.67 = bf16[48,768]{1,0:T(8,128)(2,1)} custom-call(s32[19]{0:T(128)} %pad_add_fusion.refs_0_, bf16[2,96,768]{2,1,0:T(8,128)(2,1)} %bitcast.43, f32[8,1536]{1,0:T(8,128)} %get-tuple-element.32.refs_3_.refs_2_, bf16[1536,768]{1,0:T(8,128)(2,1)} %get-tuple-element.19.refs_3_), custom_call_target="tpu_custom_call" | custom-call | tf_op jit(solution)/shard_map/pallas_call | solution.py:235
  191.1 3.4 %all-gather.4 = bf16[96,768]{1,0:T(8,128)(2,1)} all-gather(bf16[48,768]{1,0:T(8,128)(2,1)} %shard_map.67), channel_id=6, replica_groups=mesh['zh'=4,'co'=2,'zl'=4,'y'=4,'x'=4] {'co'}, dimensions={0}, use_global_device_ids=true | all-gather | bytes 221184 | tf_op jit(solution)/shard_map/all_gather | solution.py:341
  194.5 3.4 %shard_map.68 = bf16[16,768]{1,0:T(8,128)(2,1)} custom-call(s32[19]{0:T(128)} %pad_add_fusion.refs_0_, bf16[2,48,768]{2,1,0:T(8,128)(2,1)} %bitcast.46, f32[8,1536]{1,0:T(8,128)} %get-tuple-element.31.refs_3_.refs_2_, bf16[1536,768]{1,0:T(8,128)(2,1)} %get-tuple-element.20.refs_3_), custom_call_target="tpu_custom_call" | custom-call | tf_op jit(solution)/shard_map/pallas_call | solution.py:235
  197.9 0.7 collective-permute-start.18
  198.5 0.8 fusion.8
  199.3 0.7 collective-permute-start.17
  200.0 0.7 collective-permute-start.19
  200.7 2.0 all-gather.5
  202.8 3.4 %shard_map.69 = bf16[16,768]{1,0:T(8,128)(2,1)} custom-call(s32[19]{0:T(128)} %pad_add_fusion.refs_0_, bf16[2,48,768]{2,1,0:T(8,128)(2,1)} %bitcast.45, f32[8,1536]{1,0:T(8,128)} %get-tuple-element.32.refs_3_.refs_2_, bf16[1536,768]{1,0:T(8,128)(2,1)} %get-tuple-element.19.refs_3_), custom_call_target="tpu_custom_call" | custom-call | tf_op jit(solution)/shard_map/pallas_call | solution.py:235
  206.2 3.4 %all-gather.6 = bf16[32,768]{1,0:T(8,128)(2,1)} all-gather(bf16[16,768]{1,0:T(8,128)(2,1)} %shard_map.69), channel_id=8, replica_groups=mesh['zh'=4,'co'=2,'zl'=4,'y'=4,'x'=4] {'co'}, dimensions={0}, use_global_device_ids=true | all-gather | bytes 73728 | tf_op jit(solution)/shard_map/all_gather | solution.py:341
  209.5 2.9 %shard_map.70 = bf16[4,768]{1,0:T(4,128)(2,1)} custom-call(s32[19]{0:T(128)} %pad_add_fusion.refs_0_, bf16[2,16,768]{2,1,0:T(8,128)(2,1)} %bitcast.47, f32[8,1536]{1,0:T(8,128)} %get-tuple-element.31.refs_3_.refs_2_, bf16[1536,768]{1,0:T(8,128)(2,1)} %get-tuple-element.20.refs_3_), custom_call_target="tpu_custom_call" | custom-call | tf_op jit(solution)/shard_map/pallas_call | solution.py:235
  212.4 0.8 reshape.54
  213.2 0.6 broadcast_in_dim.11
  213.9 28.2 %all-to-all-start.2 = ((bf16[32,2,192]{2,1,0:T(2,128)(2,1)}), bf16[32,2,192]{2,1,0:T(2,128)(2,1)S(1)}, u32[]{:S(2)}, u32[]{:S(2)}) async-start(bf16[32,2,192]{2,1,0:T(2,128)(2,1)} %bitcast.26), calls=%async_computation.2 | async-start | bytes 65536 | tf_op jit(solution)/shard_map/all_to_all | solution.py:349
  242.1 14.4 %all-to-all-done.2 = bf16[32,2,192]{2,1,0:T(2,128)(2,1)S(1)} async-done(((bf16[32,2,192]{2,1,0:T(2,128)(2,1)}), bf16[32,2,192]{2,1,0:T(2,128)(2,1)S(1)}, u32[]{:S(2)}, u32[]{:S(2)}) %all-to-all-start.2) | async-done | bytes 24608 | tf_op jit(solution)/shard_map/all_to_all | solution.py:349
  256.5 0.6 dynamic-slice_bitcast_fusion.2
  (87 shorter events, 2.2 us)
Async XLA Ops:
  29.6 22.6 %collective-permute-start = (s32[512]{0:T(512)S(1)}, s32[512]{0:T(512)S(1)}, u32[]{:S(2)}, u32[]{:S(2)}) collective-permute-start(s32[512]{0:T(512)S(1)} %bitcast.54), channel_id=1, source_target_pairs={{3,4},{7,8},{11,12},{15,16},{19,20},{23,24},{27,28},{31,32},{35,36... | collective-permute-start | bytes 6152 | tf_op jit(solution)/shard_map/ppermute | solution.py:273
  30.2 22.0 %collective-permute-start.1 = (s32[512]{0:T(512)S(1)}, s32[512]{0:T(512)S(1)}, u32[]{:S(2)}, u32[]{:S(2)}) collective-permute-start(s32[512]{0:T(512)S(1)} %bitcast.55), channel_id=1, source_target_pairs={{0,0},{4,4},{8,8},{12,12},{16,16},{20,20},{24,24},{28,28},{32,32},... | collective-permute-start | bytes 6152 | tf_op jit(solution)/shard_map/ppermute | solution.py:273
  30.9 21.4 %collective-permute-start.2 = (s32[512]{0:T(512)S(1)}, s32[512]{0:T(512)S(1)}, u32[]{:S(2)}, u32[]{:S(2)}) collective-permute-start(s32[512]{0:T(512)S(1)} %bitcast.56), channel_id=1, source_target_pairs={{1,0},{5,4},{9,8},{13,12},{17,16},{21,20},{25,24},{29,28},{33,32},... | collective-permute-start | bytes 6152 | tf_op jit(solution)/shard_map/ppermute | solution.py:273
  32.2 20.1 %collective-permute-start.3 = (s32[512]{0:T(512)S(1)}, s32[512]{0:T(512)S(1)}, u32[]{:S(2)}, u32[]{:S(2)}) collective-permute-start(s32[512]{0:T(512)S(1)} %bitcast.57), channel_id=1, source_target_pairs={{2,0},{6,4},{10,8},{14,12},{18,16},{22,20},{26,24},{30,28},{34,32}... | collective-permute-start | bytes 6152 | tf_op jit(solution)/shard_map/ppermute | solution.py:273
  34.8 13.2 %copy-start.10 = (s32[4]{0:T(128)S(1)}, s32[4]{0:T(128)}, u32[]{:S(2)}) copy-start(s32[4]{0:T(128)} %constant.155) | copy-start | bytes 52
  34.8 15.2 %copy-start.9 = (bf16[15,4,1536]{2,1,0:T(4,128)(2,1)S(1)}, bf16[15,4,1536]{2,1,0:T(4,128)(2,1)}, u32[]{:S(2)}) copy-start(bf16[15,4,1536]{2,1,0:T(4,128)(2,1)} %param.7) | copy-start | bytes 552964
  34.8 31.1 %all-to-all-start = ((bf16[32,24,768]{2,1,0:T(8,128)(2,1)}), bf16[32,24,768]{2,1,0:T(8,128)(2,1)S(1)}, u32[]{:S(2)}, u32[]{:S(2)}) async-start(bf16[32,24,768]{2,1,0:T(8,128)(2,1)} %bitcast.10), calls=%async_computation | async-start | bytes 2359296 | tf_op jit(solution)/shard_map/all_to_all | solution.py:301
  65.9 9.0 %collective-permute-start.6 = (bf16[96,768]{1,0:T(8,128)(2,1)S(1)}, bf16[96,768]{1,0:T(8,128)(2,1)S(1)}, u32[]{:S(2)}, u32[]{:S(2)}) collective-permute-start(bf16[96,768]{1,0:T(8,128)(2,1)S(1)} %get-tuple-element.23), channel_id=1, source_target_pairs={{0,32},{16,48},{32,128},{48,144},{128,160},{144,176},{160,256},{17... | collective-permute-start | bytes 442376 | tf_op jit(solution)/shard_map/ppermute | solution.py:304
  68.6 10.5 %collective-permute-start.7 = (bf16[96,768]{1,0:T(8,128)(2,1)S(1)}, bf16[96,768]{1,0:T(8,128)(2,1)S(1)}, u32[]{:S(2)}, u32[]{:S(2)}) collective-permute-start(bf16[96,768]{1,0:T(8,128)(2,1)S(1)} %get-tuple-element.24), channel_id=1, source_target_pairs={{0,416},{16,432},{32,0},{48,16},{128,32},{144,48},{160,128},{176,1... | collective-permute-start | bytes 442376 | tf_op jit(solution)/shard_map/ppermute | solution.py:305
  80.3 27.1 %all-to-all-start.1 = ((bf16[4,2,96,768]{3,2,1,0:T(8,128)(2,1)}), bf16[4,2,96,768]{3,2,1,0:T(8,128)(2,1)S(1)}, u32[]{:S(2)}, u32[]{:S(2)}) async-start(bf16[4,2,96,768]{3,2,1,0:T(8,128)(2,1)} %broadcast_in_dim.10), calls=%async_computation.1 | async-start | bytes 2359296 | tf_op jit(solution)/shard_map/all_to_all | solution.py:250
  84.0 6.7 %copy-start.3 = (s32[60,1056]{0,1:T(8,128)S(1)}, s32[60,1056]{0,1:T(8,128)}, u32[]{:S(2)}) copy-start(s32[60,1056]{0,1:T(8,128)} %copy.15) | copy-start | bytes 760324
  84.1 23.3 %copy-start.2 = (bf16[4,96,768]{2,1,0:T(8,128)(2,1)}, bf16[4,96,768]{2,1,0:T(8,128)(2,1)S(1)}, u32[]{:S(2)}) copy-start(bf16[4,96,768]{2,1,0:T(8,128)(2,1)S(1)} %get-tuple-element.22.refs_3_) | copy-start | bytes 1769476
  84.1 40.0 %copy-start.1 = (bf16[4,96,768]{2,1,0:T(8,128)(2,1)}, bf16[4,96,768]{2,1,0:T(8,128)(2,1)S(1)}, u32[]{:S(2)}) copy-start(bf16[4,96,768]{2,1,0:T(8,128)(2,1)S(1)} %get-tuple-element.21.refs_4_) | copy-start | bytes 1769476
  84.1 23.2 %collective-permute-start.4 = (bf16[4,96,768]{2,1,0:T(8,128)(2,1)S(1)}, bf16[4,96,768]{2,1,0:T(8,128)(2,1)S(1)}, u32[]{:S(2)}, u32[]{:S(2)}) collective-permute-start(bf16[4,96,768]{2,1,0:T(8,128)(2,1)S(1)} %get-tuple-element.22.refs_3_), channel_id=1, source_target_pairs={{0,16},{16,32},{32,48},{48,128},{128,144},{144,160},{160,176},{176... | collective-permute-start | bytes 1769480 | tf_op jit(solution)/shard_map/ppermute | solution.py:310
  86.2 21.2 %collective-permute-start.5 = (bf16[4,96,768]{2,1,0:T(8,128)(2,1)S(1)}, bf16[4,96,768]{2,1,0:T(8,128)(2,1)S(1)}, u32[]{:S(2)}, u32[]{:S(2)}) collective-permute-start(bf16[4,96,768]{2,1,0:T(8,128)(2,1)S(1)} %get-tuple-element.22.refs_3_), channel_id=1, source_target_pairs={{0,432},{16,0},{32,16},{48,32},{128,48},{144,128},{160,144},{176,1... | collective-permute-start | bytes 1769480 | tf_op jit(solution)/shard_map/ppermute | solution.py:310
  107.4 0.8 copy-start.7
  107.4 1.0 copy-start.8
  107.4 1.5 copy-start
  116.9 24.9 %collective-permute-start.8 = (bf16[528,768]{1,0:T(8,128)(2,1)}, bf16[528,768]{1,0:T(8,128)(2,1)S(1)}, u32[]{:S(2)}, u32[]{:S(2)}) collective-permute-start(bf16[528,768]{1,0:T(8,128)(2,1)} %get-tuple-element.17.refs_1_), channel_id=1, source_target_pairs={{0,64},{64,0},{1,65},{65,1},{2,66},{66,2},{3,67},{67,3},{4,68},{68... | collective-permute-start | bytes 2433032 | tf_op jit(solution)/shard_map/ppermute | solution.py:333
  120.9 16.8 %collective-permute-start.10 = (bf16[4,96,768]{2,1,0:T(8,128)(2,1)S(1)}, bf16[4,96,768]{2,1,0:T(8,128)(2,1)S(1)}, u32[]{:S(2)}, u32[]{:S(2)}) collective-permute-start(bf16[4,96,768]{2,1,0:T(8,128)(2,1)S(1)} %get-tuple-element.21.refs_4_), channel_id=1, source_target_pairs={{0,432},{16,0},{32,16},{48,32},{128,48},{144,128},{160,144},{176,1... | collective-permute-start | bytes 1769480 | tf_op jit(solution)/shard_map/ppermute | solution.py:310
  124.1 17.7 %collective-permute-start.9 = (bf16[4,96,768]{2,1,0:T(8,128)(2,1)S(1)}, bf16[4,96,768]{2,1,0:T(8,128)(2,1)S(1)}, u32[]{:S(2)}, u32[]{:S(2)}) collective-permute-start(bf16[4,96,768]{2,1,0:T(8,128)(2,1)S(1)} %get-tuple-element.21.refs_4_), channel_id=1, source_target_pairs={{0,16},{16,32},{32,48},{48,128},{128,144},{144,160},{160,176},{176... | collective-permute-start | bytes 1769480 | tf_op jit(solution)/shard_map/ppermute | solution.py:310
  137.7 4.2 %copy-start.5 = (bf16[4,96,768]{2,1,0:T(8,128)(2,1)}, bf16[4,96,768]{2,1,0:T(8,128)(2,1)S(1)}, u32[]{:S(2)}) copy-start(bf16[4,96,768]{2,1,0:T(8,128)(2,1)S(1)} %collective-permute-done.10.refs_6_) | copy-start | bytes 1769476
  141.8 0.8 copy-start.6
  141.8 1.1 copy-start.4
  152.6 9.7 %collective-permute-start.12 = (bf16[256,768]{1,0:T(8,128)(2,1)}, bf16[256,768]{1,0:T(8,128)(2,1)S(1)}, u32[]{:S(2)}, u32[]{:S(2)}) collective-permute-start(bf16[256,768]{1,0:T(8,128)(2,1)} %get-tuple-element.18), channel_id=1, source_target_pairs={{0,1},{4,5},{8,9},{12,13},{16,17},{20,21},{24,25},{28,29},{32,33},... | collective-permute-start | bytes 1179656 | tf_op jit(solution)/shard_map/ppermute | solution.py:284
  155.5 4.6 %collective-permute-start.11 = (bf16[12,768]{1,0:T(8,128)(2,1)S(1)}, bf16[12,768]{1,0:T(8,128)(2,1)S(1)}, u32[]{:S(2)}, u32[]{:S(2)}) collective-permute-start(bf16[12,768]{1,0:T(8,128)(2,1)S(1)} %get-tuple-element.25), channel_id=1, source_target_pairs={{0,129},{128,5},{4,133},{132,9},{8,137},{136,13},{12,141},{140,17}... | collective-permute-start | bytes 55304 | tf_op jit(solution)/shard_map/ppermute | solution.py:282
  159.2 0.9 collective-permute-start.13
  181.9 3.0 %collective-permute-start.15 = (bf16[64,768]{1,0:T(8,128)(2,1)}, bf16[64,768]{1,0:T(8,128)(2,1)S(1)}, u32[]{:S(2)}, u32[]{:S(2)}) collective-permute-start(bf16[64,768]{1,0:T(8,128)(2,1)} %shard_map.66), channel_id=1, source_target_pairs={{1,2},{5,6},{9,10},{13,14},{17,18},{21,22},{25,26},{29,30},{33,34}... | collective-permute-start | bytes 294920 | tf_op jit(solution)/shard_map/ppermute | solution.py:284
  183.4 1.5 collective-permute-start.14
  184.0 0.9 collective-permute-start.16
  197.9 2.8 %collective-permute-start.18 = (bf16[16,768]{1,0:T(8,128)(2,1)}, bf16[16,768]{1,0:T(8,128)(2,1)S(1)}, u32[]{:S(2)}, u32[]{:S(2)}) collective-permute-start(bf16[16,768]{1,0:T(8,128)(2,1)} %shard_map.68), channel_id=1, source_target_pairs={{2,3},{6,7},{10,11},{14,15},{18,19},{22,23},{26,27},{30,31},{34,35... | collective-permute-start | bytes 73736 | tf_op jit(solution)/shard_map/ppermute | solution.py:284
  199.3 1.3 collective-permute-start.17
  200.0 0.7 collective-permute-start.19
  213.9 42.6 %all-to-all-start.2 = ((bf16[32,2,192]{2,1,0:T(2,128)(2,1)}), bf16[32,2,192]{2,1,0:T(2,128)(2,1)S(1)}, u32[]{:S(2)}, u32[]{:S(2)}) async-start(bf16[32,2,192]{2,1,0:T(2,128)(2,1)} %bitcast.26), calls=%async_computation.2 | async-start | bytes 65536 | tf_op jit(solution)/shard_map/all_to_all | solution.py:349

commit v4 on v3

--- a/solution.py
+++ b/solution.py
@@ -260,7 +260,12 @@
     return ((zh * 4 + zl) * 4 + y) * 4 + role
 
 
-def gathered_bases(bases, sequence, before, count):
+def by_role(array):
+    pairs = [(r * 4 + zh, zh * 4 + r) for zh in range(4) for r in range(4)]
+    return lax.ppermute(array, ("zh", "x"), pairs)
+
+
+def gathered_bases(bases, sequence):
     mine = lax.dynamic_index_in_dim(bases + 1, sequence, 0, keepdims=False)
     parts = []
     for by in (-1, 0, 1, 2):
@@ -271,7 +276,7 @@
                 if 0 <= place < 64:
                     pairs.append((zh * 64 + place, zh * 64 + row * 4))
         parts.append(lax.ppermute(mine, ("zh", "zl", "y", "x"), pairs))
-    return jnp.concatenate(parts)[mine.shape[0] - before :][:count]
+    return parts
 
 
 def pass_on(array, role):
@@ -292,10 +297,14 @@
     group = (zl * 4 + y) * 2 + zh % 2
     sequence = zh // 2
 
-    held = [point_weight[0], gains, depth_taps[0], jnp.zeros((2, C), gains.dtype)]
-    held = lax.all_gather(jnp.concatenate(held, axis=0), "zh")
-    held, bases = lax.optimization_barrier((held, bases))
-    blocks = held[:, :24].reshape(4, 24, 2, HALF).transpose(2, 0, 1, 3)
+    rows = RUN + 2 * EDGE
+    size = up16(rows)
+    ids = gathered_bases(bases, sequence)
+    params = jnp.concatenate([gains, depth_taps[0], jnp.zeros((2, C), gains.dtype)], axis=0)
+    params = by_role(params)
+
+    held = lax.all_gather(point_weight[0], "zh")
+    blocks = held.reshape(4, 24, 2, HALF).transpose(2, 0, 1, 3)
     blocks = jnp.broadcast_to(blocks[:, None], (2, 4, 4, 24, HALF)).reshape(32, 24, HALF)
     blocks = lax.optimization_barrier(blocks)
     blocks = lax.all_to_all(blocks, ("co", "y", "x"), 0, 0, tiled=True)
@@ -311,7 +320,6 @@
         beside.append(sides)
     opposite = around_y(jnp.stack([share0, share1]))
     pieces = [sides + [opposite] for sides in beside]
-    params = lax.dynamic_index_in_dim(held, x, 0, keepdims=False)[24:]
     params = lax.all_gather(params, "co")
     params = own_first(params, co).astype(jnp.float32)
     four = jnp.arange(4, dtype=jnp.int32)
@@ -320,9 +328,7 @@
     flags = jnp.stack([co, (group == 0).astype(jnp.int32), (group == 31).astype(jnp.int32)])
     meta = jnp.concatenate([flags.astype(jnp.int32), (place + 8 * co) % 16])
 
-    rows = RUN + 2 * EDGE
-    size = up16(rows)
-    ids = gathered_bases(bases, sequence, EDGE + margin, size + 2 * margin)
+    ids = jnp.concatenate(ids)[bases.shape[1] - EDGE - margin :][: size + 2 * margin]
     windows = jnp.stack([ids[k : k + size] for k in range(2 * margin + 1)])
     kinds = jnp.arange(1, 5, dtype=jnp.int32)[None, :, None]
     hot = (windows[:, None, :] == kinds).astype(jnp.bfloat16).reshape(-1, size)

time: 259 us -> 259 us (level)
  waiting for transfers between devices: 50.3 us -> 40 us
  starting transfers between devices: 82.9 us -> 90.8 us
    all_to_all x1, starting transfers between devices: 13.2 us -> 18 us  [relay(): blocks = lax.all_to_all(blocks, ('co', 'y', 'x'), 0, 0, tiled=True)]
    ppermute x1, waiting for transfers between devices: 4.19 us -> 0.01 us  [relay(): share1 = lax.ppermute(share[1], ('zh', 'zl'), ring(16, -2))]
    ppermute x4, waiting for transfers between devices: 15.6 us -> 12.4 us  [relay(): sides.append(lax.ppermute(near[slot], ('zh', 'zl'), ring(16, by)))]
  transfers between devices with their start and end apart: 23 -> 24, of which waited for: 7 -> 6; matrix products, arithmetic and copies ran while one was open for 3% -> 4% of each run, Pallas kernels for 6% -> 6%
where the time goes in v4:
time: 259 us; the launch traced here: 258 us
  starting transfers between devices  90.8 us (35%)
  Pallas kernels  58.3 us (23%)
  blocking collectives  50.6 us (20%)
  waiting for transfers between devices  40 us (15%)
  local copies, waits for them, and re-layouts  12.3 us (5%)
  other arithmetic  4.85 us (2%)
    all_gather x1, blocking collectives, relay(): held = lax.all_gather(point_weight[0], 'zh')  29.7 us
    all_to_all x1, starting transfers between devices, relay(): got = lax.all_to_all(blocks, ('zh', 'co', 'x'), 0, 0, tiled=True)  28.9 us
    pallas_call x6, Pallas kernels, run_level(): pl.pallas_call(lambda *refs: paired_level(rows, edge, *refs), in_specs=[s...  24.9 us
    all_to_all x1, starting transfers between devices, relay(): blocks = lax.all_to_all(blocks, ('co', 'y', 'x'), 0, 0, tiled=True)  18 us
    pallas_call x1, Pallas kernels, run_first_half(): pl.pallas_call(lambda *refs: first_half(rows, *refs), in_specs=[spec(pltp...  15.7 us
    all_to_all x1, waiting for transfers between devices, relay(): got = lax.all_to_all(blocks, ('zh', 'co', 'x'), 0, 0, tiled=True)  14.4 us
    ppermute x4, starting transfers between devices, relay(): sides.append(lax.ppermute(near[slot], ('zh', 'zl'), ring(16, by)))  13 us
    ppermute x4, waiting for transfers between devices, relay(): sides.append(lax.ppermute(near[slot], ('zh', 'zl'), ring(16, by)))  12.4 us
  transfers between devices with their start and end apart: 24, of which 6 were waited for; matrix products, arithmetic and copies ran while one was open for 4% of the time, Pallas kernels for 6%

profile of v4, /device:TPU:1, one launch (start us, length us, event | category | flops | bytes accessed | tf_op | source)
XLA Modules:
  0.0 257.5 jit_solution(1554894105883502659)
XLA Ops:
  0.0 0.7 dynamic-slice_add_fusion
  0.7 0.6 collective-permute-start
  1.4 0.7 collective-permute-start.1
  2.0 1.3 collective-permute-start.2
  3.3 1.3 collective-permute-start.3
  4.7 0.8 maximum_maximum_fusion
  5.5 0.7 collective-permute-start.4
  6.2 29.7 %all_gather.47 = bf16[4,24,1536]{2,1,0:T(8,128)(2,1)S(1)} all-gather(bf16[1,24,1536]{2,1,0:T(8,128)(2,1)} %param.10), channel_id=1, replica_groups=mesh['zh'=4,'co'=2,'zl'=4,'y'=4,'x'=4] {'zh'}, dimensions={0}, use_global_device_ids=true | all-gather | bytes 368640 | tf_op jit(solution)/shard_map/all_gather | solution.py:306
  35.9 1.1 broadcast_in_dim.9
  37.1 18.0 %all-to-all-start = ((bf16[32,24,768]{2,1,0:T(8,128)(2,1)}), bf16[32,24,768]{2,1,0:T(8,128)(2,1)S(1)}, u32[]{:S(2)}, u32[]{:S(2)}) async-start(bf16[32,24,768]{2,1,0:T(8,128)(2,1)} %bitcast.9), calls=%async_computation | async-start | bytes 2359296 | tf_op jit(solution)/shard_map/all_to_all | solution.py:310
  55.5 0.7 maximum_select_fusion.refs_2_
  57.9 0.8 fusion.refs_1_
  58.7 1.8 all-gather
  60.5 0.6 copy-done.8
  61.1 0.6 fusion.7
  61.7 11.3 %all-to-all-done = bf16[32,24,768]{2,1,0:T(8,128)(2,1)S(1)} async-done(((bf16[32,24,768]{2,1,0:T(8,128)(2,1)}), bf16[32,24,768]{2,1,0:T(8,128)(2,1)S(1)}, u32[]{:S(2)}, u32[]{:S(2)}) %all-to-all-start) | async-done | bytes 1179680 | tf_op jit(solution)/shard_map/all_to_all | solution.py:310
  73.1 1.9 collective-permute-start.7
  75.0 5.5 %collective-permute-start.8 = (bf16[96,768]{1,0:T(8,128)(2,1)S(1)}, bf16[96,768]{1,0:T(8,128)(2,1)S(1)}, u32[]{:S(2)}, u32[]{:S(2)}) collective-permute-start(bf16[96,768]{1,0:T(8,128)(2,1)S(1)} %get-tuple-element.20), channel_id=1, source_target_pairs={{0,416},{16,432},{32,0},{48,16},{128,32},{144,48},{160,128},{176,1... | collective-permute-start | bytes 442376 | tf_op jit(solution)/shard_map/ppermute | solution.py:314
  80.6 1.9 collective-permute-start.5
  82.5 4.6 %collective-permute-start.6 = (bf16[4,96,768]{2,1,0:T(8,128)(2,1)S(1)}, bf16[4,96,768]{2,1,0:T(8,128)(2,1)S(1)}, u32[]{:S(2)}, u32[]{:S(2)}) collective-permute-start(bf16[4,96,768]{2,1,0:T(8,128)(2,1)S(1)} %get-tuple-element.18.refs_3_), channel_id=1, source_target_pairs={{0,432},{16,0},{32,16},{48,32},{128,48},{144,128},{160,144},{176,1... | collective-permute-start | bytes 1769480 | tf_op jit(solution)/shard_map/ppermute | solution.py:319
  87.1 1.1 broadcast_in_dim.10
  88.3 3.5 %all-to-all-start.1 = ((bf16[4,2,96,768]{3,2,1,0:T(8,128)(2,1)}), bf16[4,2,96,768]{3,2,1,0:T(8,128)(2,1)S(1)}, u32[]{:S(2)}, u32[]{:S(2)}) async-start(bf16[4,2,96,768]{3,2,1,0:T(8,128)(2,1)} %broadcast_in_dim.10), calls=%async_computation.1 | async-start | bytes 2359296 | tf_op jit(solution)/shard_map/all_to_all | solution.py:250
  91.8 0.9 fusion.1
  92.6 0.7 slice_bitcast_fusion.2
  93.3 15.7 %stem_and_taps.1 = (bf16[1056,768]{1,0:T(8,128)(2,1)}, bf16[1056,1536]{1,0:T(8,128)(2,1)}) custom-call(s32[19]{0:T(128)} %pad_add_fusion.refs_0_, bf16[1056,64]{1,0:T(8,128)(2,1)} %fusion.refs_1_, bf16[64,1536]{1,0:T(8,128)(2,1)} %maximum_select_fusion.refs_2_, f32[8,1536]{1,0:T(8,128)} %get-tuple-element.28.refs_3_.refs_2_), custom_call_target="tpu_custom_call" | custom-call | tf_op jit(solution)/shard_map/stem_and_taps/pallas_call | solution.py:203
  109.0 0.8 copy-done.6
  110.5 8.0 %mix_first.1 = (bf16[528,768]{1,0:T(8,128)(2,1)}, bf16[1536,768]{1,0:T(8,128)(2,1)}) custom-call(s32[19]{0:T(128)} %pad_add_fusion.refs_0_, bf16[1056,768]{1,0:T(8,128)(2,1)} %get-tuple-element.11.refs_1_, bf16[1056,1536]{1,0:T(8,128)(2,1)} %get-tuple-element.12.refs_2_, bf16[4,96,768]{2,1,0:T(8,128)(2,1)} %copy-done.2, bf16[4,96,768]{2,1,0:T(8,128)(2,1)} %copy-done.6, ...), custom_call_target="tpu_custom_call" | custom-call | tf_op jit(solution)/shard_map/mix_first/pallas_call | solution.py:214
  118.6 4.5 %collective-permute-start.9 = (bf16[528,768]{1,0:T(8,128)(2,1)}, bf16[528,768]{1,0:T(8,128)(2,1)S(1)}, u32[]{:S(2)}, u32[]{:S(2)}) collective-permute-start(bf16[528,768]{1,0:T(8,128)(2,1)} %get-tuple-element.13.refs_1_), channel_id=1, source_target_pairs={{0,64},{64,0},{1,65},{65,1},{2,66},{66,2},{3,67},{67,3},{4,68},{68... | collective-permute-start | bytes 2433032 | tf_op jit(solution)/shard_map/ppermute | solution.py:339
  123.1 1.9 collective-permute-start.10
  125.0 4.6 %collective-permute-start.11 = (bf16[4,96,768]{2,1,0:T(8,128)(2,1)S(1)}, bf16[4,96,768]{2,1,0:T(8,128)(2,1)S(1)}, u32[]{:S(2)}, u32[]{:S(2)}) collective-permute-start(bf16[4,96,768]{2,1,0:T(8,128)(2,1)S(1)} %get-tuple-element.17.refs_4_), channel_id=1, source_target_pairs={{0,432},{16,0},{32,16},{48,32},{128,48},{144,128},{160,144},{176,1... | collective-permute-start | bytes 1769480 | tf_op jit(solution)/shard_map/ppermute | solution.py:319
  129.6 11.5 %collective-permute-done.10.refs_5_ = bf16[4,96,768]{2,1,0:T(8,128)(2,1)S(1)} collective-permute-done((bf16[4,96,768]{2,1,0:T(8,128)(2,1)S(1)}, bf16[4,96,768]{2,1,0:T(8,128)(2,1)S(1)}, u32[]{:S(2)}, u32[]{:S(2)}) %collective-permute-start.10) | collective-permute-done | bytes 589856 | tf_op jit(solution)/shard_map/ppermute | solution.py:319
  141.1 0.9 collective-permute-done.11.refs_6_
  142.0 0.8 copy-done.5
  143.1 9.6 %shard_map.64 = (bf16[256,768]{1,0:T(8,128)(2,1)}, bf16[1536,768]{1,0:T(8,128)(2,1)}) custom-call(s32[19]{0:T(128)} %pad_add_fusion.refs_0_, bf16[528,768]{1,0:T(8,128)(2,1)} %get-tuple-element.13.refs_1_, bf16[528,768]{1,0:T(8,128)(2,1)} %copy-done.3, f32[8,1536]{1,0:T(8,128)} %get-tuple-element.27.refs_3_.refs_2_, bf16[4,96,768]{2,1,0:T(8,128)(2,1)} %copy-done.1, ...), custom_call_target="tpu_custom_call" | custom-call | tf_op jit(solution)/shard_map/pallas_call | solution.py:225
  152.7 1.5 collective-permute-start.13
  154.2 0.8 fusion.5
  155.0 4.6 %collective-permute-start.12 = (bf16[12,768]{1,0:T(8,128)(2,1)S(1)}, bf16[12,768]{1,0:T(8,128)(2,1)S(1)}, u32[]{:S(2)}, u32[]{:S(2)}) collective-permute-start(bf16[12,768]{1,0:T(8,128)(2,1)S(1)} %get-tuple-element.21), channel_id=1, source_target_pairs={{0,129},{128,5},{4,133},{132,9},{8,137},{136,13},{12,141},{140,17}... | collective-permute-start | bytes 55304 | tf_op jit(solution)/shard_map/ppermute | solution.py:287
  159.6 0.7 collective-permute-start.14
  160.5 1.6 collective-permute-done.13
  162.2 4.2 %all-gather.1 = bf16[576,768]{1,0:T(8,128)(2,1)} all-gather(bf16[288,768]{1,0:T(8,128)(2,1)S(1)} %pad_maximum_fusion), channel_id=3, replica_groups=mesh['zh'=4,'co'=2,'zl'=4,'y'=4,'x'=4] {'co'}, dimensions={0}, use_global_device_ids=true | all-gather | bytes 1327104 | tf_op jit(solution)/shard_map/all_gather | solution.py:345
  166.4 6.8 %shard_map.65 = bf16[144,768]{1,0:T(8,128)(2,1)} custom-call(s32[19]{0:T(128)} %pad_add_fusion.refs_0_, bf16[2,288,768]{2,1,0:T(8,128)(2,1)} %bitcast.39, f32[8,1536]{1,0:T(8,128)} %get-tuple-element.28.refs_3_.refs_2_, bf16[1536,768]{1,0:T(8,128)(2,1)} %get-tuple-element.15.refs_3_), custom_call_target="tpu_custom_call" | custom-call | tf_op jit(solution)/shard_map/pallas_call | solution.py:235
  173.2 4.0 %all-gather.2 = bf16[288,768]{1,0:T(8,128)(2,1)} all-gather(bf16[144,768]{1,0:T(8,128)(2,1)} %shard_map.65), channel_id=4, replica_groups=mesh['zh'=4,'co'=2,'zl'=4,'y'=4,'x'=4] {'co'}, dimensions={0}, use_global_device_ids=true | all-gather | bytes 663552 | tf_op jit(solution)/shard_map/all_gather | solution.py:347
  177.1 4.5 %shard_map.66 = bf16[64,768]{1,0:T(8,128)(2,1)} custom-call(s32[19]{0:T(128)} %pad_add_fusion.refs_0_, bf16[2,144,768]{2,1,0:T(8,128)(2,1)} %bitcast.40, f32[8,1536]{1,0:T(8,128)} %get-tuple-element.27.refs_3_.refs_2_, bf16[1536,768]{1,0:T(8,128)(2,1)} %get-tuple-element.16.refs_3_), custom_call_target="tpu_custom_call" | custom-call | tf_op jit(solution)/shard_map/pallas_call | solution.py:235
  181.6 0.7 collective-permute-start.16
  182.3 0.8 fusion.6
  183.1 0.7 collective-permute-start.15
  183.7 0.8 collective-permute-start.17
  184.7 2.1 all-gather.3
  186.8 3.9 %shard_map.67 = bf16[48,768]{1,0:T(8,128)(2,1)} custom-call(s32[19]{0:T(128)} %pad_add_fusion.refs_0_, bf16[2,96,768]{2,1,0:T(8,128)(2,1)} %bitcast.41, f32[8,1536]{1,0:T(8,128)} %get-tuple-element.28.refs_3_.refs_2_, bf16[1536,768]{1,0:T(8,128)(2,1)} %get-tuple-element.15.refs_3_), custom_call_target="tpu_custom_call" | custom-call | tf_op jit(solution)/shard_map/pallas_call | solution.py:235
  190.8 3.4 %all-gather.4 = bf16[96,768]{1,0:T(8,128)(2,1)} all-gather(bf16[48,768]{1,0:T(8,128)(2,1)} %shard_map.67), channel_id=6, replica_groups=mesh['zh'=4,'co'=2,'zl'=4,'y'=4,'x'=4] {'co'}, dimensions={0}, use_global_device_ids=true | all-gather | bytes 221184 | tf_op jit(solution)/shard_map/all_gather | solution.py:347
  194.2 3.4 %shard_map.68 = bf16[16,768]{1,0:T(8,128)(2,1)} custom-call(s32[19]{0:T(128)} %pad_add_fusion.refs_0_, bf16[2,48,768]{2,1,0:T(8,128)(2,1)} %bitcast.44, f32[8,1536]{1,0:T(8,128)} %get-tuple-element.27.refs_3_.refs_2_, bf16[1536,768]{1,0:T(8,128)(2,1)} %get-tuple-element.16.refs_3_), custom_call_target="tpu_custom_call" | custom-call | tf_op jit(solution)/shard_map/pallas_call | solution.py:235
  197.6 0.7 collective-permute-start.19
  198.2 0.8 fusion.8
  199.0 0.7 collective-permute-start.18
  199.7 0.7 collective-permute-start.20
  200.4 2.0 all-gather.5
  202.5 3.4 %shard_map.69 = bf16[16,768]{1,0:T(8,128)(2,1)} custom-call(s32[19]{0:T(128)} %pad_add_fusion.refs_0_, bf16[2,48,768]{2,1,0:T(8,128)(2,1)} %bitcast.43, f32[8,1536]{1,0:T(8,128)} %get-tuple-element.28.refs_3_.refs_2_, bf16[1536,768]{1,0:T(8,128)(2,1)} %get-tuple-element.15.refs_3_), custom_call_target="tpu_custom_call" | custom-call | tf_op jit(solution)/shard_map/pallas_call | solution.py:235
  205.9 3.4 %all-gather.6 = bf16[32,768]{1,0:T(8,128)(2,1)} all-gather(bf16[16,768]{1,0:T(8,128)(2,1)} %shard_map.69), channel_id=8, replica_groups=mesh['zh'=4,'co'=2,'zl'=4,'y'=4,'x'=4] {'co'}, dimensions={0}, use_global_device_ids=true | all-gather | bytes 73728 | tf_op jit(solution)/shard_map/all_gather | solution.py:347
  209.2 2.9 %shard_map.70 = bf16[4,768]{1,0:T(4,128)(2,1)} custom-call(s32[19]{0:T(128)} %pad_add_fusion.refs_0_, bf16[2,16,768]{2,1,0:T(8,128)(2,1)} %bitcast.46, f32[8,1536]{1,0:T(8,128)} %get-tuple-element.27.refs_3_.refs_2_, bf16[1536,768]{1,0:T(8,128)(2,1)} %get-tuple-element.16.refs_3_), custom_call_target="tpu_custom_call" | custom-call | tf_op jit(solution)/shard_map/pallas_call | solution.py:235
  212.1 0.8 reshape.52
  212.9 0.6 broadcast_in_dim.11
  213.5 28.9 %all-to-all-start.2 = ((bf16[32,2,192]{2,1,0:T(2,128)(2,1)}), bf16[32,2,192]{2,1,0:T(2,128)(2,1)S(1)}, u32[]{:S(2)}, u32[]{:S(2)}) async-start(bf16[32,2,192]{2,1,0:T(2,128)(2,1)} %bitcast.25), calls=%async_computation.2 | async-start | bytes 65536 | tf_op jit(solution)/shard_map/all_to_all | solution.py:355
  242.5 14.4 %all-to-all-done.2 = bf16[32,2,192]{2,1,0:T(2,128)(2,1)S(1)} async-done(((bf16[32,2,192]{2,1,0:T(2,128)(2,1)}), bf16[32,2,192]{2,1,0:T(2,128)(2,1)S(1)}, u32[]{:S(2)}, u32[]{:S(2)}) %all-to-all-start.2) | async-done | bytes 24608 | tf_op jit(solution)/shard_map/all_to_all | solution.py:355
  256.9 0.6 dynamic-slice_bitcast_fusion.2
  (87 shorter events, 3.5 us)
Async XLA Ops:
  0.7 56.2 %collective-permute-start = (s32[512]{0:T(512)S(1)}, s32[512]{0:T(512)S(1)}, u32[]{:S(2)}, u32[]{:S(2)}) collective-permute-start(s32[512]{0:T(512)S(1)} %bitcast.52), channel_id=1, source_target_pairs={{3,4},{7,8},{11,12},{15,16},{19,20},{23,24},{27,28},{31,32},{35,36... | collective-permute-start | bytes 6152 | tf_op jit(solution)/shard_map/ppermute | solution.py:278
  1.4 55.5 %collective-permute-start.1 = (s32[512]{0:T(512)S(1)}, s32[512]{0:T(512)S(1)}, u32[]{:S(2)}, u32[]{:S(2)}) collective-permute-start(s32[512]{0:T(512)S(1)} %bitcast.53), channel_id=1, source_target_pairs={{0,0},{4,4},{8,8},{12,12},{16,16},{20,20},{24,24},{28,28},{32,32},... | collective-permute-start | bytes 6152 | tf_op jit(solution)/shard_map/ppermute | solution.py:278
  2.0 54.9 %collective-permute-start.2 = (s32[512]{0:T(512)S(1)}, s32[512]{0:T(512)S(1)}, u32[]{:S(2)}, u32[]{:S(2)}) collective-permute-start(s32[512]{0:T(512)S(1)} %bitcast.54), channel_id=1, source_target_pairs={{1,0},{5,4},{9,8},{13,12},{17,16},{21,20},{25,24},{29,28},{33,32},... | collective-permute-start | bytes 6152 | tf_op jit(solution)/shard_map/ppermute | solution.py:278
  3.3 53.6 %collective-permute-start.3 = (s32[512]{0:T(512)S(1)}, s32[512]{0:T(512)S(1)}, u32[]{:S(2)}, u32[]{:S(2)}) collective-permute-start(s32[512]{0:T(512)S(1)} %bitcast.55), channel_id=1, source_target_pairs={{2,0},{6,4},{10,8},{14,12},{18,16},{22,20},{26,24},{30,28},{34,32}... | collective-permute-start | bytes 6152 | tf_op jit(solution)/shard_map/ppermute | solution.py:278
  5.5 53.1 %collective-permute-start.4 = (bf16[8,1536]{1,0:T(8,128)(2,1)S(1)}, bf16[8,1536]{1,0:T(8,128)(2,1)S(1)}, u32[]{:S(2)}, u32[]{:S(2)}) collective-permute-start(bf16[8,1536]{1,0:T(8,128)(2,1)S(1)} %maximum_maximum_fusion), channel_id=1, source_target_pairs={{0,0},{128,1},{256,2},{384,3},{1,128},{129,129},{257,130},{385,131... | collective-permute-start | bytes 73736 | tf_op jit(solution)/shard_map/ppermute | solution.py:265
  37.1 18.1 %copy-start.10 = (s32[4]{0:T(128)S(1)}, s32[4]{0:T(128)}, u32[]{:S(2)}) copy-start(s32[4]{0:T(128)} %constant.151) | copy-start | bytes 52
  37.1 18.3 %copy-start.9 = (bf16[15,4,1536]{2,1,0:T(4,128)(2,1)S(1)}, bf16[15,4,1536]{2,1,0:T(4,128)(2,1)}, u32[]{:S(2)}) copy-start(bf16[15,4,1536]{2,1,0:T(4,128)(2,1)} %param.7) | copy-start | bytes 552964
  37.1 35.9 %all-to-all-start = ((bf16[32,24,768]{2,1,0:T(8,128)(2,1)}), bf16[32,24,768]{2,1,0:T(8,128)(2,1)S(1)}, u32[]{:S(2)}, u32[]{:S(2)}) async-start(bf16[32,24,768]{2,1,0:T(8,128)(2,1)} %bitcast.9), calls=%async_computation | async-start | bytes 2359296 | tf_op jit(solution)/shard_map/all_to_all | solution.py:310
  60.5 0.6 copy-start.8
  73.1 14.0 %collective-permute-start.7 = (bf16[96,768]{1,0:T(8,128)(2,1)S(1)}, bf16[96,768]{1,0:T(8,128)(2,1)S(1)}, u32[]{:S(2)}, u32[]{:S(2)}) collective-permute-start(bf16[96,768]{1,0:T(8,128)(2,1)S(1)} %get-tuple-element.19), channel_id=1, source_target_pairs={{0,32},{16,48},{32,128},{48,144},{128,160},{144,176},{160,256},{17... | collective-permute-start | bytes 442376 | tf_op jit(solution)/shard_map/ppermute | solution.py:313
  75.0 12.1 %collective-permute-start.8 = (bf16[96,768]{1,0:T(8,128)(2,1)S(1)}, bf16[96,768]{1,0:T(8,128)(2,1)S(1)}, u32[]{:S(2)}, u32[]{:S(2)}) collective-permute-start(bf16[96,768]{1,0:T(8,128)(2,1)S(1)} %get-tuple-element.20), channel_id=1, source_target_pairs={{0,416},{16,432},{32,0},{48,16},{128,32},{144,48},{160,128},{176,1... | collective-permute-start | bytes 442376 | tf_op jit(solution)/shard_map/ppermute | solution.py:314
  80.6 7.7 %copy-start.2 = (bf16[4,96,768]{2,1,0:T(8,128)(2,1)}, bf16[4,96,768]{2,1,0:T(8,128)(2,1)S(1)}, u32[]{:S(2)}) copy-start(bf16[4,96,768]{2,1,0:T(8,128)(2,1)S(1)} %get-tuple-element.18.refs_3_) | copy-start | bytes 1769476
  80.6 44.5 %copy-start.1 = (bf16[4,96,768]{2,1,0:T(8,128)(2,1)}, bf16[4,96,768]{2,1,0:T(8,128)(2,1)S(1)}, u32[]{:S(2)}) copy-start(bf16[4,96,768]{2,1,0:T(8,128)(2,1)S(1)} %get-tuple-element.17.refs_4_) | copy-start | bytes 1769476
  80.6 28.4 %collective-permute-start.5 = (bf16[4,96,768]{2,1,0:T(8,128)(2,1)S(1)}, bf16[4,96,768]{2,1,0:T(8,128)(2,1)S(1)}, u32[]{:S(2)}, u32[]{:S(2)}) collective-permute-start(bf16[4,96,768]{2,1,0:T(8,128)(2,1)S(1)} %get-tuple-element.18.refs_3_), channel_id=1, source_target_pairs={{0,16},{16,32},{32,48},{48,128},{128,144},{144,160},{160,176},{176... | collective-permute-start | bytes 1769480 | tf_op jit(solution)/shard_map/ppermute | solution.py:319
  82.5 26.5 %collective-permute-start.6 = (bf16[4,96,768]{2,1,0:T(8,128)(2,1)S(1)}, bf16[4,96,768]{2,1,0:T(8,128)(2,1)S(1)}, u32[]{:S(2)}, u32[]{:S(2)}) collective-permute-start(bf16[4,96,768]{2,1,0:T(8,128)(2,1)S(1)} %get-tuple-element.18.refs_3_), channel_id=1, source_target_pairs={{0,432},{16,0},{32,16},{48,32},{128,48},{144,128},{160,144},{176,1... | collective-permute-start | bytes 1769480 | tf_op jit(solution)/shard_map/ppermute | solution.py:319
  88.3 20.8 %all-to-all-start.1 = ((bf16[4,2,96,768]{3,2,1,0:T(8,128)(2,1)}), bf16[4,2,96,768]{3,2,1,0:T(8,128)(2,1)S(1)}, u32[]{:S(2)}, u32[]{:S(2)}) async-start(bf16[4,2,96,768]{3,2,1,0:T(8,128)(2,1)} %broadcast_in_dim.10), calls=%async_computation.1 | async-start | bytes 2359296 | tf_op jit(solution)/shard_map/all_to_all | solution.py:250
  109.0 0.8 copy-start.6
  109.0 1.0 copy-start.7
  109.0 1.5 copy-start
  118.6 23.4 %collective-permute-start.9 = (bf16[528,768]{1,0:T(8,128)(2,1)}, bf16[528,768]{1,0:T(8,128)(2,1)S(1)}, u32[]{:S(2)}, u32[]{:S(2)}) collective-permute-start(bf16[528,768]{1,0:T(8,128)(2,1)} %get-tuple-element.13.refs_1_), channel_id=1, source_target_pairs={{0,64},{64,0},{1,65},{65,1},{2,66},{66,2},{3,67},{67,3},{4,68},{68... | collective-permute-start | bytes 2433032 | tf_op jit(solution)/shard_map/ppermute | solution.py:339
  123.1 18.0 %collective-permute-start.10 = (bf16[4,96,768]{2,1,0:T(8,128)(2,1)S(1)}, bf16[4,96,768]{2,1,0:T(8,128)(2,1)S(1)}, u32[]{:S(2)}, u32[]{:S(2)}) collective-permute-start(bf16[4,96,768]{2,1,0:T(8,128)(2,1)S(1)} %get-tuple-element.17.refs_4_), channel_id=1, source_target_pairs={{0,16},{16,32},{32,48},{48,128},{128,144},{144,160},{160,176},{176... | collective-permute-start | bytes 1769480 | tf_op jit(solution)/shard_map/ppermute | solution.py:319
  125.0 16.9 %collective-permute-start.11 = (bf16[4,96,768]{2,1,0:T(8,128)(2,1)S(1)}, bf16[4,96,768]{2,1,0:T(8,128)(2,1)S(1)}, u32[]{:S(2)}, u32[]{:S(2)}) collective-permute-start(bf16[4,96,768]{2,1,0:T(8,128)(2,1)S(1)} %get-tuple-element.17.refs_4_), channel_id=1, source_target_pairs={{0,432},{16,0},{32,16},{48,32},{128,48},{144,128},{160,144},{176,1... | collective-permute-start | bytes 1769480 | tf_op jit(solution)/shard_map/ppermute | solution.py:319
  141.1 0.9 copy-start.4
  142.0 0.8 copy-start.5
  142.0 1.1 copy-start.3
  152.7 9.3 %collective-permute-start.13 = (bf16[256,768]{1,0:T(8,128)(2,1)}, bf16[256,768]{1,0:T(8,128)(2,1)S(1)}, u32[]{:S(2)}, u32[]{:S(2)}) collective-permute-start(bf16[256,768]{1,0:T(8,128)(2,1)} %get-tuple-element.14), channel_id=1, source_target_pairs={{0,1},{4,5},{8,9},{12,13},{16,17},{20,21},{24,25},{28,29},{32,33},... | collective-permute-start | bytes 1179656 | tf_op jit(solution)/shard_map/ppermute | solution.py:289
  155.0 5.5 %collective-permute-start.12 = (bf16[12,768]{1,0:T(8,128)(2,1)S(1)}, bf16[12,768]{1,0:T(8,128)(2,1)S(1)}, u32[]{:S(2)}, u32[]{:S(2)}) collective-permute-start(bf16[12,768]{1,0:T(8,128)(2,1)S(1)} %get-tuple-element.21), channel_id=1, source_target_pairs={{0,129},{128,5},{4,133},{132,9},{8,137},{136,13},{12,141},{140,17}... | collective-permute-start | bytes 55304 | tf_op jit(solution)/shard_map/ppermute | solution.py:287
  159.6 0.9 collective-permute-start.14
  181.6 3.0 %collective-permute-start.16 = (bf16[64,768]{1,0:T(8,128)(2,1)}, bf16[64,768]{1,0:T(8,128)(2,1)S(1)}, u32[]{:S(2)}, u32[]{:S(2)}) collective-permute-start(bf16[64,768]{1,0:T(8,128)(2,1)} %shard_map.66), channel_id=1, source_target_pairs={{1,2},{5,6},{9,10},{13,14},{17,18},{21,22},{25,26},{29,30},{33,34}... | collective-permute-start | bytes 294920 | tf_op jit(solution)/shard_map/ppermute | solution.py:289
  183.1 1.5 collective-permute-start.15
  183.7 0.9 collective-permute-start.17
  197.6 2.8 %collective-permute-start.19 = (bf16[16,768]{1,0:T(8,128)(2,1)}, bf16[16,768]{1,0:T(8,128)(2,1)S(1)}, u32[]{:S(2)}, u32[]{:S(2)}) collective-permute-start(bf16[16,768]{1,0:T(8,128)(2,1)} %shard_map.68), channel_id=1, source_target_pairs={{2,3},{6,7},{10,11},{14,15},{18,19},{22,23},{26,27},{30,31},{34,35... | collective-permute-start | bytes 73736 | tf_op jit(solution)/shard_map/ppermute | solution.py:289
  199.0 1.3 collective-permute-start.18
  199.7 0.7 collective-permute-start.20
  213.5 43.4 %all-to-all-start.2 = ((bf16[32,2,192]{2,1,0:T(2,128)(2,1)}), bf16[32,2,192]{2,1,0:T(2,128)(2,1)S(1)}, u32[]{:S(2)}, u32[]{:S(2)}) async-start(bf16[32,2,192]{2,1,0:T(2,128)(2,1)} %bitcast.25), calls=%async_computation.2 | async-start | bytes 65536 | tf_op jit(solution)/shard_map/all_to_all | solution.py:355

commit v5 on v3

--- a/solution.py
+++ b/solution.py
@@ -45,7 +45,8 @@
                 a_scr[side * TILES + t, pl.ds(start + 8, 16)] = tile
         return carry
 
-    lax.fori_loop(0, up16(rows) // 16, step, 0)
+    count = up16(rows) // 16
+    lax.fori_loop(0, count, step, 0, unroll=3 if count % 3 == 0 else 1)
 
     @pl.when(meta_ref[1] == 1)
     def _():
@@ -260,7 +261,7 @@
     return ((zh * 4 + zl) * 4 + y) * 4 + role
 
 
-def gathered_bases(bases, sequence, before, count):
+def gathered_bases(bases, sequence):
     mine = lax.dynamic_index_in_dim(bases + 1, sequence, 0, keepdims=False)
     parts = []
     for by in (-1, 0, 1, 2):
@@ -271,7 +272,7 @@
                 if 0 <= place < 64:
                     pairs.append((zh * 64 + place, zh * 64 + row * 4))
         parts.append(lax.ppermute(mine, ("zh", "zl", "y", "x"), pairs))
-    return jnp.concatenate(parts)[mine.shape[0] - before :][:count]
+    return parts
 
 
 def pass_on(array, role):
@@ -295,6 +296,7 @@
     held = [point_weight[0], gains, depth_taps[0], jnp.zeros((2, C), gains.dtype)]
     held = lax.all_gather(jnp.concatenate(held, axis=0), "zh")
     held, bases = lax.optimization_barrier((held, bases))
+    ids = gathered_bases(bases, sequence)
     blocks = held[:, :24].reshape(4, 24, 2, HALF).transpose(2, 0, 1, 3)
     blocks = jnp.broadcast_to(blocks[:, None], (2, 4, 4, 24, HALF)).reshape(32, 24, HALF)
     blocks = lax.optimization_barrier(blocks)
@@ -322,7 +324,7 @@
 
     rows = RUN + 2 * EDGE
     size = up16(rows)
-    ids = gathered_bases(bases, sequence, EDGE + margin, size + 2 * margin)
+    ids = jnp.concatenate(ids)[bases.shape[1] - EDGE - margin :][: size + 2 * margin]
     windows = jnp.stack([ids[k : k + size] for k in range(2 * margin + 1)])
     kinds = jnp.arange(1, 5, dtype=jnp.int32)[None, :, None]
     hot = (windows[:, None, :] == kinds).astype(jnp.bfloat16).reshape(-1, size)
@@ -342,14 +344,18 @@
         now = run_level(run // 2 + 8, 4, True, meta, now, params[1], odd_weights)
         run = run // 4
 
-    blocks = now.reshape(2, 2, 4, HALF // 4).transpose(2, 0, 1, 3)
-    blocks = jnp.broadcast_to(
-        blocks[None, :, None], (2, 4, 2, 2, 2, HALF // 4)
-    ).reshape(32, 2, HALF // 4)
-    got = lax.all_to_all(blocks, ("zh", "co", "x"), 0, 0, tiled=True)
-    got = got.reshape(2, 2, 2, 4, 2, HALF // 4)[:, :, :, 3]
-    got = lax.dynamic_index_in_dim(got, x // 2, 1, keepdims=False)
-    return lax.dynamic_index_in_dim(got, zh // 2, 1, keepdims=False)
+    kept = jnp.zeros((2, HALF), now.dtype)
+    for k in range(2):
+        for p in range(2):
+            pairs = [
+                (((2 * b + h) * 2 + c) * 4 + 3, ((2 * c + k) * 2 + b) * 4 + 2 * h + p)
+                for b in range(2)
+                for h in range(2)
+                for c in range(2)
+            ]
+            kept = kept + lax.ppermute(now[2 * p : 2 * p + 2], ("zh", "co", "x"), pairs)
+    kept = lax.all_gather(kept, "co").reshape(2, 2, 4, HALF // 4)
+    return lax.dynamic_index_in_dim(kept, (zh % 2) * 2 + co, 2, keepdims=False)
 
 
 def solution(mesh):

time: 259 us -> 244 us (0.942)
  the two profiles are of different devices: /device:TPU:1 before, /device:TPU:135 now
where the time goes in v5:
time: 244 us; the launch traced here: 243 us
  starting transfers between devices  66.1 us (27%)
  waiting for transfers between devices  65.9 us (27%)
  Pallas kernels  49.6 us (20%)
  blocking collectives  45.1 us (18%)
  local copies, waits for them, and re-layouts  11.2 us (5%)
  other arithmetic  4.23 us (2%)
    ppermute x3, waiting for transfers between devices, pass_on(): before = lax.ppermute(array[rows - EDGE:], axes, up)  23.8 us
    pallas_call x6, Pallas kernels, run_level(): pl.pallas_call(lambda *refs: paired_level(rows, edge, *refs), in_specs=[s...  22.6 us
    all_gather x1, blocking collectives, relay(): held = lax.all_gather(jnp.concatenate(held, axis=0), 'zh')  22.5 us
    ppermute x4, waiting for transfers between devices, relay(): sides.append(lax.ppermute(near[slot], ('zh', 'zl'), ring(16, by)))  16.1 us
    ppermute x4, starting transfers between devices, relay(): kept = kept + lax.ppermute(now[2 * p:2 * p + 2], ('zh', 'co', 'x'), pairs)  14.4 us
    ppermute x4, starting transfers between devices, relay(): sides.append(lax.ppermute(near[slot], ('zh', 'zl'), ring(16, by)))  12.5 us
    all_to_all x1, waiting for transfers between devices, relay(): blocks = lax.all_to_all(blocks, ('co', 'y', 'x'), 0, 0, tiled=True)  11.9 us
    pallas_call x1, Pallas kernels, run_first_half(): pl.pallas_call(lambda *refs: first_half(rows, *refs), in_specs=[spec(pltp...  11.5 us
  transfers between devices with their start and end apart: 26, of which 8 were waited for; matrix products, arithmetic and copies ran while one was open for 3% of the time, Pallas kernels for 5%

profile of v5, /device:TPU:135, one launch (start us, length us, event | category | flops | bytes accessed | tf_op | source)
XLA Modules:
  0.0 242.7 jit_solution(7297593024523005519)
XLA Ops:
  0.1 1.0 maximum_maximum_fusion
  1.1 22.5 %all-gather = bf16[128,1536]{1,0:T(8,128)(2,1)S(1)} all-gather(bf16[32,1536]{1,0:T(8,128)(2,1)S(1)} %maximum_maximum_fusion), channel_id=2, replica_groups=mesh['zh'=4,'co'=2,'zl'=4,'y'=4,'x'=4] {'zh'}, dimensions={0}, use_global_device_ids=true | all-gather | bytes 491520 | tf_op jit(solution)/shard_map/all_gather | solution.py:297
  23.5 0.7 dynamic-slice_add_fusion
  24.2 0.6 collective-permute-start
  24.9 0.7 collective-permute-start.1
  25.6 3.4 %collective-permute-start.2 = (s32[512]{0:T(512)S(1)}, s32[512]{0:T(512)S(1)}, u32[]{:S(2)}, u32[]{:S(2)}) collective-permute-start(s32[512]{0:T(512)S(1)} %bitcast.54), channel_id=1, source_target_pairs={{1,0},{5,4},{9,8},{13,12},{17,16},{21,20},{25,24},{29,28},{33,32},... | collective-permute-start | bytes 6152 | tf_op jit(solution)/shard_map/ppermute | solution.py:274
  28.9 0.7 collective-permute-start.3
  29.8 1.2 broadcast_in_dim.7
  30.9 11.0 %all-to-all-start = ((bf16[32,24,768]{2,1,0:T(8,128)(2,1)}), bf16[32,24,768]{2,1,0:T(8,128)(2,1)S(1)}, u32[]{:S(2)}, u32[]{:S(2)}) async-start(bf16[32,24,768]{2,1,0:T(8,128)(2,1)} %bitcast.10), calls=%async_computation | async-start | bytes 2359296 | tf_op jit(solution)/shard_map/all_to_all | solution.py:303
  42.1 1.9 all_gather.54
  44.1 0.8 maximum_select_fusion.refs_2_
  44.9 0.7 slice_bitcast_fusion.2
  46.3 11.9 %all-to-all-done = bf16[32,24,768]{2,1,0:T(8,128)(2,1)S(1)} async-done(((bf16[32,24,768]{2,1,0:T(8,128)(2,1)}), bf16[32,24,768]{2,1,0:T(8,128)(2,1)S(1)}, u32[]{:S(2)}, u32[]{:S(2)}) %all-to-all-start) | async-done | bytes 1179680 | tf_op jit(solution)/shard_map/all_to_all | solution.py:303
  58.2 2.9 %collective-permute-start.6 = (bf16[96,768]{1,0:T(8,128)(2,1)S(1)}, bf16[96,768]{1,0:T(8,128)(2,1)S(1)}, u32[]{:S(2)}, u32[]{:S(2)}) collective-permute-start(bf16[96,768]{1,0:T(8,128)(2,1)S(1)} %get-tuple-element.23), channel_id=1, source_target_pairs={{0,32},{16,48},{32,128},{48,144},{128,160},{144,176},{160,256},{17... | collective-permute-start | bytes 442376 | tf_op jit(solution)/shard_map/ppermute | solution.py:306
  61.1 4.5 %collective-permute-start.7 = (bf16[96,768]{1,0:T(8,128)(2,1)S(1)}, bf16[96,768]{1,0:T(8,128)(2,1)S(1)}, u32[]{:S(2)}, u32[]{:S(2)}) collective-permute-start(bf16[96,768]{1,0:T(8,128)(2,1)S(1)} %get-tuple-element.24), channel_id=1, source_target_pairs={{0,416},{16,432},{32,0},{48,16},{128,32},{144,48},{160,128},{176,1... | collective-permute-start | bytes 442376 | tf_op jit(solution)/shard_map/ppermute | solution.py:307
  66.2 1.0 copy.14
  67.2 5.9 %collective-permute-done.7 = bf16[96,768]{1,0:T(8,128)(2,1)S(1)} collective-permute-done((bf16[96,768]{1,0:T(8,128)(2,1)S(1)}, bf16[96,768]{1,0:T(8,128)(2,1)S(1)}, u32[]{:S(2)}, u32[]{:S(2)}) %collective-permute-start.7) | collective-permute-done | bytes 147488 | tf_op jit(solution)/shard_map/ppermute | solution.py:307
  73.1 1.1 broadcast_in_dim.8
  74.2 3.5 %all-to-all-start.1 = ((bf16[4,2,96,768]{3,2,1,0:T(8,128)(2,1)}), bf16[4,2,96,768]{3,2,1,0:T(8,128)(2,1)S(1)}, u32[]{:S(2)}, u32[]{:S(2)}) async-start(bf16[4,2,96,768]{3,2,1,0:T(8,128)(2,1)} %broadcast_in_dim.8), calls=%async_computation.1 | async-start | bytes 2359296 | tf_op jit(solution)/shard_map/all_to_all | solution.py:251
  77.9 2.1 collective-permute-start.4
  79.9 4.6 %collective-permute-start.5 = (bf16[4,96,768]{2,1,0:T(8,128)(2,1)S(1)}, bf16[4,96,768]{2,1,0:T(8,128)(2,1)S(1)}, u32[]{:S(2)}, u32[]{:S(2)}) collective-permute-start(bf16[4,96,768]{2,1,0:T(8,128)(2,1)S(1)} %get-tuple-element.22.refs_3_), channel_id=1, source_target_pairs={{0,432},{16,0},{32,16},{48,32},{128,48},{144,128},{160,144},{176,1... | collective-permute-start | bytes 1769480 | tf_op jit(solution)/shard_map/ppermute | solution.py:312
  84.6 0.8 fusion.refs_1_
  85.4 11.5 %stem_and_taps.1 = (bf16[1056,768]{1,0:T(8,128)(2,1)}, bf16[1056,1536]{1,0:T(8,128)(2,1)}) custom-call(s32[19]{0:T(128)} %pad_add_fusion.refs_0_, bf16[1056,64]{1,0:T(8,128)(2,1)} %fusion.refs_1_, bf16[64,1536]{1,0:T(8,128)(2,1)} %maximum_select_fusion.refs_2_, f32[8,1536]{1,0:T(8,128)} %get-tuple-element.32.refs_3_.refs_2_), custom_call_target="tpu_custom_call" | custom-call | tf_op jit(solution)/shard_map/stem_and_taps/pallas_call | solution.py:204
  98.5 8.0 %mix_first.1 = (bf16[528,768]{1,0:T(8,128)(2,1)}, bf16[1536,768]{1,0:T(8,128)(2,1)}) custom-call(s32[19]{0:T(128)} %pad_add_fusion.refs_0_, bf16[1056,768]{1,0:T(8,128)(2,1)} %get-tuple-element.15.refs_1_, bf16[1056,1536]{1,0:T(8,128)(2,1)} %get-tuple-element.16.refs_2_, bf16[4,96,768]{2,1,0:T(8,128)(2,1)} %copy-done.2, bf16[4,96,768]{2,1,0:T(8,128)(2,1)} %copy-done.7, ...), custom_call_target="tpu_custom_call" | custom-call | tf_op jit(solution)/shard_map/mix_first/pallas_call | solution.py:215
  106.5 4.1 %collective-permute-start.8 = (bf16[528,768]{1,0:T(8,128)(2,1)}, bf16[528,768]{1,0:T(8,128)(2,1)S(1)}, u32[]{:S(2)}, u32[]{:S(2)}) collective-permute-start(bf16[528,768]{1,0:T(8,128)(2,1)} %get-tuple-element.17.refs_1_), channel_id=1, source_target_pairs={{0,64},{64,0},{1,65},{65,1},{2,66},{66,2},{3,67},{67,3},{4,68},{68... | collective-permute-start | bytes 2433032 | tf_op jit(solution)/shard_map/ppermute | solution.py:335
  110.7 3.9 %collective-permute-start.10 = (bf16[4,96,768]{2,1,0:T(8,128)(2,1)S(1)}, bf16[4,96,768]{2,1,0:T(8,128)(2,1)S(1)}, u32[]{:S(2)}, u32[]{:S(2)}) collective-permute-start(bf16[4,96,768]{2,1,0:T(8,128)(2,1)S(1)} %get-tuple-element.21.refs_4_), channel_id=1, source_target_pairs={{0,432},{16,0},{32,16},{48,32},{128,48},{144,128},{160,144},{176,1... | collective-permute-start | bytes 1769480 | tf_op jit(solution)/shard_map/ppermute | solution.py:312
  114.6 1.9 collective-permute-start.9
  116.5 10.9 %collective-permute-done.10.refs_6_ = bf16[4,96,768]{2,1,0:T(8,128)(2,1)S(1)} collective-permute-done((bf16[4,96,768]{2,1,0:T(8,128)(2,1)S(1)}, bf16[4,96,768]{2,1,0:T(8,128)(2,1)S(1)}, u32[]{:S(2)}, u32[]{:S(2)}) %collective-permute-start.10) | collective-permute-done | bytes 589856 | tf_op jit(solution)/shard_map/ppermute | solution.py:312
  127.4 4.9 %collective-permute-done.9.refs_5_ = bf16[4,96,768]{2,1,0:T(8,128)(2,1)S(1)} collective-permute-done((bf16[4,96,768]{2,1,0:T(8,128)(2,1)S(1)}, bf16[4,96,768]{2,1,0:T(8,128)(2,1)S(1)}, u32[]{:S(2)}, u32[]{:S(2)}) %collective-permute-start.9) | collective-permute-done | bytes 589856 | tf_op jit(solution)/shard_map/ppermute | solution.py:312
  132.3 0.8 copy-done.6
  133.4 7.6 %shard_map.64 = (bf16[256,768]{1,0:T(8,128)(2,1)}, bf16[1536,768]{1,0:T(8,128)(2,1)}) custom-call(s32[19]{0:T(128)} %pad_add_fusion.refs_0_, bf16[528,768]{1,0:T(8,128)(2,1)} %get-tuple-element.17.refs_1_, bf16[528,768]{1,0:T(8,128)(2,1)} %copy-done.4, f32[8,1536]{1,0:T(8,128)} %get-tuple-element.31.refs_3_.refs_2_, bf16[4,96,768]{2,1,0:T(8,128)(2,1)} %copy-done.1, ...), custom_call_target="tpu_custom_call" | custom-call | tf_op jit(solution)/shard_map/pallas_call | solution.py:226
  140.9 0.7 collective-permute-start.12
  141.6 0.8 fusion.5
  142.4 0.7 collective-permute-start.11
  143.1 0.7 collective-permute-start.13
  143.9 3.3 %all-gather.1 = bf16[576,768]{1,0:T(8,128)(2,1)} all-gather(bf16[288,768]{1,0:T(8,128)(2,1)S(1)} %pad_maximum_fusion), channel_id=3, replica_groups=mesh['zh'=4,'co'=2,'zl'=4,'y'=4,'x'=4] {'co'}, dimensions={0}, use_global_device_ids=true | all-gather | bytes 1327104 | tf_op jit(solution)/shard_map/all_gather | solution.py:341
  147.2 5.6 %shard_map.65 = bf16[144,768]{1,0:T(8,128)(2,1)} custom-call(s32[19]{0:T(128)} %pad_add_fusion.refs_0_, bf16[2,288,768]{2,1,0:T(8,128)(2,1)} %bitcast.39, f32[8,1536]{1,0:T(8,128)} %get-tuple-element.32.refs_3_.refs_2_, bf16[1536,768]{1,0:T(8,128)(2,1)} %get-tuple-element.19.refs_3_), custom_call_target="tpu_custom_call" | custom-call | tf_op jit(solution)/shard_map/pallas_call | solution.py:236
  152.8 4.0 %all-gather.2 = bf16[288,768]{1,0:T(8,128)(2,1)} all-gather(bf16[144,768]{1,0:T(8,128)(2,1)} %shard_map.65), channel_id=4, replica_groups=mesh['zh'=4,'co'=2,'zl'=4,'y'=4,'x'=4] {'co'}, dimensions={0}, use_global_device_ids=true | all-gather | bytes 663552 | tf_op jit(solution)/shard_map/all_gather | solution.py:343
  156.8 4.1 %shard_map.66 = bf16[64,768]{1,0:T(8,128)(2,1)} custom-call(s32[19]{0:T(128)} %pad_add_fusion.refs_0_, bf16[2,144,768]{2,1,0:T(8,128)(2,1)} %bitcast.40, f32[8,1536]{1,0:T(8,128)} %get-tuple-element.31.refs_3_.refs_2_, bf16[1536,768]{1,0:T(8,128)(2,1)} %get-tuple-element.20.refs_3_), custom_call_target="tpu_custom_call" | custom-call | tf_op jit(solution)/shard_map/pallas_call | solution.py:236
  160.9 0.7 collective-permute-start.15
  161.6 0.8 fusion.6
  162.4 0.7 collective-permute-start.14
  163.0 0.7 collective-permute-start.16
  163.8 2.1 all-gather.3
  165.9 3.5 %shard_map.67 = bf16[48,768]{1,0:T(8,128)(2,1)} custom-call(s32[19]{0:T(128)} %pad_add_fusion.refs_0_, bf16[2,96,768]{2,1,0:T(8,128)(2,1)} %bitcast.43, f32[8,1536]{1,0:T(8,128)} %get-tuple-element.32.refs_3_.refs_2_, bf16[1536,768]{1,0:T(8,128)(2,1)} %get-tuple-element.19.refs_3_), custom_call_target="tpu_custom_call" | custom-call | tf_op jit(solution)/shard_map/pallas_call | solution.py:236
  169.5 3.4 %all-gather.4 = bf16[96,768]{1,0:T(8,128)(2,1)} all-gather(bf16[48,768]{1,0:T(8,128)(2,1)} %shard_map.67), channel_id=6, replica_groups=mesh['zh'=4,'co'=2,'zl'=4,'y'=4,'x'=4] {'co'}, dimensions={0}, use_global_device_ids=true | all-gather | bytes 221184 | tf_op jit(solution)/shard_map/all_gather | solution.py:343
  172.9 3.2 %shard_map.68 = bf16[16,768]{1,0:T(8,128)(2,1)} custom-call(s32[19]{0:T(128)} %pad_add_fusion.refs_0_, bf16[2,48,768]{2,1,0:T(8,128)(2,1)} %bitcast.46, f32[8,1536]{1,0:T(8,128)} %get-tuple-element.31.refs_3_.refs_2_, bf16[1536,768]{1,0:T(8,128)(2,1)} %get-tuple-element.20.refs_3_), custom_call_target="tpu_custom_call" | custom-call | tf_op jit(solution)/shard_map/pallas_call | solution.py:236
  176.1 1.3 collective-permute-start.18
  177.3 0.8 fusion.8
  178.2 1.3 collective-permute-start.17
  179.5 1.3 collective-permute-start.19
  180.8 23.7 %collective-permute-done.17 = bf16[12,768]{1,0:T(8,128)(2,1)S(1)} collective-permute-done((bf16[12,768]{1,0:T(8,128)(2,1)S(1)}, bf16[12,768]{1,0:T(8,128)(2,1)S(1)}, u32[]{:S(2)}, u32[]{:S(2)}) %collective-permute-start.17) | collective-permute-done | bytes 18464 | tf_op jit(solution)/shard_map/ppermute | solution.py:283
  204.5 2.1 collective-permute-done.19
  206.6 2.7 %all-gather.5 = bf16[96,768]{1,0:T(8,128)(2,1)} all-gather(bf16[48,768]{1,0:T(8,128)(2,1)S(1)} %pad_maximum_fusion.3), channel_id=7, replica_groups=mesh['zh'=4,'co'=2,'zl'=4,'y'=4,'x'=4] {'co'}, dimensions={0}, use_global_device_ids=true | all-gather | bytes 221184 | tf_op jit(solution)/shard_map/all_gather | solution.py:341
  209.3 3.2 %shard_map.69 = bf16[16,768]{1,0:T(8,128)(2,1)} custom-call(s32[19]{0:T(128)} %pad_add_fusion.refs_0_, bf16[2,48,768]{2,1,0:T(8,128)(2,1)} %bitcast.45, f32[8,1536]{1,0:T(8,128)} %get-tuple-element.32.refs_3_.refs_2_, bf16[1536,768]{1,0:T(8,128)(2,1)} %get-tuple-element.19.refs_3_), custom_call_target="tpu_custom_call" | custom-call | tf_op jit(solution)/shard_map/pallas_call | solution.py:236
  212.5 3.4 %all-gather.6 = bf16[32,768]{1,0:T(8,128)(2,1)} all-gather(bf16[16,768]{1,0:T(8,128)(2,1)} %shard_map.69), channel_id=8, replica_groups=mesh['zh'=4,'co'=2,'zl'=4,'y'=4,'x'=4] {'co'}, dimensions={0}, use_global_device_ids=true | all-gather | bytes 73728 | tf_op jit(solution)/shard_map/all_gather | solution.py:343
  215.9 2.9 %shard_map.70 = bf16[4,768]{1,0:T(4,128)(2,1)} custom-call(s32[19]{0:T(128)} %pad_add_fusion.refs_0_, bf16[2,16,768]{2,1,0:T(8,128)(2,1)} %bitcast.47, f32[8,1536]{1,0:T(8,128)} %get-tuple-element.31.refs_3_.refs_2_, bf16[1536,768]{1,0:T(8,128)(2,1)} %get-tuple-element.20.refs_3_), custom_call_target="tpu_custom_call" | custom-call | tf_op jit(solution)/shard_map/pallas_call | solution.py:236
  218.8 0.8 fusion.10
  219.6 1.3 collective-permute-start.20
  220.9 4.4 %collective-permute-start.21 = (bf16[2,768]{1,0:T(2,128)(2,1)S(1)}, bf16[2,768]{1,0:T(2,128)(2,1)S(1)}, u32[]{:S(2)}, u32[]{:S(2)}) collective-permute-start(bf16[2,768]{1,0:T(2,128)(2,1)S(1)} %get-tuple-element.53), channel_id=1, source_target_pairs={{3,1},{67,257},{131,3},{195,259},{259,65},{323,321},{387,67},{451,... | collective-permute-start | bytes 9224 | tf_op jit(solution)/shard_map/ppermute | solution.py:356
  225.3 1.3 collective-permute-start.22
  226.6 7.4 %collective-permute-start.23 = (bf16[2,768]{1,0:T(2,128)(2,1)S(1)}, bf16[2,768]{1,0:T(2,128)(2,1)S(1)}, u32[]{:S(2)}, u32[]{:S(2)}) collective-permute-start(bf16[2,768]{1,0:T(2,128)(2,1)S(1)} %get-tuple-element.53), channel_id=1, source_target_pairs={{3,129},{67,385},{131,131},{195,387},{259,193},{323,449},{387,195}... | collective-permute-start | bytes 9224 | tf_op jit(solution)/shard_map/ppermute | solution.py:356
  234.0 6.2 %collective-permute-done.23 = bf16[2,768]{1,0:T(2,128)(2,1)S(1)} collective-permute-done((bf16[2,768]{1,0:T(2,128)(2,1)S(1)}, bf16[2,768]{1,0:T(2,128)(2,1)S(1)}, u32[]{:S(2)}, u32[]{:S(2)}) %collective-permute-start.23) | collective-permute-done | bytes 3104 | tf_op jit(solution)/shard_map/ppermute | solution.py:356
  240.2 1.8 all-gather.8
  (94 shorter events, 4.6 us)
Async XLA Ops:
  24.2 22.0 %collective-permute-start = (s32[512]{0:T(512)S(1)}, s32[512]{0:T(512)S(1)}, u32[]{:S(2)}, u32[]{:S(2)}) collective-permute-start(s32[512]{0:T(512)S(1)} %bitcast.52), channel_id=1, source_target_pairs={{3,4},{7,8},{11,12},{15,16},{19,20},{23,24},{27,28},{31,32},{35,36... | collective-permute-start | bytes 6152 | tf_op jit(solution)/shard_map/ppermute | solution.py:274
  24.9 21.3 %collective-permute-start.1 = (s32[512]{0:T(512)S(1)}, s32[512]{0:T(512)S(1)}, u32[]{:S(2)}, u32[]{:S(2)}) collective-permute-start(s32[512]{0:T(512)S(1)} %bitcast.53), channel_id=1, source_target_pairs={{0,0},{4,4},{8,8},{12,12},{16,16},{20,20},{24,24},{28,28},{32,32},... | collective-permute-start | bytes 6152 | tf_op jit(solution)/shard_map/ppermute | solution.py:274
  25.6 20.7 %collective-permute-start.2 = (s32[512]{0:T(512)S(1)}, s32[512]{0:T(512)S(1)}, u32[]{:S(2)}, u32[]{:S(2)}) collective-permute-start(s32[512]{0:T(512)S(1)} %bitcast.54), channel_id=1, source_target_pairs={{1,0},{5,4},{9,8},{13,12},{17,16},{21,20},{25,24},{29,28},{33,32},... | collective-permute-start | bytes 6152 | tf_op jit(solution)/shard_map/ppermute | solution.py:274
  28.9 17.4 %collective-permute-start.3 = (s32[512]{0:T(512)S(1)}, s32[512]{0:T(512)S(1)}, u32[]{:S(2)}, u32[]{:S(2)}) collective-permute-start(s32[512]{0:T(512)S(1)} %bitcast.55), channel_id=1, source_target_pairs={{2,0},{6,4},{10,8},{14,12},{18,16},{22,20},{26,24},{30,28},{34,32}... | collective-permute-start | bytes 6152 | tf_op jit(solution)/shard_map/ppermute | solution.py:274
  30.9 11.0 %copy-start.10 = (s32[4]{0:T(128)S(1)}, s32[4]{0:T(128)}, u32[]{:S(2)}) copy-start(s32[4]{0:T(128)} %constant.115) | copy-start | bytes 52
  30.9 13.1 %copy-start.9 = (bf16[15,4,1536]{2,1,0:T(4,128)(2,1)S(1)}, bf16[15,4,1536]{2,1,0:T(4,128)(2,1)}, u32[]{:S(2)}) copy-start(bf16[15,4,1536]{2,1,0:T(4,128)(2,1)} %param.7) | copy-start | bytes 552964
  30.9 27.3 %all-to-all-start = ((bf16[32,24,768]{2,1,0:T(8,128)(2,1)}), bf16[32,24,768]{2,1,0:T(8,128)(2,1)S(1)}, u32[]{:S(2)}, u32[]{:S(2)}) async-start(bf16[32,24,768]{2,1,0:T(8,128)(2,1)} %bitcast.10), calls=%async_computation | async-start | bytes 2359296 | tf_op jit(solution)/shard_map/all_to_all | solution.py:303
  58.2 9.0 %collective-permute-start.6 = (bf16[96,768]{1,0:T(8,128)(2,1)S(1)}, bf16[96,768]{1,0:T(8,128)(2,1)S(1)}, u32[]{:S(2)}, u32[]{:S(2)}) collective-permute-start(bf16[96,768]{1,0:T(8,128)(2,1)S(1)} %get-tuple-element.23), channel_id=1, source_target_pairs={{0,32},{16,48},{32,128},{48,144},{128,160},{144,176},{160,256},{17... | collective-permute-start | bytes 442376 | tf_op jit(solution)/shard_map/ppermute | solution.py:306
  61.1 12.0 %collective-permute-start.7 = (bf16[96,768]{1,0:T(8,128)(2,1)S(1)}, bf16[96,768]{1,0:T(8,128)(2,1)S(1)}, u32[]{:S(2)}, u32[]{:S(2)}) collective-permute-start(bf16[96,768]{1,0:T(8,128)(2,1)S(1)} %get-tuple-element.24), channel_id=1, source_target_pairs={{0,416},{16,432},{32,0},{48,16},{128,32},{144,48},{160,128},{176,1... | collective-permute-start | bytes 442376 | tf_op jit(solution)/shard_map/ppermute | solution.py:307
  74.2 23.0 %all-to-all-start.1 = ((bf16[4,2,96,768]{3,2,1,0:T(8,128)(2,1)}), bf16[4,2,96,768]{3,2,1,0:T(8,128)(2,1)S(1)}, u32[]{:S(2)}, u32[]{:S(2)}) async-start(bf16[4,2,96,768]{3,2,1,0:T(8,128)(2,1)} %broadcast_in_dim.8), calls=%async_computation.1 | async-start | bytes 2359296 | tf_op jit(solution)/shard_map/all_to_all | solution.py:251
  77.8 6.8 %copy-start.3 = (s32[60,1056]{0,1:T(8,128)S(1)}, s32[60,1056]{0,1:T(8,128)}, u32[]{:S(2)}) copy-start(s32[60,1056]{0,1:T(8,128)} %copy.14) | copy-start | bytes 760324
  77.9 19.4 %copy-start.2 = (bf16[4,96,768]{2,1,0:T(8,128)(2,1)}, bf16[4,96,768]{2,1,0:T(8,128)(2,1)S(1)}, u32[]{:S(2)}) copy-start(bf16[4,96,768]{2,1,0:T(8,128)(2,1)S(1)} %get-tuple-element.22.refs_3_) | copy-start | bytes 1769476
  77.9 36.7 %copy-start.1 = (bf16[4,96,768]{2,1,0:T(8,128)(2,1)}, bf16[4,96,768]{2,1,0:T(8,128)(2,1)S(1)}, u32[]{:S(2)}) copy-start(bf16[4,96,768]{2,1,0:T(8,128)(2,1)S(1)} %get-tuple-element.21.refs_4_) | copy-start | bytes 1769476
  77.9 19.0 %collective-permute-start.4 = (bf16[4,96,768]{2,1,0:T(8,128)(2,1)S(1)}, bf16[4,96,768]{2,1,0:T(8,128)(2,1)S(1)}, u32[]{:S(2)}, u32[]{:S(2)}) collective-permute-start(bf16[4,96,768]{2,1,0:T(8,128)(2,1)S(1)} %get-tuple-element.22.refs_3_), channel_id=1, source_target_pairs={{0,16},{16,32},{32,48},{48,128},{128,144},{144,160},{160,176},{176... | collective-permute-start | bytes 1769480 | tf_op jit(solution)/shard_map/ppermute | solution.py:312
  79.9 17.3 %collective-permute-start.5 = (bf16[4,96,768]{2,1,0:T(8,128)(2,1)S(1)}, bf16[4,96,768]{2,1,0:T(8,128)(2,1)S(1)}, u32[]{:S(2)}, u32[]{:S(2)}) collective-permute-start(bf16[4,96,768]{2,1,0:T(8,128)(2,1)S(1)} %get-tuple-element.22.refs_3_), channel_id=1, source_target_pairs={{0,432},{16,0},{32,16},{48,32},{128,48},{144,128},{160,144},{176,1... | collective-permute-start | bytes 1769480 | tf_op jit(solution)/shard_map/ppermute | solution.py:312
  96.9 0.8 copy-start.7
  97.2 0.8 copy-start.8
  97.2 1.3 copy-start
  106.5 25.8 %collective-permute-start.8 = (bf16[528,768]{1,0:T(8,128)(2,1)}, bf16[528,768]{1,0:T(8,128)(2,1)S(1)}, u32[]{:S(2)}, u32[]{:S(2)}) collective-permute-start(bf16[528,768]{1,0:T(8,128)(2,1)} %get-tuple-element.17.refs_1_), channel_id=1, source_target_pairs={{0,64},{64,0},{1,65},{65,1},{2,66},{66,2},{3,67},{67,3},{4,68},{68... | collective-permute-start | bytes 2433032 | tf_op jit(solution)/shard_map/ppermute | solution.py:335
  110.7 16.8 %collective-permute-start.10 = (bf16[4,96,768]{2,1,0:T(8,128)(2,1)S(1)}, bf16[4,96,768]{2,1,0:T(8,128)(2,1)S(1)}, u32[]{:S(2)}, u32[]{:S(2)}) collective-permute-start(bf16[4,96,768]{2,1,0:T(8,128)(2,1)S(1)} %get-tuple-element.21.refs_4_), channel_id=1, source_target_pairs={{0,432},{16,0},{32,16},{48,32},{128,48},{144,128},{160,144},{176,1... | collective-permute-start | bytes 1769480 | tf_op jit(solution)/shard_map/ppermute | solution.py:312
  114.6 17.7 %collective-permute-start.9 = (bf16[4,96,768]{2,1,0:T(8,128)(2,1)S(1)}, bf16[4,96,768]{2,1,0:T(8,128)(2,1)S(1)}, u32[]{:S(2)}, u32[]{:S(2)}) collective-permute-start(bf16[4,96,768]{2,1,0:T(8,128)(2,1)S(1)} %get-tuple-element.21.refs_4_), channel_id=1, source_target_pairs={{0,16},{16,32},{32,48},{48,128},{128,144},{144,160},{160,176},{176... | collective-permute-start | bytes 1769480 | tf_op jit(solution)/shard_map/ppermute | solution.py:312
  127.4 4.9 %copy-start.5 = (bf16[4,96,768]{2,1,0:T(8,128)(2,1)}, bf16[4,96,768]{2,1,0:T(8,128)(2,1)S(1)}, u32[]{:S(2)}) copy-start(bf16[4,96,768]{2,1,0:T(8,128)(2,1)S(1)} %collective-permute-done.10.refs_6_) | copy-start | bytes 1769476
  132.3 0.8 copy-start.6
  132.3 1.1 copy-start.4
  140.9 2.8 %collective-permute-start.12 = (bf16[256,768]{1,0:T(8,128)(2,1)}, bf16[256,768]{1,0:T(8,128)(2,1)S(1)}, u32[]{:S(2)}, u32[]{:S(2)}) collective-permute-start(bf16[256,768]{1,0:T(8,128)(2,1)} %get-tuple-element.18), channel_id=1, source_target_pairs={{0,1},{4,5},{8,9},{12,13},{16,17},{20,21},{24,25},{28,29},{32,33},... | collective-permute-start | bytes 1179656 | tf_op jit(solution)/shard_map/ppermute | solution.py:285
  142.4 1.3 collective-permute-start.11
  143.1 0.7 collective-permute-start.13
  160.9 2.8 %collective-permute-start.15 = (bf16[64,768]{1,0:T(8,128)(2,1)}, bf16[64,768]{1,0:T(8,128)(2,1)S(1)}, u32[]{:S(2)}, u32[]{:S(2)}) collective-permute-start(bf16[64,768]{1,0:T(8,128)(2,1)} %shard_map.66), channel_id=1, source_target_pairs={{1,2},{5,6},{9,10},{13,14},{17,18},{21,22},{25,26},{29,30},{33,34}... | collective-permute-start | bytes 294920 | tf_op jit(solution)/shard_map/ppermute | solution.py:285
  162.4 1.3 collective-permute-start.14
  163.0 0.7 collective-permute-start.16
  176.1 30.5 %collective-permute-start.18 = (bf16[16,768]{1,0:T(8,128)(2,1)}, bf16[16,768]{1,0:T(8,128)(2,1)S(1)}, u32[]{:S(2)}, u32[]{:S(2)}) collective-permute-start(bf16[16,768]{1,0:T(8,128)(2,1)} %shard_map.68), channel_id=1, source_target_pairs={{2,3},{6,7},{10,11},{14,15},{18,19},{22,23},{26,27},{30,31},{34,35... | collective-permute-start | bytes 73736 | tf_op jit(solution)/shard_map/ppermute | solution.py:285
  178.2 26.3 %collective-permute-start.17 = (bf16[12,768]{1,0:T(8,128)(2,1)S(1)}, bf16[12,768]{1,0:T(8,128)(2,1)S(1)}, u32[]{:S(2)}, u32[]{:S(2)}) collective-permute-start(bf16[12,768]{1,0:T(8,128)(2,1)S(1)} %get-tuple-element.35), channel_id=1, source_target_pairs={{2,131},{130,7},{6,135},{134,11},{10,139},{138,15},{14,143},{142,1... | collective-permute-start | bytes 55304 | tf_op jit(solution)/shard_map/ppermute | solution.py:283
  179.5 27.1 %collective-permute-start.19 = (bf16[12,768]{1,0:T(8,128)(2,1)S(1)}, bf16[12,768]{1,0:T(8,128)(2,1)S(1)}, u32[]{:S(2)}, u32[]{:S(2)}) collective-permute-start(bf16[12,768]{1,0:T(8,128)(2,1)S(1)} %get-tuple-element.36), channel_id=1, source_target_pairs={{130,3},{6,131},{134,7},{10,135},{138,11},{14,139},{142,15},{18,14... | collective-permute-start | bytes 55304 | tf_op jit(solution)/shard_map/ppermute | solution.py:284
  219.6 14.4 %collective-permute-start.20 = (bf16[2,768]{1,0:T(2,128)(2,1)S(1)}, bf16[2,768]{1,0:T(2,128)(2,1)S(1)}, u32[]{:S(2)}, u32[]{:S(2)}) collective-permute-start(bf16[2,768]{1,0:T(2,128)(2,1)S(1)} %get-tuple-element.52), channel_id=1, source_target_pairs={{3,0},{67,256},{131,2},{195,258},{259,64},{323,320},{387,66},{451,... | collective-permute-start | bytes 9224 | tf_op jit(solution)/shard_map/ppermute | solution.py:356
  220.9 13.1 %collective-permute-start.21 = (bf16[2,768]{1,0:T(2,128)(2,1)S(1)}, bf16[2,768]{1,0:T(2,128)(2,1)S(1)}, u32[]{:S(2)}, u32[]{:S(2)}) collective-permute-start(bf16[2,768]{1,0:T(2,128)(2,1)S(1)} %get-tuple-element.53), channel_id=1, source_target_pairs={{3,1},{67,257},{131,3},{195,259},{259,65},{323,321},{387,67},{451,... | collective-permute-start | bytes 9224 | tf_op jit(solution)/shard_map/ppermute | solution.py:356
  225.3 8.7 %collective-permute-start.22 = (bf16[2,768]{1,0:T(2,128)(2,1)S(1)}, bf16[2,768]{1,0:T(2,128)(2,1)S(1)}, u32[]{:S(2)}, u32[]{:S(2)}) collective-permute-start(bf16[2,768]{1,0:T(2,128)(2,1)S(1)} %get-tuple-element.52), channel_id=1, source_target_pairs={{3,128},{67,384},{131,130},{195,386},{259,192},{323,448},{387,194}... | collective-permute-start | bytes 9224 | tf_op jit(solution)/shard_map/ppermute | solution.py:356
  226.6 13.6 %collective-permute-start.23 = (bf16[2,768]{1,0:T(2,128)(2,1)S(1)}, bf16[2,768]{1,0:T(2,128)(2,1)S(1)}, u32[]{:S(2)}, u32[]{:S(2)}) collective-permute-start(bf16[2,768]{1,0:T(2,128)(2,1)S(1)} %get-tuple-element.53), channel_id=1, source_target_pairs={{3,129},{67,385},{131,131},{195,387},{259,193},{323,449},{387,195}... | collective-permute-start | bytes 9224 | tf_op jit(solution)/shard_map/ppermute | solution.py:356

commit v6 on v5

--- a/solution.py
+++ b/solution.py
@@ -18,6 +18,7 @@
 SHIFTS = (0, 1, -1, 2)
 TILES = HALF // 128
 GELU = 0.7978845608028654
+GRANT = pltpu.CompilerParams(vmem_limit_bytes=24 << 20)
 
 
 def up16(rows):
@@ -46,7 +47,7 @@
         return carry
 
     count = up16(rows) // 16
-    lax.fori_loop(0, count, step, 0, unroll=3 if count % 3 == 0 else 1)
+    lax.fori_loop(0, count, step, 0, unroll=next(n for n in (11, 9, 6, 3, 1) if count % n == 0))
 
     @pl.when(meta_ref[1] == 1)
     def _():
@@ -218,6 +219,7 @@
         out_specs=[spec(), spec()],
         out_shape=[half_rows(out_rows(rows, False)), half_rows(C)],
         scratch_shapes=scratch(rows, "ys"),
+        compiler_params=GRANT,
         name="mix_first",
     )(meta, x, d, *pieces)
 
@@ -229,6 +231,7 @@
         out_specs=[spec(), spec()],
         out_shape=[half_rows(out_rows(rows, True)), half_rows(C)],
         scratch_shapes=scratch(rows, "adys"),
+        compiler_params=GRANT,
     )(meta, own, other, par, *pieces)
 
 
@@ -239,6 +242,7 @@
         out_specs=spec(),
         out_shape=half_rows(out_rows(rows, last)),
         scratch_shapes=scratch(rows, "ady"),
+        compiler_params=GRANT,
     )(meta, x, par, weights)
 
 

time: 244 us -> 225 us (0.922)
  Pallas kernels: 49.6 us -> 35.4 us
  blocking collectives: 45.1 us -> 40.1 us
  waiting for transfers between devices: 65.9 us -> 68.4 us
    pallas_call x6, Pallas kernels: 22.6 us -> 10.3 us  [run_level(): pl.pallas_call(lambda *refs: paired_level(rows, edge, *refs), in_specs=[s...]
    all_gather x3, blocking collectives: 10.7 us -> 5.91 us  [relay(): now = lax.all_gather(now, 'co')]
  transfers between devices with their start and end apart: 26 -> 26, of which waited for: 8 -> 9; matrix products, arithmetic and copies ran while one was open for 3% -> 3% of each run, Pallas kernels for 5% -> 4%
where the time goes in v6:
time: 225 us; the launch traced here: 224 us
  waiting for transfers between devices  68.4 us (30%)
  starting transfers between devices  65.9 us (29%)
  blocking collectives  40.1 us (18%)
  Pallas kernels  35.4 us (16%)
  local copies, waits for them, and re-layouts  9.47 us (4%)
  other arithmetic  4.22 us (2%)
    ppermute x3, waiting for transfers between devices, pass_on(): before = lax.ppermute(array[rows - EDGE:], axes, up)  23.6 us
    all_gather x1, blocking collectives, relay(): held = lax.all_gather(jnp.concatenate(held, axis=0), 'zh')  22.5 us
    ppermute x4, waiting for transfers between devices, relay(): sides.append(lax.ppermute(near[slot], ('zh', 'zl'), ring(16, by)))  17.7 us
    ppermute x4, starting transfers between devices, relay(): kept = kept + lax.ppermute(now[2 * p:2 * p + 2], ('zh', 'co', 'x'), pairs)  14.1 us
    ppermute x4, starting transfers between devices, relay(): sides.append(lax.ppermute(near[slot], ('zh', 'zl'), ring(16, by)))  12.3 us
    all_to_all x1, waiting for transfers between devices, relay(): blocks = lax.all_to_all(blocks, ('co', 'y', 'x'), 0, 0, tiled=True)  11.9 us
    all_to_all x1, starting transfers between devices, relay(): blocks = lax.all_to_all(blocks, ('co', 'y', 'x'), 0, 0, tiled=True)  11 us
    pallas_call x6, Pallas kernels, run_level(): pl.pallas_call(lambda *refs: paired_level(rows, edge, *refs), in_specs=[s...  10.3 us
  transfers between devices with their start and end apart: 26, of which 9 were waited for; matrix products, arithmetic and copies ran while one was open for 3% of the time, Pallas kernels for 4%

profile of v6, /device:TPU:135, one launch (start us, length us, event | category | flops | bytes accessed | tf_op | source)
XLA Modules:
  0.0 224.2 jit_solution(8989294369740869192)
XLA Ops:
  0.1 1.0 maximum_maximum_fusion
  1.1 22.5 %all-gather = bf16[128,1536]{1,0:T(8,128)(2,1)S(1)} all-gather(bf16[32,1536]{1,0:T(8,128)(2,1)S(1)} %maximum_maximum_fusion), channel_id=2, replica_groups=mesh['zh'=4,'co'=2,'zl'=4,'y'=4,'x'=4] {'zh'}, dimensions={0}, use_global_device_ids=true | all-gather | bytes 491520 | tf_op jit(solution)/shard_map/all_gather | solution.py:301
  23.5 0.7 dynamic-slice_add_fusion
  24.2 0.6 collective-permute-start
  24.9 0.7 collective-permute-start.1
  25.6 3.4 %collective-permute-start.2 = (s32[512]{0:T(512)S(1)}, s32[512]{0:T(512)S(1)}, u32[]{:S(2)}, u32[]{:S(2)}) collective-permute-start(s32[512]{0:T(512)S(1)} %bitcast.54), channel_id=1, source_target_pairs={{1,0},{5,4},{9,8},{13,12},{17,16},{21,20},{25,24},{29,28},{33,32},... | collective-permute-start | bytes 6152 | tf_op jit(solution)/shard_map/ppermute | solution.py:278
  28.9 0.7 collective-permute-start.3
  29.8 1.1 broadcast_in_dim.7
  30.9 11.0 %all-to-all-start = ((bf16[32,24,768]{2,1,0:T(8,128)(2,1)}), bf16[32,24,768]{2,1,0:T(8,128)(2,1)S(1)}, u32[]{:S(2)}, u32[]{:S(2)}) async-start(bf16[32,24,768]{2,1,0:T(8,128)(2,1)} %bitcast.10), calls=%async_computation | async-start | bytes 2359296 | tf_op jit(solution)/shard_map/all_to_all | solution.py:307
  42.1 1.9 all_gather.54
  44.1 0.7 maximum_select_fusion.refs_2_
  44.8 0.6 slice_bitcast_fusion.2
  45.5 0.6 pad_add_fusion.refs_0_
  46.3 11.9 %all-to-all-done = bf16[32,24,768]{2,1,0:T(8,128)(2,1)S(1)} async-done(((bf16[32,24,768]{2,1,0:T(8,128)(2,1)}), bf16[32,24,768]{2,1,0:T(8,128)(2,1)S(1)}, u32[]{:S(2)}, u32[]{:S(2)}) %all-to-all-start) | async-done | bytes 1179680 | tf_op jit(solution)/shard_map/all_to_all | solution.py:307
  58.2 2.9 %collective-permute-start.6 = (bf16[96,768]{1,0:T(8,128)(2,1)S(1)}, bf16[96,768]{1,0:T(8,128)(2,1)S(1)}, u32[]{:S(2)}, u32[]{:S(2)}) collective-permute-start(bf16[96,768]{1,0:T(8,128)(2,1)S(1)} %get-tuple-element.23), channel_id=1, source_target_pairs={{0,32},{16,48},{32,128},{48,144},{128,160},{144,176},{160,256},{17... | collective-permute-start | bytes 442376 | tf_op jit(solution)/shard_map/ppermute | solution.py:310
  61.1 4.5 %collective-permute-start.7 = (bf16[96,768]{1,0:T(8,128)(2,1)S(1)}, bf16[96,768]{1,0:T(8,128)(2,1)S(1)}, u32[]{:S(2)}, u32[]{:S(2)}) collective-permute-start(bf16[96,768]{1,0:T(8,128)(2,1)S(1)} %get-tuple-element.24), channel_id=1, source_target_pairs={{0,416},{16,432},{32,0},{48,16},{128,32},{144,48},{160,128},{176,1... | collective-permute-start | bytes 442376 | tf_op jit(solution)/shard_map/ppermute | solution.py:311
  66.5 6.6 %collective-permute-done.7 = bf16[96,768]{1,0:T(8,128)(2,1)S(1)} collective-permute-done((bf16[96,768]{1,0:T(8,128)(2,1)S(1)}, bf16[96,768]{1,0:T(8,128)(2,1)S(1)}, u32[]{:S(2)}, u32[]{:S(2)}) %collective-permute-start.7) | collective-permute-done | bytes 147488 | tf_op jit(solution)/shard_map/ppermute | solution.py:311
  73.1 1.1 broadcast_in_dim.8
  74.3 3.5 %all-to-all-start.1 = ((bf16[4,2,96,768]{3,2,1,0:T(8,128)(2,1)}), bf16[4,2,96,768]{3,2,1,0:T(8,128)(2,1)S(1)}, u32[]{:S(2)}, u32[]{:S(2)}) async-start(bf16[4,2,96,768]{3,2,1,0:T(8,128)(2,1)} %broadcast_in_dim.8), calls=%async_computation.1 | async-start | bytes 2359296 | tf_op jit(solution)/shard_map/all_to_all | solution.py:255
  77.8 1.3 slice_bitcast_fusion
  79.1 1.9 collective-permute-start.4
  81.1 4.6 %collective-permute-start.5 = (bf16[4,96,768]{2,1,0:T(8,128)(2,1)S(1)}, bf16[4,96,768]{2,1,0:T(8,128)(2,1)}, u32[]{:S(2)}, u32[]{:S(2)}) collective-permute-start(bf16[4,96,768]{2,1,0:T(8,128)(2,1)S(1)} %get-tuple-element.22.refs_3_), channel_id=1, source_target_pairs={{0,432},{16,0},{32,16},{48,32},{128,48},{144,128},{160,144},{176,1... | collective-permute-start | bytes 1769480 | tf_op jit(solution)/shard_map/ppermute | solution.py:316
  85.7 0.8 fusion.refs_1_
  86.5 10.0 %stem_and_taps.1 = (bf16[1056,768]{1,0:T(8,128)(2,1)}, bf16[1056,1536]{1,0:T(8,128)(2,1)}) custom-call(s32[19]{0:T(128)} %pad_add_fusion.refs_0_, bf16[1056,64]{1,0:T(8,128)(2,1)} %fusion.refs_1_, bf16[64,1536]{1,0:T(8,128)(2,1)} %maximum_select_fusion.refs_2_, f32[8,1536]{1,0:T(8,128)} %get-tuple-element.32.refs_3_.refs_2_), custom_call_target="tpu_custom_call" | custom-call | tf_op jit(solution)/shard_map/stem_and_taps/pallas_call | solution.py:205
  96.5 1.9 collective-permute-done.5.refs_5_
  98.4 1.9 copy-done
  100.4 1.4 copy-done.1
  101.8 6.4 %mix_first.1 = (bf16[528,768]{1,0:T(8,128)(2,1)S(1)}, bf16[1536,768]{1,0:T(8,128)(2,1)S(1)}) custom-call(s32[19]{0:T(128)S(1)} %copy-done.3, bf16[1056,768]{1,0:T(8,128)(2,1)S(1)} %copy-done.1, bf16[1056,1536]{1,0:T(8,128)(2,1)S(1)} %copy-done, bf16[4,96,768]{2,1,0:T(8,128)(2,1)S(1)} %get-tuple-element.22.refs_3_, ...), custom_call_target="tpu_custom_call" | custom-call | tf_op jit(solution)/shard_map/mix_first/pallas_call | solution.py:216
  108.2 4.1 %collective-permute-start.8 = (bf16[528,768]{1,0:T(8,128)(2,1)S(1)}, bf16[528,768]{1,0:T(8,128)(2,1)S(1)}, u32[]{:S(2)}, u32[]{:S(2)}) collective-permute-start(bf16[528,768]{1,0:T(8,128)(2,1)S(1)} %get-tuple-element.17.refs_1_), channel_id=1, source_target_pairs={{0,64},{64,0},{1,65},{65,1},{2,66},{66,2},{3,67},{67,3},{4,68},{68... | collective-permute-start | bytes 2433032 | tf_op jit(solution)/shard_map/ppermute | solution.py:339
  112.3 3.9 %collective-permute-start.10 = (bf16[4,96,768]{2,1,0:T(8,128)(2,1)S(1)}, bf16[4,96,768]{2,1,0:T(8,128)(2,1)S(1)}, u32[]{:S(2)}, u32[]{:S(2)}) collective-permute-start(bf16[4,96,768]{2,1,0:T(8,128)(2,1)S(1)} %get-tuple-element.21.refs_4_), channel_id=1, source_target_pairs={{0,432},{16,0},{32,16},{48,32},{128,48},{144,128},{160,144},{176,1... | collective-permute-start | bytes 1769480 | tf_op jit(solution)/shard_map/ppermute | solution.py:316
  116.2 1.9 collective-permute-start.9
  118.2 10.9 %collective-permute-done.10.refs_6_ = bf16[4,96,768]{2,1,0:T(8,128)(2,1)S(1)} collective-permute-done((bf16[4,96,768]{2,1,0:T(8,128)(2,1)S(1)}, bf16[4,96,768]{2,1,0:T(8,128)(2,1)S(1)}, u32[]{:S(2)}, u32[]{:S(2)}) %collective-permute-start.10) | collective-permute-done | bytes 589856 | tf_op jit(solution)/shard_map/ppermute | solution.py:316
  129.1 4.9 %collective-permute-done.9.refs_5_ = bf16[4,96,768]{2,1,0:T(8,128)(2,1)S(1)} collective-permute-done((bf16[4,96,768]{2,1,0:T(8,128)(2,1)S(1)}, bf16[4,96,768]{2,1,0:T(8,128)(2,1)S(1)}, u32[]{:S(2)}, u32[]{:S(2)}) %collective-permute-start.9) | collective-permute-done | bytes 589856 | tf_op jit(solution)/shard_map/ppermute | solution.py:316
  133.9 8.7 %shard_map.64 = (bf16[256,768]{1,0:T(8,128)(2,1)S(1)}, bf16[1536,768]{1,0:T(8,128)(2,1)S(1)}) custom-call(s32[19]{0:T(128)S(1)} %copy-done.3, bf16[528,768]{1,0:T(8,128)(2,1)S(1)} %get-tuple-element.17.refs_1_, bf16[528,768]{1,0:T(8,128)(2,1)S(1)} %collective-permute-done.8.refs_2_, f32[8,1536]{1,0:T(8,128)S(1)} %get-tuple-element.31.refs_3_.refs_2_, ...), custom_call_target="tpu_custom_call" | custom-call | tf_op jit(solution)/shard_map/pallas_call | solution.py:228
  142.7 0.8 collective-permute-start.12
  143.5 0.7 collective-permute-start.11
  144.2 0.7 collective-permute-start.13
  145.0 3.2 %all-gather.1 = bf16[576,768]{1,0:T(8,128)(2,1)S(1)} all-gather(bf16[288,768]{1,0:T(8,128)(2,1)S(1)} %pad_maximum_fusion), channel_id=3, replica_groups=mesh['zh'=4,'co'=2,'zl'=4,'y'=4,'x'=4] {'co'}, dimensions={0}, use_global_device_ids=true | all-gather | bytes 1327104 | tf_op jit(solution)/shard_map/all_gather | solution.py:345
  148.2 3.3 %shard_map.65 = bf16[144,768]{1,0:T(8,128)(2,1)S(1)} custom-call(s32[19]{0:T(128)S(1)} %copy-done.3, bf16[2,288,768]{2,1,0:T(8,128)(2,1)S(1)} %bitcast.37, f32[8,1536]{1,0:T(8,128)S(1)} %copy-done.2, bf16[1536,768]{1,0:T(8,128)(2,1)S(1)} %get-tuple-element.19.refs_3_), custom_call_target="tpu_custom_call" | custom-call | tf_op jit(solution)/shard_map/pallas_call | solution.py:239
  151.5 2.1 all-gather.2
  153.6 1.8 shard_map.66
  155.4 0.7 collective-permute-start.15
  156.1 0.7 collective-permute-start.14
  156.8 0.7 collective-permute-start.16
  157.6 2.0 all-gather.3
  159.6 1.5 shard_map.67
  161.1 1.9 all-gather.4
  163.1 1.3 shard_map.68
  164.4 1.3 collective-permute-start.18
  165.7 1.3 collective-permute-start.17
  167.0 1.3 collective-permute-start.19
  168.3 23.6 %collective-permute-done.17 = bf16[12,768]{1,0:T(8,128)(2,1)S(1)} collective-permute-done((bf16[12,768]{1,0:T(8,128)(2,1)S(1)}, bf16[12,768]{1,0:T(8,128)(2,1)S(1)}, u32[]{:S(2)}, u32[]{:S(2)}) %collective-permute-start.17) | collective-permute-done | bytes 18464 | tf_op jit(solution)/shard_map/ppermute | solution.py:287
  191.9 2.1 collective-permute-done.19
  194.1 2.8 %all-gather.5 = bf16[96,768]{1,0:T(8,128)(2,1)S(1)} all-gather(bf16[48,768]{1,0:T(8,128)(2,1)S(1)} %pad_maximum_fusion.3), channel_id=7, replica_groups=mesh['zh'=4,'co'=2,'zl'=4,'y'=4,'x'=4] {'co'}, dimensions={0}, use_global_device_ids=true | all-gather | bytes 221184 | tf_op jit(solution)/shard_map/all_gather | solution.py:345
  196.8 1.3 shard_map.69
  198.2 1.8 all-gather.6
  200.0 1.1 shard_map.70
  201.2 1.3 collective-permute-start.20
  202.5 4.3 %collective-permute-start.21 = (bf16[2,768]{1,0:T(2,128)(2,1)S(1)}, bf16[2,768]{1,0:T(2,128)(2,1)S(1)}, u32[]{:S(2)}, u32[]{:S(2)}) collective-permute-start(bf16[2,768]{1,0:T(2,128)(2,1)S(1)} %get-tuple-element.53), channel_id=1, source_target_pairs={{3,1},{67,257},{131,3},{195,259},{259,65},{323,321},{387,67},{451,... | collective-permute-start | bytes 9224 | tf_op jit(solution)/shard_map/ppermute | solution.py:360
  206.8 1.3 collective-permute-start.22
  208.1 7.2 %collective-permute-start.23 = (bf16[2,768]{1,0:T(2,128)(2,1)S(1)}, bf16[2,768]{1,0:T(2,128)(2,1)S(1)}, u32[]{:S(2)}, u32[]{:S(2)}) collective-permute-start(bf16[2,768]{1,0:T(2,128)(2,1)S(1)} %get-tuple-element.53), channel_id=1, source_target_pairs={{3,129},{67,385},{131,131},{195,387},{259,193},{323,449},{387,195}... | collective-permute-start | bytes 9224 | tf_op jit(solution)/shard_map/ppermute | solution.py:360
  215.3 6.4 %collective-permute-done.23 = bf16[2,768]{1,0:T(2,128)(2,1)S(1)} collective-permute-done((bf16[2,768]{1,0:T(2,128)(2,1)S(1)}, bf16[2,768]{1,0:T(2,128)(2,1)S(1)}, u32[]{:S(2)}, u32[]{:S(2)}) %collective-permute-start.23) | collective-permute-done | bytes 3104 | tf_op jit(solution)/shard_map/ppermute | solution.py:360
  221.7 1.8 all-gather.8
  223.6 0.6 copy.20
  (86 shorter events, 1.9 us)
Async XLA Ops:
  24.2 21.9 %collective-permute-start = (s32[512]{0:T(512)S(1)}, s32[512]{0:T(512)S(1)}, u32[]{:S(2)}, u32[]{:S(2)}) collective-permute-start(s32[512]{0:T(512)S(1)} %bitcast.52), channel_id=1, source_target_pairs={{3,4},{7,8},{11,12},{15,16},{19,20},{23,24},{27,28},{31,32},{35,36... | collective-permute-start | bytes 6152 | tf_op jit(solution)/shard_map/ppermute | solution.py:278
  24.9 21.3 %collective-permute-start.1 = (s32[512]{0:T(512)S(1)}, s32[512]{0:T(512)S(1)}, u32[]{:S(2)}, u32[]{:S(2)}) collective-permute-start(s32[512]{0:T(512)S(1)} %bitcast.53), channel_id=1, source_target_pairs={{0,0},{4,4},{8,8},{12,12},{16,16},{20,20},{24,24},{28,28},{32,32},... | collective-permute-start | bytes 6152 | tf_op jit(solution)/shard_map/ppermute | solution.py:278
  25.6 20.6 %collective-permute-start.2 = (s32[512]{0:T(512)S(1)}, s32[512]{0:T(512)S(1)}, u32[]{:S(2)}, u32[]{:S(2)}) collective-permute-start(s32[512]{0:T(512)S(1)} %bitcast.54), channel_id=1, source_target_pairs={{1,0},{5,4},{9,8},{13,12},{17,16},{21,20},{25,24},{29,28},{33,32},... | collective-permute-start | bytes 6152 | tf_op jit(solution)/shard_map/ppermute | solution.py:278
  28.9 17.3 %collective-permute-start.3 = (s32[512]{0:T(512)S(1)}, s32[512]{0:T(512)S(1)}, u32[]{:S(2)}, u32[]{:S(2)}) collective-permute-start(s32[512]{0:T(512)S(1)} %bitcast.55), channel_id=1, source_target_pairs={{2,0},{6,4},{10,8},{14,12},{18,16},{22,20},{26,24},{30,28},{34,32}... | collective-permute-start | bytes 6152 | tf_op jit(solution)/shard_map/ppermute | solution.py:278
  30.9 11.0 %copy-start.6 = (s32[4]{0:T(128)S(1)}, s32[4]{0:T(128)}, u32[]{:S(2)}) copy-start(s32[4]{0:T(128)} %constant.115) | copy-start | bytes 52
  30.9 13.1 %copy-start.5 = (bf16[15,4,1536]{2,1,0:T(4,128)(2,1)S(1)}, bf16[15,4,1536]{2,1,0:T(4,128)(2,1)}, u32[]{:S(2)}) copy-start(bf16[15,4,1536]{2,1,0:T(4,128)(2,1)} %param.7) | copy-start | bytes 552964
  30.9 27.3 %all-to-all-start = ((bf16[32,24,768]{2,1,0:T(8,128)(2,1)}), bf16[32,24,768]{2,1,0:T(8,128)(2,1)S(1)}, u32[]{:S(2)}, u32[]{:S(2)}) async-start(bf16[32,24,768]{2,1,0:T(8,128)(2,1)} %bitcast.10), calls=%async_computation | async-start | bytes 2359296 | tf_op jit(solution)/shard_map/all_to_all | solution.py:307
  58.2 8.3 %copy-start.4 = (bf16[32,24,768]{2,1,0:T(8,128)(2,1)}, bf16[32,24,768]{2,1,0:T(8,128)(2,1)S(1)}, u32[]{:S(2)}) copy-start(bf16[32,24,768]{2,1,0:T(8,128)(2,1)S(1)} %all-to-all-done) | copy-start | bytes 3538948
  58.2 8.3 %collective-permute-start.6 = (bf16[96,768]{1,0:T(8,128)(2,1)S(1)}, bf16[96,768]{1,0:T(8,128)(2,1)S(1)}, u32[]{:S(2)}, u32[]{:S(2)}) collective-permute-start(bf16[96,768]{1,0:T(8,128)(2,1)S(1)} %get-tuple-element.23), channel_id=1, source_target_pairs={{0,32},{16,48},{32,128},{48,144},{128,160},{144,176},{160,256},{17... | collective-permute-start | bytes 442376 | tf_op jit(solution)/shard_map/ppermute | solution.py:310
  61.1 12.0 %collective-permute-start.7 = (bf16[96,768]{1,0:T(8,128)(2,1)S(1)}, bf16[96,768]{1,0:T(8,128)(2,1)S(1)}, u32[]{:S(2)}, u32[]{:S(2)}) collective-permute-start(bf16[96,768]{1,0:T(8,128)(2,1)S(1)} %get-tuple-element.24), channel_id=1, source_target_pairs={{0,416},{16,432},{32,0},{48,16},{128,32},{144,48},{160,128},{176,1... | collective-permute-start | bytes 442376 | tf_op jit(solution)/shard_map/ppermute | solution.py:311
  74.3 24.2 %all-to-all-start.1 = ((bf16[4,2,96,768]{3,2,1,0:T(8,128)(2,1)}), bf16[4,2,96,768]{3,2,1,0:T(8,128)(2,1)S(1)}, u32[]{:S(2)}, u32[]{:S(2)}) async-start(bf16[4,2,96,768]{3,2,1,0:T(8,128)(2,1)} %broadcast_in_dim.8), calls=%async_computation.1 | async-start | bytes 2359296 | tf_op jit(solution)/shard_map/all_to_all | solution.py:255
  79.1 19.3 %copy-start.3 = (s32[19]{0:T(128)S(1)}, s32[19]{0:T(128)}, u32[]{:S(2)}) copy-start(s32[19]{0:T(128)} %pad_add_fusion.refs_0_) | copy-start | bytes 232
  79.1 17.4 %collective-permute-start.4 = (bf16[4,96,768]{2,1,0:T(8,128)(2,1)S(1)}, bf16[4,96,768]{2,1,0:T(8,128)(2,1)S(1)}, u32[]{:S(2)}, u32[]{:S(2)}) collective-permute-start(bf16[4,96,768]{2,1,0:T(8,128)(2,1)S(1)} %get-tuple-element.22.refs_3_), channel_id=1, source_target_pairs={{0,16},{16,32},{32,48},{48,128},{128,144},{144,160},{160,176},{176... | collective-permute-start | bytes 1769480 | tf_op jit(solution)/shard_map/ppermute | solution.py:316
  81.1 17.4 %collective-permute-start.5 = (bf16[4,96,768]{2,1,0:T(8,128)(2,1)S(1)}, bf16[4,96,768]{2,1,0:T(8,128)(2,1)}, u32[]{:S(2)}, u32[]{:S(2)}) collective-permute-start(bf16[4,96,768]{2,1,0:T(8,128)(2,1)S(1)} %get-tuple-element.22.refs_3_), channel_id=1, source_target_pairs={{0,432},{16,0},{32,16},{48,32},{128,48},{144,128},{160,144},{176,1... | collective-permute-start | bytes 1769480 | tf_op jit(solution)/shard_map/ppermute | solution.py:316
  98.4 1.9 copy-start
  100.4 1.4 copy-start.1
  108.2 25.8 %collective-permute-start.8 = (bf16[528,768]{1,0:T(8,128)(2,1)S(1)}, bf16[528,768]{1,0:T(8,128)(2,1)S(1)}, u32[]{:S(2)}, u32[]{:S(2)}) collective-permute-start(bf16[528,768]{1,0:T(8,128)(2,1)S(1)} %get-tuple-element.17.refs_1_), channel_id=1, source_target_pairs={{0,64},{64,0},{1,65},{65,1},{2,66},{66,2},{3,67},{67,3},{4,68},{68... | collective-permute-start | bytes 2433032 | tf_op jit(solution)/shard_map/ppermute | solution.py:339
  112.3 16.8 %collective-permute-start.10 = (bf16[4,96,768]{2,1,0:T(8,128)(2,1)S(1)}, bf16[4,96,768]{2,1,0:T(8,128)(2,1)S(1)}, u32[]{:S(2)}, u32[]{:S(2)}) collective-permute-start(bf16[4,96,768]{2,1,0:T(8,128)(2,1)S(1)} %get-tuple-element.21.refs_4_), channel_id=1, source_target_pairs={{0,432},{16,0},{32,16},{48,32},{128,48},{144,128},{160,144},{176,1... | collective-permute-start | bytes 1769480 | tf_op jit(solution)/shard_map/ppermute | solution.py:316
  116.2 17.7 %collective-permute-start.9 = (bf16[4,96,768]{2,1,0:T(8,128)(2,1)S(1)}, bf16[4,96,768]{2,1,0:T(8,128)(2,1)S(1)}, u32[]{:S(2)}, u32[]{:S(2)}) collective-permute-start(bf16[4,96,768]{2,1,0:T(8,128)(2,1)S(1)} %get-tuple-element.21.refs_4_), channel_id=1, source_target_pairs={{0,16},{16,32},{32,48},{48,128},{128,144},{144,160},{160,176},{176... | collective-permute-start | bytes 1769480 | tf_op jit(solution)/shard_map/ppermute | solution.py:316
  142.7 5.6 %copy-start.2 = (f32[8,1536]{1,0:T(8,128)S(1)}, f32[8,1536]{1,0:T(8,128)}, u32[]{:S(2)}) copy-start(f32[8,1536]{1,0:T(8,128)} %get-tuple-element.32.refs_3_.refs_2_) | copy-start | bytes 147460
  142.7 2.2 collective-permute-start.12
  143.5 1.3 collective-permute-start.11
  144.2 0.7 collective-permute-start.13
  155.4 2.1 collective-permute-start.15
  156.1 1.3 collective-permute-start.14
  156.8 0.7 collective-permute-start.16
  164.4 29.6 %collective-permute-start.18 = (bf16[16,768]{1,0:T(8,128)(2,1)S(1)}, bf16[16,768]{1,0:T(8,128)(2,1)S(1)}, u32[]{:S(2)}, u32[]{:S(2)}) collective-permute-start(bf16[16,768]{1,0:T(8,128)(2,1)S(1)} %shard_map.68), channel_id=1, source_target_pairs={{2,3},{6,7},{10,11},{14,15},{18,19},{22,23},{26,27},{30,31},{34,35... | collective-permute-start | bytes 73736 | tf_op jit(solution)/shard_map/ppermute | solution.py:289
  165.7 26.2 %collective-permute-start.17 = (bf16[12,768]{1,0:T(8,128)(2,1)S(1)}, bf16[12,768]{1,0:T(8,128)(2,1)S(1)}, u32[]{:S(2)}, u32[]{:S(2)}) collective-permute-start(bf16[12,768]{1,0:T(8,128)(2,1)S(1)} %get-tuple-element.35), channel_id=1, source_target_pairs={{2,131},{130,7},{6,135},{134,11},{10,139},{138,15},{14,143},{142,1... | collective-permute-start | bytes 55304 | tf_op jit(solution)/shard_map/ppermute | solution.py:287
  167.0 27.0 %collective-permute-start.19 = (bf16[12,768]{1,0:T(8,128)(2,1)S(1)}, bf16[12,768]{1,0:T(8,128)(2,1)S(1)}, u32[]{:S(2)}, u32[]{:S(2)}) collective-permute-start(bf16[12,768]{1,0:T(8,128)(2,1)S(1)} %get-tuple-element.36), channel_id=1, source_target_pairs={{130,3},{6,131},{134,7},{10,135},{138,11},{14,139},{142,15},{18,14... | collective-permute-start | bytes 55304 | tf_op jit(solution)/shard_map/ppermute | solution.py:288
  201.2 14.2 %collective-permute-start.20 = (bf16[2,768]{1,0:T(2,128)(2,1)S(1)}, bf16[2,768]{1,0:T(2,128)(2,1)S(1)}, u32[]{:S(2)}, u32[]{:S(2)}) collective-permute-start(bf16[2,768]{1,0:T(2,128)(2,1)S(1)} %get-tuple-element.52), channel_id=1, source_target_pairs={{3,0},{67,256},{131,2},{195,258},{259,64},{323,320},{387,66},{451,... | collective-permute-start | bytes 9224 | tf_op jit(solution)/shard_map/ppermute | solution.py:360
  202.5 12.9 %collective-permute-start.21 = (bf16[2,768]{1,0:T(2,128)(2,1)S(1)}, bf16[2,768]{1,0:T(2,128)(2,1)S(1)}, u32[]{:S(2)}, u32[]{:S(2)}) collective-permute-start(bf16[2,768]{1,0:T(2,128)(2,1)S(1)} %get-tuple-element.53), channel_id=1, source_target_pairs={{3,1},{67,257},{131,3},{195,259},{259,65},{323,321},{387,67},{451,... | collective-permute-start | bytes 9224 | tf_op jit(solution)/shard_map/ppermute | solution.py:360
  206.8 8.6 %collective-permute-start.22 = (bf16[2,768]{1,0:T(2,128)(2,1)S(1)}, bf16[2,768]{1,0:T(2,128)(2,1)S(1)}, u32[]{:S(2)}, u32[]{:S(2)}) collective-permute-start(bf16[2,768]{1,0:T(2,128)(2,1)S(1)} %get-tuple-element.52), channel_id=1, source_target_pairs={{3,128},{67,384},{131,130},{195,386},{259,192},{323,448},{387,194}... | collective-permute-start | bytes 9224 | tf_op jit(solution)/shard_map/ppermute | solution.py:360
  208.1 13.6 %collective-permute-start.23 = (bf16[2,768]{1,0:T(2,128)(2,1)S(1)}, bf16[2,768]{1,0:T(2,128)(2,1)S(1)}, u32[]{:S(2)}, u32[]{:S(2)}) collective-permute-start(bf16[2,768]{1,0:T(2,128)(2,1)S(1)} %get-tuple-element.53), channel_id=1, source_target_pairs={{3,129},{67,385},{131,131},{195,387},{259,193},{323,449},{387,195}... | collective-permute-start | bytes 9224 | tf_op jit(solution)/shard_map/ppermute | solution.py:360

commit v7 on v6

--- a/solution.py
+++ b/solution.py
@@ -127,33 +127,39 @@
     spread(par_ref, a_scr, d_ref, rows)
 
 
-def second_half(rows, meta_ref, x_ref, d_ref, *refs):
-    *pieces, out_ref, w_ref, y_scr, sems = refs
+def second_half(rows, meta_ref, x_hbm, d_hbm, *refs):
+    *pieces, out_ref, w_ref, x_scr, d_scr, y_scr, sems, row_sems = refs
     copies = weight_copies(0, meta_ref, pieces, w_ref, sems)
+    copies.append(pltpu.make_async_copy(d_hbm, d_scr, row_sems.at[0]))
+    copies.append(pltpu.make_async_copy(x_hbm, x_scr, row_sems.at[1]))
     for copy in copies:
         copy.start()
     for copy in copies:
         copy.wait()
 
     def residual(start, chunk):
-        return x_ref[start : start + chunk].astype(jnp.float32)
-
-    mix_and_pool(d_ref, w_ref, residual, y_scr, out_ref, rows)
-
-
-def swapped_level(rows, edge, meta_ref, own_ref, other_ref, par_ref, *refs):
-    *pieces, out_ref, w_ref, a_scr, d_scr, y_scr, sems = refs
-    copies = weight_copies(1, meta_ref, pieces, w_ref, sems)
+        return x_scr[start : start + chunk].astype(jnp.float32)
+
+    mix_and_pool(d_scr, w_ref, residual, y_scr, out_ref, rows)
+
+
+def assemble(slot, meta_ref, *refs):
+    *pieces, w_ref, sems = refs
+    copies = weight_copies(slot, meta_ref, pieces, w_ref, sems)
     for copy in copies:
         copy.start()
-
+    for copy in copies:
+        copy.wait()
+
+
+def swapped_level(
+    rows, edge, meta_ref, own_ref, other_ref, par_ref, w_ref, out_ref, a_scr, d_scr, y_scr
+):
     def load(start):
         return [ref[pl.ds(start, 16)].astype(jnp.float32) for ref in (own_ref, other_ref)]
 
     activate(load, par_ref, a_scr, rows, edge, meta_ref)
     spread(par_ref, a_scr, d_scr, rows)
-    for copy in copies:
-        copy.wait()
 
     def residual(start, chunk):
         return own_ref[start : start + chunk].astype(jnp.float32)
@@ -192,6 +198,7 @@
         "x": pltpu.VMEM((size, HALF), jnp.bfloat16),
         "y": pltpu.VMEM((TILES, size, 128), jnp.float32),
         "s": pltpu.SemaphoreType.DMA((16,)),
+        "r": pltpu.SemaphoreType.DMA((2,)),
     }
     return [shapes[name] for name in names]
 
@@ -215,24 +222,36 @@
 def run_second_half(rows, meta, x, d, pieces):
     return pl.pallas_call(
         lambda *refs: second_half(rows, *refs),
-        in_specs=[spec(pltpu.SMEM), spec(), spec()] + [spec(pl.ANY)] * len(pieces),
+        in_specs=[spec(pltpu.SMEM), spec(pltpu.HBM), spec(pltpu.HBM)] + [spec(pl.ANY)] * len(pieces),
         out_specs=[spec(), spec()],
         out_shape=[half_rows(out_rows(rows, False)), half_rows(C)],
-        scratch_shapes=scratch(rows, "ys"),
+        scratch_shapes=scratch(rows, "xdysr"),
         compiler_params=GRANT,
         name="mix_first",
-    )(meta, x, d, *pieces)
-
-
-def run_swapped_level(rows, edge, meta, own, other, par, pieces):
+    )(meta, *(pltpu.with_memory_space_constraint(part, pltpu.HBM) for part in (x, d)), *pieces)
+
+
+def run_assemble(slot, meta, pieces):
+    return pl.pallas_call(
+        lambda *refs: assemble(slot, *refs),
+        in_specs=[spec(pltpu.SMEM)] + [spec(pl.ANY)] * len(pieces),
+        out_specs=spec(),
+        out_shape=half_rows(C),
+        scratch_shapes=scratch(16, "s"),
+        compiler_params=GRANT,
+        name="assemble",
+    )(meta, *pieces)
+
+
+def run_swapped_level(rows, edge, meta, own, other, par, weights):
     return pl.pallas_call(
         lambda *refs: swapped_level(rows, edge, *refs),
-        in_specs=[spec(pltpu.SMEM)] + [spec()] * 3 + [spec(pl.ANY)] * len(pieces),
-        out_specs=[spec(), spec()],
-        out_shape=[half_rows(out_rows(rows, True)), half_rows(C)],
-        scratch_shapes=scratch(rows, "adys"),
+        in_specs=[spec(pltpu.SMEM)] + [spec()] * 4,
+        out_specs=spec(),
+        out_shape=half_rows(out_rows(rows, True)),
+        scratch_shapes=scratch(rows, "ady"),
         compiler_params=GRANT,
-    )(meta, own, other, par, *pieces)
+    )(meta, own, other, par, weights)
 
 
 def run_level(rows, edge, last, meta, x, par, weights):
@@ -337,9 +356,8 @@
     level_rows, taps = run_first_half(rows, meta, hot, stem, params[0])
     now, even_weights = run_second_half(rows, meta, level_rows, taps, pieces[0])
     other = lax.ppermute(now, "co", [(0, 1), (1, 0)])
-    now, odd_weights = run_swapped_level(
-        RUN // 2 + 8, 4, meta, now, other, params[1], pieces[1]
-    )
+    odd_weights = run_assemble(1, meta, pieces[1])
+    now = run_swapped_level(RUN // 2 + 8, 4, meta, now, other, params[1], odd_weights)
     run = RUN // 4
     for role in range(3):
         now = lax.all_gather(pass_on(now, role), "co")

time: 225 us -> 220 us (0.978)
  the two profiles are of different devices: /device:TPU:135 before, /device:TPU:35 now
where the time goes in v7:
time: 220 us
  waiting for transfers between devices  72.3 us (33%)
  starting transfers between devices  54.2 us (25%)
  blocking collectives  43.7 us (20%)
  Pallas kernels  38.2 us (17%)
  local copies, waits for them, and re-layouts  6.12 us (3%)
  other arithmetic  4.17 us (2%)
    all_gather x1, blocking collectives, relay(): held = lax.all_gather(jnp.concatenate(held, axis=0), 'zh')  25.4 us
    ppermute x4, waiting for transfers between devices, relay(): kept = kept + lax.ppermute(now[2 * p:2 * p + 2], ('zh', 'co', 'x'), pairs)  22.2 us
    ppermute x4, waiting for transfers between devices, relay(): sides.append(lax.ppermute(near[slot], ('zh', 'zl'), ring(16, by)))  16 us
    all_to_all x1, starting transfers between devices, relay(): blocks = lax.all_to_all(blocks, ('co', 'y', 'x'), 0, 0, tiled=True)  12.8 us
    all_to_all x1, waiting for transfers between devices, relay(): blocks = lax.all_to_all(blocks, ('co', 'y', 'x'), 0, 0, tiled=True)  12.4 us
    ppermute x4, starting transfers between devices, relay(): sides.append(lax.ppermute(near[slot], ('zh', 'zl'), ring(16, by)))  10.6 us
    pallas_call x6, Pallas kernels, run_level(): pl.pallas_call(lambda *refs: paired_level(rows, edge, *refs), in_specs=[s...  10.4 us
    pallas_call x1, Pallas kernels, run_first_half(): pl.pallas_call(lambda *refs: first_half(rows, *refs), in_specs=[spec(pltp...  10 us
  transfers between devices with their start and end apart: 26, of which 11 were waited for; matrix products, arithmetic and copies ran while one was open for 3% of the time, Pallas kernels for 6%

profile of v7, /device:TPU:35, one launch (start us, length us, event | category | flops | bytes accessed | tf_op | source)
XLA Modules:
  0.0 219.6 jit_solution(1263481804611552316)
XLA Ops:
  0.1 1.0 maximum_maximum_fusion
  1.1 25.4 %all-gather = bf16[128,1536]{1,0:T(8,128)(2,1)S(1)} all-gather(bf16[32,1536]{1,0:T(8,128)(2,1)S(1)} %maximum_maximum_fusion), channel_id=2, replica_groups=mesh['zh'=4,'co'=2,'zl'=4,'y'=4,'x'=4] {'zh'}, dimensions={0}, use_global_device_ids=true | all-gather | bytes 491520 | tf_op jit(solution)/shard_map/all_gather | solution.py:320
  26.5 0.7 dynamic-slice_add_fusion
  27.2 0.6 collective-permute-start
  27.8 0.7 collective-permute-start.1
  28.5 2.8 %collective-permute-start.2 = (s32[512]{0:T(512)S(1)}, s32[512]{0:T(512)S(1)}, u32[]{:S(2)}, u32[]{:S(2)}) collective-permute-start(s32[512]{0:T(512)S(1)} %bitcast.54), channel_id=1, source_target_pairs={{1,0},{5,4},{9,8},{13,12},{17,16},{21,20},{25,24},{29,28},{33,32},... | collective-permute-start | bytes 6152 | tf_op jit(solution)/shard_map/ppermute | solution.py:297
  31.3 0.7 collective-permute-start.3
  32.1 1.1 broadcast_in_dim.7
  33.2 12.8 %all-to-all-start = ((bf16[32,24,768]{2,1,0:T(8,128)(2,1)}), bf16[32,24,768]{2,1,0:T(8,128)(2,1)S(1)}, u32[]{:S(2)}, u32[]{:S(2)}) async-start(bf16[32,24,768]{2,1,0:T(8,128)(2,1)} %bitcast.10), calls=%async_computation | async-start | bytes 2359296 | tf_op jit(solution)/shard_map/all_to_all | solution.py:326
  46.3 1.9 all_gather.54
  48.2 0.7 maximum_select_fusion.refs_2_
  49.0 0.6 slice_bitcast_fusion.2
  50.4 12.4 %all-to-all-done = bf16[32,24,768]{2,1,0:T(8,128)(2,1)S(1)} async-done(((bf16[32,24,768]{2,1,0:T(8,128)(2,1)}), bf16[32,24,768]{2,1,0:T(8,128)(2,1)S(1)}, u32[]{:S(2)}, u32[]{:S(2)}) %all-to-all-start) | async-done | bytes 1179680 | tf_op jit(solution)/shard_map/all_to_all | solution.py:326
  62.8 3.7 %collective-permute-start.7 = (bf16[96,768]{1,0:T(8,128)(2,1)S(1)}, bf16[96,768]{1,0:T(8,128)(2,1)S(1)}, u32[]{:S(2)}, u32[]{:S(2)}) collective-permute-start(bf16[96,768]{1,0:T(8,128)(2,1)S(1)} %get-tuple-element.20), channel_id=1, source_target_pairs={{0,416},{16,432},{32,0},{48,16},{128,32},{144,48},{160,128},{176,1... | collective-permute-start | bytes 442376 | tf_op jit(solution)/shard_map/ppermute | solution.py:330
  66.5 2.5 %collective-permute-start.6 = (bf16[96,768]{1,0:T(8,128)(2,1)S(1)}, bf16[96,768]{1,0:T(8,128)(2,1)S(1)}, u32[]{:S(2)}, u32[]{:S(2)}) collective-permute-start(bf16[96,768]{1,0:T(8,128)(2,1)S(1)} %get-tuple-element.19), channel_id=1, source_target_pairs={{0,32},{16,48},{32,128},{48,144},{128,160},{144,176},{160,256},{17... | collective-permute-start | bytes 442376 | tf_op jit(solution)/shard_map/ppermute | solution.py:329
  69.8 1.7 collective-permute-done.7
  71.5 7.8 %collective-permute-done.6 = bf16[96,768]{1,0:T(8,128)(2,1)S(1)} collective-permute-done((bf16[96,768]{1,0:T(8,128)(2,1)S(1)}, bf16[96,768]{1,0:T(8,128)(2,1)S(1)}, u32[]{:S(2)}, u32[]{:S(2)}) %collective-permute-start.6) | collective-permute-done | bytes 147488 | tf_op jit(solution)/shard_map/ppermute | solution.py:329
  79.4 1.1 broadcast_in_dim.8
  80.5 3.5 %all-to-all-start.1 = ((bf16[4,2,96,768]{3,2,1,0:T(8,128)(2,1)}), bf16[4,2,96,768]{3,2,1,0:T(8,128)(2,1)S(1)}, u32[]{:S(2)}, u32[]{:S(2)}) async-start(bf16[4,2,96,768]{3,2,1,0:T(8,128)(2,1)} %broadcast_in_dim.8), calls=%async_computation.1 | async-start | bytes 2359296 | tf_op jit(solution)/shard_map/all_to_all | solution.py:274
  84.1 1.3 slice_bitcast_fusion
  85.4 1.9 collective-permute-start.4
  87.3 3.4 %collective-permute-start.5 = (bf16[4,96,768]{2,1,0:T(8,128)(2,1)S(1)}, bf16[4,96,768]{2,1,0:T(8,128)(2,1)}, u32[]{:S(2)}, u32[]{:S(2)}) collective-permute-start(bf16[4,96,768]{2,1,0:T(8,128)(2,1)S(1)} %get-tuple-element.18.refs_3_), channel_id=1, source_target_pairs={{0,432},{16,0},{32,16},{48,32},{128,48},{144,128},{160,144},{176,1... | collective-permute-start | bytes 1769480 | tf_op jit(solution)/shard_map/ppermute | solution.py:335
  90.8 0.8 fusion.refs_1_
  91.5 10.0 %stem_and_taps.1 = (bf16[1056,768]{1,0:T(8,128)(2,1)}, bf16[1056,1536]{1,0:T(8,128)(2,1)}) custom-call(s32[19]{0:T(128)} %pad_add_fusion.refs_0_, bf16[1056,64]{1,0:T(8,128)(2,1)} %fusion.refs_1_, bf16[64,1536]{1,0:T(8,128)(2,1)} %maximum_select_fusion.refs_2_, f32[8,1536]{1,0:T(8,128)} %get-tuple-element.28.refs_3_.refs_2_), custom_call_target="tpu_custom_call" | custom-call | tf_op jit(solution)/shard_map/stem_and_taps/pallas_call | solution.py:212
  101.8 1.9 collective-permute-done.5.refs_5_
  103.7 8.6 %mix_first.1 = (bf16[528,768]{1,0:T(8,128)(2,1)S(1)}, bf16[1536,768]{1,0:T(8,128)(2,1)S(1)}) custom-call(s32[19]{0:T(128)S(1)} %copy-done.1, bf16[1056,768]{1,0:T(8,128)(2,1)} %get-tuple-element.13.refs_1_, bf16[1056,1536]{1,0:T(8,128)(2,1)} %get-tuple-element.14.refs_2_, bf16[4,96,768]{2,1,0:T(8,128)(2,1)S(1)} %get-tuple-element.18.refs_3_, ...), custom_call_target="tpu_custom_call" | custom-call | tf_op jit(solution)/shard_map/mix_first/pallas_call | solution.py:223
  112.4 3.3 %collective-permute-start.8 = (bf16[528,768]{1,0:T(8,128)(2,1)S(1)}, bf16[528,768]{1,0:T(8,128)(2,1)S(1)}, u32[]{:S(2)}, u32[]{:S(2)}) collective-permute-start(bf16[528,768]{1,0:T(8,128)(2,1)S(1)} %get-tuple-element.15.refs_1_), channel_id=1, source_target_pairs={{0,64},{64,0},{1,65},{65,1},{2,66},{66,2},{3,67},{67,3},{4,68},{68... | collective-permute-start | bytes 2433032 | tf_op jit(solution)/shard_map/ppermute | solution.py:358
  115.6 1.9 collective-permute-start.9
  117.6 3.4 %collective-permute-start.10 = (bf16[4,96,768]{2,1,0:T(8,128)(2,1)S(1)}, bf16[4,96,768]{2,1,0:T(8,128)(2,1)S(1)}, u32[]{:S(2)}, u32[]{:S(2)}) collective-permute-start(bf16[4,96,768]{2,1,0:T(8,128)(2,1)S(1)} %get-tuple-element.17.refs_1_), channel_id=1, source_target_pairs={{0,432},{16,0},{32,16},{48,32},{128,48},{144,128},{160,144},{176,1... | collective-permute-start | bytes 1769480 | tf_op jit(solution)/shard_map/ppermute | solution.py:335
  120.9 11.5 %collective-permute-done.9.refs_2_ = bf16[4,96,768]{2,1,0:T(8,128)(2,1)S(1)} collective-permute-done((bf16[4,96,768]{2,1,0:T(8,128)(2,1)S(1)}, bf16[4,96,768]{2,1,0:T(8,128)(2,1)S(1)}, u32[]{:S(2)}, u32[]{:S(2)}) %collective-permute-start.9) | collective-permute-done | bytes 589856 | tf_op jit(solution)/shard_map/ppermute | solution.py:335
  132.4 2.4 %collective-permute-done.10.refs_3_ = bf16[4,96,768]{2,1,0:T(8,128)(2,1)S(1)} collective-permute-done((bf16[4,96,768]{2,1,0:T(8,128)(2,1)S(1)}, bf16[4,96,768]{2,1,0:T(8,128)(2,1)S(1)}, u32[]{:S(2)}, u32[]{:S(2)}) %collective-permute-start.10) | collective-permute-done | bytes 589856 | tf_op jit(solution)/shard_map/ppermute | solution.py:335
  134.8 4.3 %assemble.1.refs_4_.refs_3_ = bf16[1536,768]{1,0:T(8,128)(2,1)S(1)} custom-call(s32[19]{0:T(128)S(1)} %copy-done.1, bf16[4,96,768]{2,1,0:T(8,128)(2,1)S(1)} %get-tuple-element.17.refs_1_, bf16[4,96,768]{2,1,0:T(8,128)(2,1)S(1)} %collective-permute-done.9.refs_2_, bf16[4,96,768]{2,1,0:T(8,128)(2,1)S(1)} %collective-permute-done.10.refs_3_, ...), custom_call_target="tpu_custom_call" | custom-call | tf_op jit(solution)/shard_map/assemble/pallas_call | solution.py:235
  139.0 5.0 %shard_map.64 = bf16[256,768]{1,0:T(8,128)(2,1)S(1)} custom-call(s32[19]{0:T(128)S(1)} %copy-done.1, bf16[528,768]{1,0:T(8,128)(2,1)S(1)} %get-tuple-element.15.refs_1_, bf16[528,768]{1,0:T(8,128)(2,1)S(1)} %collective-permute-done.8.refs_2_, f32[8,1536]{1,0:T(8,128)S(1)} %get-tuple-element.27.refs_3_.refs_2_, bf16[1536,768]{1,0:T(8,128)(2,1)S(1)} %assemble.1.refs_4_.refs_3_), custom_call_target="tpu_custom_call" | custom-call | tf_op jit(solution)/shard_map/pallas_call | solution.py:247
  144.0 1.4 collective-permute-start.12
  145.5 1.3 collective-permute-start.13
  146.8 1.3 collective-permute-start.11
  148.1 6.9 %collective-permute-done.13 = bf16[12,768]{1,0:T(8,128)(2,1)S(1)} collective-permute-done((bf16[12,768]{1,0:T(8,128)(2,1)S(1)}, bf16[12,768]{1,0:T(8,128)(2,1)S(1)}, u32[]{:S(2)}, u32[]{:S(2)}) %collective-permute-start.13) | collective-permute-done | bytes 18464 | tf_op jit(solution)/shard_map/ppermute | solution.py:307
  155.0 4.3 %collective-permute-done.11 = bf16[12,768]{1,0:T(8,128)(2,1)S(1)} collective-permute-done((bf16[12,768]{1,0:T(8,128)(2,1)S(1)}, bf16[12,768]{1,0:T(8,128)(2,1)S(1)}, u32[]{:S(2)}, u32[]{:S(2)}) %collective-permute-start.11) | collective-permute-done | bytes 18464 | tf_op jit(solution)/shard_map/ppermute | solution.py:306
  159.4 4.2 %all-gather.1 = bf16[576,768]{1,0:T(8,128)(2,1)S(1)} all-gather(bf16[288,768]{1,0:T(8,128)(2,1)S(1)} %pad_maximum_fusion), channel_id=3, replica_groups=mesh['zh'=4,'co'=2,'zl'=4,'y'=4,'x'=4] {'co'}, dimensions={0}, use_global_device_ids=true | all-gather | bytes 1327104 | tf_op jit(solution)/shard_map/all_gather | solution.py:363
  163.7 3.3 %shard_map.65 = bf16[144,768]{1,0:T(8,128)(2,1)S(1)} custom-call(s32[19]{0:T(128)S(1)} %copy-done.1, bf16[2,288,768]{2,1,0:T(8,128)(2,1)S(1)} %bitcast.37, f32[8,1536]{1,0:T(8,128)S(1)} %copy-done, bf16[1536,768]{1,0:T(8,128)(2,1)S(1)} %get-tuple-element.16.refs_3_), custom_call_target="tpu_custom_call" | custom-call | tf_op jit(solution)/shard_map/pallas_call | solution.py:258
  166.9 2.1 all-gather.2
  169.1 1.8 shard_map.66
  170.9 1.3 collective-permute-start.15
  172.2 1.3 collective-permute-start.16
  173.5 1.3 collective-permute-start.14
  174.8 0.9 collective-permute-done.14
  175.8 2.6 %all-gather.3 = bf16[192,768]{1,0:T(8,128)(2,1)S(1)} all-gather(bf16[96,768]{1,0:T(8,128)(2,1)S(1)} %pad_maximum_fusion.2), channel_id=5, replica_groups=mesh['zh'=4,'co'=2,'zl'=4,'y'=4,'x'=4] {'co'}, dimensions={0}, use_global_device_ids=true | all-gather | bytes 442368 | tf_op jit(solution)/shard_map/all_gather | solution.py:363
  178.4 1.5 shard_map.67
  179.9 1.9 all-gather.4
  181.8 1.3 shard_map.68
  183.2 0.7 collective-permute-start.18
  183.8 0.7 collective-permute-start.19
  184.5 0.7 collective-permute-start.17
  185.2 1.9 all-gather.5
  187.2 1.3 shard_map.69
  188.5 1.9 all-gather.6
  190.3 1.1 shard_map.70
  191.5 0.7 collective-permute-start.23
  192.2 0.7 collective-permute-start.22
  192.8 0.7 collective-permute-start.20
  193.5 1.3 collective-permute-start.21
  194.8 22.2 %collective-permute-done.21 = bf16[2,768]{1,0:T(2,128)(2,1)S(1)} collective-permute-done((bf16[2,768]{1,0:T(2,128)(2,1)S(1)}, bf16[2,768]{1,0:T(2,128)(2,1)S(1)}, u32[]{:S(2)}, u32[]{:S(2)}) %collective-permute-start.21) | collective-permute-done | bytes 3104 | tf_op jit(solution)/shard_map/ppermute | solution.py:378
  217.0 1.8 all-gather.8
  219.0 0.6 copy.20
  (83 shorter events, 2.6 us)
Async XLA Ops:
  27.2 23.1 %collective-permute-start = (s32[512]{0:T(512)S(1)}, s32[512]{0:T(512)S(1)}, u32[]{:S(2)}, u32[]{:S(2)}) collective-permute-start(s32[512]{0:T(512)S(1)} %bitcast.52), channel_id=1, source_target_pairs={{3,4},{7,8},{11,12},{15,16},{19,20},{23,24},{27,28},{31,32},{35,36... | collective-permute-start | bytes 6152 | tf_op jit(solution)/shard_map/ppermute | solution.py:297
  27.8 22.5 %collective-permute-start.1 = (s32[512]{0:T(512)S(1)}, s32[512]{0:T(512)S(1)}, u32[]{:S(2)}, u32[]{:S(2)}) collective-permute-start(s32[512]{0:T(512)S(1)} %bitcast.53), channel_id=1, source_target_pairs={{0,0},{4,4},{8,8},{12,12},{16,16},{20,20},{24,24},{28,28},{32,32},... | collective-permute-start | bytes 6152 | tf_op jit(solution)/shard_map/ppermute | solution.py:297
  28.5 21.8 %collective-permute-start.2 = (s32[512]{0:T(512)S(1)}, s32[512]{0:T(512)S(1)}, u32[]{:S(2)}, u32[]{:S(2)}) collective-permute-start(s32[512]{0:T(512)S(1)} %bitcast.54), channel_id=1, source_target_pairs={{1,0},{5,4},{9,8},{13,12},{17,16},{21,20},{25,24},{29,28},{33,32},... | collective-permute-start | bytes 6152 | tf_op jit(solution)/shard_map/ppermute | solution.py:297
  31.3 19.1 %collective-permute-start.3 = (s32[512]{0:T(512)S(1)}, s32[512]{0:T(512)S(1)}, u32[]{:S(2)}, u32[]{:S(2)}) collective-permute-start(s32[512]{0:T(512)S(1)} %bitcast.55), channel_id=1, source_target_pairs={{2,0},{6,4},{10,8},{14,12},{18,16},{22,20},{26,24},{30,28},{34,32}... | collective-permute-start | bytes 6152 | tf_op jit(solution)/shard_map/ppermute | solution.py:297
  33.2 12.8 %copy-start.4 = (s32[4]{0:T(128)S(1)}, s32[4]{0:T(128)}, u32[]{:S(2)}) copy-start(s32[4]{0:T(128)} %constant.115) | copy-start | bytes 52
  33.2 13.0 %copy-start.3 = (bf16[15,4,1536]{2,1,0:T(4,128)(2,1)S(1)}, bf16[15,4,1536]{2,1,0:T(4,128)(2,1)}, u32[]{:S(2)}) copy-start(bf16[15,4,1536]{2,1,0:T(4,128)(2,1)} %param.7) | copy-start | bytes 552964
  33.2 29.5 %all-to-all-start = ((bf16[32,24,768]{2,1,0:T(8,128)(2,1)}), bf16[32,24,768]{2,1,0:T(8,128)(2,1)S(1)}, u32[]{:S(2)}, u32[]{:S(2)}) async-start(bf16[32,24,768]{2,1,0:T(8,128)(2,1)} %bitcast.10), calls=%async_computation | async-start | bytes 2359296 | tf_op jit(solution)/shard_map/all_to_all | solution.py:326
  62.8 7.0 %copy-start.2 = (bf16[32,24,768]{2,1,0:T(8,128)(2,1)}, bf16[32,24,768]{2,1,0:T(8,128)(2,1)S(1)}, u32[]{:S(2)}) copy-start(bf16[32,24,768]{2,1,0:T(8,128)(2,1)S(1)} %all-to-all-done) | copy-start | bytes 3538948
  62.8 8.7 %collective-permute-start.7 = (bf16[96,768]{1,0:T(8,128)(2,1)S(1)}, bf16[96,768]{1,0:T(8,128)(2,1)S(1)}, u32[]{:S(2)}, u32[]{:S(2)}) collective-permute-start(bf16[96,768]{1,0:T(8,128)(2,1)S(1)} %get-tuple-element.20), channel_id=1, source_target_pairs={{0,416},{16,432},{32,0},{48,16},{128,32},{144,48},{160,128},{176,1... | collective-permute-start | bytes 442376 | tf_op jit(solution)/shard_map/ppermute | solution.py:330
  66.5 12.9 %collective-permute-start.6 = (bf16[96,768]{1,0:T(8,128)(2,1)S(1)}, bf16[96,768]{1,0:T(8,128)(2,1)S(1)}, u32[]{:S(2)}, u32[]{:S(2)}) collective-permute-start(bf16[96,768]{1,0:T(8,128)(2,1)S(1)} %get-tuple-element.19), channel_id=1, source_target_pairs={{0,32},{16,48},{32,128},{48,144},{128,160},{144,176},{160,256},{17... | collective-permute-start | bytes 442376 | tf_op jit(solution)/shard_map/ppermute | solution.py:329
  80.5 23.2 %all-to-all-start.1 = ((bf16[4,2,96,768]{3,2,1,0:T(8,128)(2,1)}), bf16[4,2,96,768]{3,2,1,0:T(8,128)(2,1)S(1)}, u32[]{:S(2)}, u32[]{:S(2)}) async-start(bf16[4,2,96,768]{3,2,1,0:T(8,128)(2,1)} %broadcast_in_dim.8), calls=%async_computation.1 | async-start | bytes 2359296 | tf_op jit(solution)/shard_map/all_to_all | solution.py:274
  85.4 18.3 %copy-start.1 = (s32[19]{0:T(128)S(1)}, s32[19]{0:T(128)}, u32[]{:S(2)}) copy-start(s32[19]{0:T(128)} %pad_add_fusion.refs_0_) | copy-start | bytes 232
  85.4 16.4 %collective-permute-start.4 = (bf16[4,96,768]{2,1,0:T(8,128)(2,1)S(1)}, bf16[4,96,768]{2,1,0:T(8,128)(2,1)S(1)}, u32[]{:S(2)}, u32[]{:S(2)}) collective-permute-start(bf16[4,96,768]{2,1,0:T(8,128)(2,1)S(1)} %get-tuple-element.18.refs_3_), channel_id=1, source_target_pairs={{0,16},{16,32},{32,48},{48,128},{128,144},{144,160},{160,176},{176... | collective-permute-start | bytes 1769480 | tf_op jit(solution)/shard_map/ppermute | solution.py:335
  87.3 16.4 %collective-permute-start.5 = (bf16[4,96,768]{2,1,0:T(8,128)(2,1)S(1)}, bf16[4,96,768]{2,1,0:T(8,128)(2,1)}, u32[]{:S(2)}, u32[]{:S(2)}) collective-permute-start(bf16[4,96,768]{2,1,0:T(8,128)(2,1)S(1)} %get-tuple-element.18.refs_3_), channel_id=1, source_target_pairs={{0,432},{16,0},{32,16},{48,32},{128,48},{144,128},{160,144},{176,1... | collective-permute-start | bytes 1769480 | tf_op jit(solution)/shard_map/ppermute | solution.py:335
  112.4 26.7 %collective-permute-start.8 = (bf16[528,768]{1,0:T(8,128)(2,1)S(1)}, bf16[528,768]{1,0:T(8,128)(2,1)S(1)}, u32[]{:S(2)}, u32[]{:S(2)}) collective-permute-start(bf16[528,768]{1,0:T(8,128)(2,1)S(1)} %get-tuple-element.15.refs_1_), channel_id=1, source_target_pairs={{0,64},{64,0},{1,65},{65,1},{2,66},{66,2},{3,67},{67,3},{4,68},{68... | collective-permute-start | bytes 2433032 | tf_op jit(solution)/shard_map/ppermute | solution.py:358
  115.6 16.8 %collective-permute-start.9 = (bf16[4,96,768]{2,1,0:T(8,128)(2,1)S(1)}, bf16[4,96,768]{2,1,0:T(8,128)(2,1)S(1)}, u32[]{:S(2)}, u32[]{:S(2)}) collective-permute-start(bf16[4,96,768]{2,1,0:T(8,128)(2,1)S(1)} %get-tuple-element.17.refs_1_), channel_id=1, source_target_pairs={{0,16},{16,32},{32,48},{48,128},{128,144},{144,160},{160,176},{176... | collective-permute-start | bytes 1769480 | tf_op jit(solution)/shard_map/ppermute | solution.py:335
  117.6 17.2 %collective-permute-start.10 = (bf16[4,96,768]{2,1,0:T(8,128)(2,1)S(1)}, bf16[4,96,768]{2,1,0:T(8,128)(2,1)S(1)}, u32[]{:S(2)}, u32[]{:S(2)}) collective-permute-start(bf16[4,96,768]{2,1,0:T(8,128)(2,1)S(1)} %get-tuple-element.17.refs_1_), channel_id=1, source_target_pairs={{0,432},{16,0},{32,16},{48,32},{128,48},{144,128},{160,144},{176,1... | collective-permute-start | bytes 1769480 | tf_op jit(solution)/shard_map/ppermute | solution.py:335
  144.0 19.6 %copy-start = (f32[8,1536]{1,0:T(8,128)S(1)}, f32[8,1536]{1,0:T(8,128)}, u32[]{:S(2)}) copy-start(f32[8,1536]{1,0:T(8,128)} %get-tuple-element.28.refs_3_.refs_2_) | copy-start | bytes 147460
  144.0 15.3 %collective-permute-start.12 = (bf16[256,768]{1,0:T(8,128)(2,1)S(1)}, bf16[256,768]{1,0:T(8,128)(2,1)S(1)}, u32[]{:S(2)}, u32[]{:S(2)}) collective-permute-start(bf16[256,768]{1,0:T(8,128)(2,1)S(1)} %shard_map.64), channel_id=1, source_target_pairs={{0,1},{4,5},{8,9},{12,13},{16,17},{20,21},{24,25},{28,29},{32,33},... | collective-permute-start | bytes 1179656 | tf_op jit(solution)/shard_map/ppermute | solution.py:308
  145.5 9.5 %collective-permute-start.13 = (bf16[12,768]{1,0:T(8,128)(2,1)S(1)}, bf16[12,768]{1,0:T(8,128)(2,1)S(1)}, u32[]{:S(2)}, u32[]{:S(2)}) collective-permute-start(bf16[12,768]{1,0:T(8,128)(2,1)S(1)} %get-tuple-element.22), channel_id=1, source_target_pairs={{128,1},{4,129},{132,5},{8,133},{136,9},{12,137},{140,13},{16,141}... | collective-permute-start | bytes 55304 | tf_op jit(solution)/shard_map/ppermute | solution.py:307
  146.8 12.5 %collective-permute-start.11 = (bf16[12,768]{1,0:T(8,128)(2,1)S(1)}, bf16[12,768]{1,0:T(8,128)(2,1)S(1)}, u32[]{:S(2)}, u32[]{:S(2)}) collective-permute-start(bf16[12,768]{1,0:T(8,128)(2,1)S(1)} %get-tuple-element.21), channel_id=1, source_target_pairs={{0,129},{128,5},{4,133},{132,9},{8,137},{136,13},{12,141},{140,17}... | collective-permute-start | bytes 55304 | tf_op jit(solution)/shard_map/ppermute | solution.py:306
  170.9 4.8 %collective-permute-start.15 = (bf16[64,768]{1,0:T(8,128)(2,1)S(1)}, bf16[64,768]{1,0:T(8,128)(2,1)S(1)}, u32[]{:S(2)}, u32[]{:S(2)}) collective-permute-start(bf16[64,768]{1,0:T(8,128)(2,1)S(1)} %shard_map.66), channel_id=1, source_target_pairs={{1,2},{5,6},{9,10},{13,14},{17,18},{21,22},{25,26},{29,30},{33,34}... | collective-permute-start | bytes 294920 | tf_op jit(solution)/shard_map/ppermute | solution.py:308
  172.2 2.6 %collective-permute-start.16 = (bf16[12,768]{1,0:T(8,128)(2,1)S(1)}, bf16[12,768]{1,0:T(8,128)(2,1)S(1)}, u32[]{:S(2)}, u32[]{:S(2)}) collective-permute-start(bf16[12,768]{1,0:T(8,128)(2,1)S(1)} %get-tuple-element.26), channel_id=1, source_target_pairs={{129,2},{5,130},{133,6},{9,134},{137,10},{13,138},{141,14},{17,142... | collective-permute-start | bytes 55304 | tf_op jit(solution)/shard_map/ppermute | solution.py:307
  173.5 2.2 %collective-permute-start.14 = (bf16[12,768]{1,0:T(8,128)(2,1)S(1)}, bf16[12,768]{1,0:T(8,128)(2,1)S(1)}, u32[]{:S(2)}, u32[]{:S(2)}) collective-permute-start(bf16[12,768]{1,0:T(8,128)(2,1)S(1)} %get-tuple-element.25), channel_id=1, source_target_pairs={{1,130},{129,6},{5,134},{133,10},{9,138},{137,14},{13,142},{141,18... | collective-permute-start | bytes 55304 | tf_op jit(solution)/shard_map/ppermute | solution.py:306
  183.2 2.1 collective-permute-start.18
  183.8 1.3 collective-permute-start.19
  184.5 0.7 collective-permute-start.17
  191.5 3.3 %collective-permute-start.23 = (bf16[2,768]{1,0:T(2,128)(2,1)S(1)}, bf16[2,768]{1,0:T(2,128)(2,1)S(1)}, u32[]{:S(2)}, u32[]{:S(2)}) collective-permute-start(bf16[2,768]{1,0:T(2,128)(2,1)S(1)} %get-tuple-element.49), channel_id=1, source_target_pairs={{3,129},{67,385},{131,131},{195,387},{259,193},{323,449},{387,195}... | collective-permute-start | bytes 9224 | tf_op jit(solution)/shard_map/ppermute | solution.py:378
  192.2 2.7 %collective-permute-start.22 = (bf16[2,768]{1,0:T(2,128)(2,1)S(1)}, bf16[2,768]{1,0:T(2,128)(2,1)S(1)}, u32[]{:S(2)}, u32[]{:S(2)}) collective-permute-start(bf16[2,768]{1,0:T(2,128)(2,1)S(1)} %get-tuple-element.48), channel_id=1, source_target_pairs={{3,128},{67,384},{131,130},{195,386},{259,192},{323,448},{387,194}... | collective-permute-start | bytes 9224 | tf_op jit(solution)/shard_map/ppermute | solution.py:378
  192.8 2.0 collective-permute-start.20
  193.5 23.5 %collective-permute-start.21 = (bf16[2,768]{1,0:T(2,128)(2,1)S(1)}, bf16[2,768]{1,0:T(2,128)(2,1)S(1)}, u32[]{:S(2)}, u32[]{:S(2)}) collective-permute-start(bf16[2,768]{1,0:T(2,128)(2,1)S(1)} %get-tuple-element.49), channel_id=1, source_target_pairs={{3,1},{67,257},{131,3},{195,259},{259,65},{323,321},{387,67},{451,... | collective-permute-start | bytes 9224 | tf_op jit(solution)/shard_map/ppermute | solution.py:378

commit v8 on v7

--- a/solution.py
+++ b/solution.py
@@ -77,12 +77,12 @@
         lax.fori_loop(0, up16(rows) // chunk, step, 0)
 
 
-def weight_copies(slot, meta_ref, pieces, w_ref, sems):
+def weight_copies(slot, meta_ref, pieces, w_ref, sems, before=0):
     copies = []
     for piece in pieces:
         for k in range(4):
             n = len(copies)
-            row = pl.multiple_of(meta_ref[3 + n] * BLOCK, 16)
+            row = pl.multiple_of(meta_ref[3 + before + n] * BLOCK, 16)
             source = piece.at[k, slot] if len(piece.shape) == 4 else piece.at[k]
             copies.append(
                 pltpu.make_async_copy(source, w_ref.at[pl.ds(row, BLOCK)], sems.at[n])
@@ -93,7 +93,7 @@
 def mix_and_pool(d_ref, w_ref, residual, y_scr, out_ref, rows):
     count = (rows - 8) // 2
     total = up16(rows)
-    chunk = even_chunk(rows, 272)
+    chunk = even_chunk(rows, 528)
     for start in range(0, total, chunk):
         product = jnp.dot(
             d_ref[start : start + chunk], w_ref[...], preferred_element_type=jnp.float32
@@ -128,8 +128,8 @@
 
 
 def second_half(rows, meta_ref, x_hbm, d_hbm, *refs):
-    *pieces, out_ref, w_ref, x_scr, d_scr, y_scr, sems, row_sems = refs
-    copies = weight_copies(0, meta_ref, pieces, w_ref, sems)
+    _, piece, out_ref, w_ref, x_scr, d_scr, y_scr, sems, row_sems = refs
+    copies = weight_copies(0, meta_ref, [piece], w_ref, sems, 12)
     copies.append(pltpu.make_async_copy(d_hbm, d_scr, row_sems.at[0]))
     copies.append(pltpu.make_async_copy(x_hbm, x_scr, row_sems.at[1]))
     for copy in copies:
@@ -219,16 +219,17 @@
     )(meta, hot, stem, par)
 
 
-def run_second_half(rows, meta, x, d, pieces):
+def run_second_half(rows, meta, x, d, begun, piece):
     return pl.pallas_call(
         lambda *refs: second_half(rows, *refs),
-        in_specs=[spec(pltpu.SMEM), spec(pltpu.HBM), spec(pltpu.HBM)] + [spec(pl.ANY)] * len(pieces),
+        in_specs=[spec(pltpu.SMEM), spec(pltpu.HBM), spec(pltpu.HBM), spec(), spec(pl.ANY)],
         out_specs=[spec(), spec()],
         out_shape=[half_rows(out_rows(rows, False)), half_rows(C)],
         scratch_shapes=scratch(rows, "xdysr"),
+        input_output_aliases={3: 1},
         compiler_params=GRANT,
         name="mix_first",
-    )(meta, *(pltpu.with_memory_space_constraint(part, pltpu.HBM) for part in (x, d)), *pieces)
+    )(meta, *(pltpu.with_memory_space_constraint(part, pltpu.HBM) for part in (x, d)), begun, piece)
 
 
 def run_assemble(slot, meta, pieces):
@@ -354,7 +355,8 @@
     hot = jnp.pad(hot, ((0, 4), (0, 0))).T
     stem = own_first(jnp.pad(stem_weight.reshape(-1, C), ((0, 4), (0, 0))), co)
     level_rows, taps = run_first_half(rows, meta, hot, stem, params[0])
-    now, even_weights = run_second_half(rows, meta, level_rows, taps, pieces[0])
+    begun = run_assemble(0, meta, pieces[0][:3])
+    now, even_weights = run_second_half(rows, meta, level_rows, taps, begun, pieces[0][3])
     other = lax.ppermute(now, "co", [(0, 1), (1, 0)])
     odd_weights = run_assemble(1, meta, pieces[1])
     now = run_swapped_level(RUN // 2 + 8, 4, meta, now, other, params[1], odd_weights)

time: 220 us -> 226 us (1.027)
  local copies, waits for them, and re-layouts: 6.12 us -> 11.5 us
    unnamed x14 -> x30, local copies, waits for them, and re-layouts: 0.62 us -> 5.56 us
    pallas_call x1 -> x2, Pallas kernels: 4.25 us -> 7.57 us  [run_assemble(): pl.pallas_call(lambda *refs: assemble(slot, *refs), in_specs=[spec(pltpu....]
  transfers between devices with their start and end apart: 26 -> 26, of which waited for: 11 -> 11; matrix products, arithmetic and copies ran while one was open for 3% -> 3% of each run, Pallas kernels for 6% -> 8%
where the time goes in v8:
time: 226 us; the launch traced here: 225 us
  waiting for transfers between devices  70.3 us (31%)
  starting transfers between devices  54.5 us (24%)
  blocking collectives  43.9 us (19%)
  Pallas kernels  39.5 us (17%)
  local copies, waits for them, and re-layouts  11.5 us (5%)
  other arithmetic  4.32 us (2%)
    all_gather x1, blocking collectives, relay(): held = lax.all_gather(jnp.concatenate(held, axis=0), 'zh')  25.4 us
    ppermute x4, waiting for transfers between devices, relay(): kept = kept + lax.ppermute(now[2 * p:2 * p + 2], ('zh', 'co', 'x'), pairs)  22.2 us
    ppermute x4, waiting for transfers between devices, relay(): sides.append(lax.ppermute(near[slot], ('zh', 'zl'), ring(16, by)))  15 us
    all_to_all x1, starting transfers between devices, relay(): blocks = lax.all_to_all(blocks, ('co', 'y', 'x'), 0, 0, tiled=True)  12.8 us
    all_to_all x1, waiting for transfers between devices, relay(): blocks = lax.all_to_all(blocks, ('co', 'y', 'x'), 0, 0, tiled=True)  12.3 us
    ppermute x4, starting transfers between devices, relay(): sides.append(lax.ppermute(near[slot], ('zh', 'zl'), ring(16, by)))  10.8 us
    pallas_call x6, Pallas kernels, run_level(): pl.pallas_call(lambda *refs: paired_level(rows, edge, *refs), in_specs=[s...  10.2 us
    pallas_call x1, Pallas kernels, run_first_half(): pl.pallas_call(lambda *refs: first_half(rows, *refs), in_specs=[spec(pltp...  10 us
  transfers between devices with their start and end apart: 26, of which 11 were waited for; matrix products, arithmetic and copies ran while one was open for 3% of the time, Pallas kernels for 8%

profile of v8, /device:TPU:35, one launch (start us, length us, event | category | flops | bytes accessed | tf_op | source)
XLA Modules:
  0.0 224.8 jit_solution(11775637080916551547)
XLA Ops:
  0.1 1.0 maximum_maximum_fusion
  1.1 25.4 %all-gather = bf16[128,1536]{1,0:T(8,128)(2,1)S(1)} all-gather(bf16[32,1536]{1,0:T(8,128)(2,1)S(1)} %maximum_maximum_fusion), channel_id=2, replica_groups=mesh['zh'=4,'co'=2,'zl'=4,'y'=4,'x'=4] {'zh'}, dimensions={0}, use_global_device_ids=true | all-gather | bytes 491520 | tf_op jit(solution)/shard_map/all_gather | solution.py:321
  26.5 0.7 dynamic-slice_add_fusion
  27.8 0.7 collective-permute-start.1
  28.5 2.8 %collective-permute-start.2 = (s32[512]{0:T(512)S(1)}, s32[512]{0:T(512)S(1)}, u32[]{:S(2)}, u32[]{:S(2)}) collective-permute-start(s32[512]{0:T(512)S(1)} %bitcast.54), channel_id=1, source_target_pairs={{1,0},{5,4},{9,8},{13,12},{17,16},{21,20},{25,24},{29,28},{33,32},... | collective-permute-start | bytes 6152 | tf_op jit(solution)/shard_map/ppermute | solution.py:298
  32.1 1.2 broadcast_in_dim.7
  33.3 12.8 %all-to-all-start = ((bf16[32,24,768]{2,1,0:T(8,128)(2,1)}), bf16[32,24,768]{2,1,0:T(8,128)(2,1)S(1)}, u32[]{:S(2)}, u32[]{:S(2)}) async-start(bf16[32,24,768]{2,1,0:T(8,128)(2,1)} %bitcast.10), calls=%async_computation | async-start | bytes 2359296 | tf_op jit(solution)/shard_map/all_to_all | solution.py:327
  46.3 1.9 all_gather.54
  48.2 0.8 maximum_select_fusion.refs_2_
  50.5 12.3 %all-to-all-done = bf16[32,24,768]{2,1,0:T(8,128)(2,1)S(1)} async-done(((bf16[32,24,768]{2,1,0:T(8,128)(2,1)}), bf16[32,24,768]{2,1,0:T(8,128)(2,1)S(1)}, u32[]{:S(2)}, u32[]{:S(2)}) %all-to-all-start) | async-done | bytes 1179680 | tf_op jit(solution)/shard_map/all_to_all | solution.py:327
  62.8 3.7 %collective-permute-start.7 = (bf16[96,768]{1,0:T(8,128)(2,1)S(1)}, bf16[96,768]{1,0:T(8,128)(2,1)S(1)}, u32[]{:S(2)}, u32[]{:S(2)}) collective-permute-start(bf16[96,768]{1,0:T(8,128)(2,1)S(1)} %get-tuple-element.20), channel_id=1, source_target_pairs={{0,416},{16,432},{32,0},{48,16},{128,32},{144,48},{160,128},{176,1... | collective-permute-start | bytes 442376 | tf_op jit(solution)/shard_map/ppermute | solution.py:331
  66.5 2.5 %collective-permute-start.6 = (bf16[96,768]{1,0:T(8,128)(2,1)S(1)}, bf16[96,768]{1,0:T(8,128)(2,1)S(1)}, u32[]{:S(2)}, u32[]{:S(2)}) collective-permute-start(bf16[96,768]{1,0:T(8,128)(2,1)S(1)} %get-tuple-element.19), channel_id=1, source_target_pairs={{0,32},{16,48},{32,128},{48,144},{128,160},{144,176},{160,256},{17... | collective-permute-start | bytes 442376 | tf_op jit(solution)/shard_map/ppermute | solution.py:330
  69.6 1.0 copy.15
  70.6 0.9 collective-permute-done.7
  71.5 7.8 %collective-permute-done.6 = bf16[96,768]{1,0:T(8,128)(2,1)S(1)} collective-permute-done((bf16[96,768]{1,0:T(8,128)(2,1)S(1)}, bf16[96,768]{1,0:T(8,128)(2,1)S(1)}, u32[]{:S(2)}, u32[]{:S(2)}) %collective-permute-start.6) | collective-permute-done | bytes 147488 | tf_op jit(solution)/shard_map/ppermute | solution.py:330
  79.4 1.1 broadcast_in_dim.8
  80.5 3.5 %all-to-all-start.1 = ((bf16[4,2,96,768]{3,2,1,0:T(8,128)(2,1)}), bf16[4,2,96,768]{3,2,1,0:T(8,128)(2,1)S(1)}, u32[]{:S(2)}, u32[]{:S(2)}) async-start(bf16[4,2,96,768]{3,2,1,0:T(8,128)(2,1)} %broadcast_in_dim.8), calls=%async_computation.1 | async-start | bytes 2359296 | tf_op jit(solution)/shard_map/all_to_all | solution.py:275
  84.1 0.9 slice_bitcast_fusion
  85.0 2.0 collective-permute-start.4
  87.0 3.4 %collective-permute-start.5 = (bf16[4,96,768]{2,1,0:T(8,128)(2,1)S(1)}, bf16[4,96,768]{2,1,0:T(8,128)(2,1)S(1)}, u32[]{:S(2)}, u32[]{:S(2)}) collective-permute-start(bf16[4,96,768]{2,1,0:T(8,128)(2,1)S(1)} %get-tuple-element.18.refs_1_), channel_id=1, source_target_pairs={{0,432},{16,0},{32,16},{48,32},{128,48},{144,128},{160,144},{176,1... | collective-permute-start | bytes 1769480 | tf_op jit(solution)/shard_map/ppermute | solution.py:336
  90.5 0.8 fusion.refs_1_
  91.3 10.0 %stem_and_taps.1 = (bf16[1056,768]{1,0:T(8,128)(2,1)}, bf16[1056,1536]{1,0:T(8,128)(2,1)}) custom-call(s32[19]{0:T(128)} %pad_add_fusion.refs_0_, bf16[1056,64]{1,0:T(8,128)(2,1)} %fusion.refs_1_, bf16[64,1536]{1,0:T(8,128)(2,1)} %maximum_select_fusion.refs_2_, f32[8,1536]{1,0:T(8,128)} %get-tuple-element.28.refs_3_.refs_2_), custom_call_target="tpu_custom_call" | custom-call | tf_op jit(solution)/shard_map/stem_and_taps/pallas_call | solution.py:212
  101.4 0.9 copy-done.5
  102.3 1.1 collective-permute-done.5.refs_3_
  103.3 0.9 copy-done.7
  104.2 1.1 copy-done.1
  105.2 1.1 copy-done.6
  106.3 1.1 copy-done.8
  107.4 3.3 %assemble.2.refs_3_ = bf16[1536,768]{1,0:T(8,128)(2,1)S(1)} custom-call(s32[19]{0:T(128)S(1)} %copy-done.9, bf16[4,96,768]{2,1,0:T(8,128)(2,1)S(1)} %copy-done.1, bf16[4,96,768]{2,1,0:T(8,128)(2,1)S(1)} %copy-done.6, bf16[4,96,768]{2,1,0:T(8,128)(2,1)S(1)} %copy-done.8), custom_call_target="tpu_custom_call" | custom-call | tf_op jit(solution)/shard_map/assemble/pallas_call | solution.py:236
  110.7 6.7 %mix_first.1 = (bf16[528,768]{1,0:T(8,128)(2,1)S(1)}, bf16[1536,768]{1,0:T(8,128)(2,1)S(1)}) custom-call(s32[19]{0:T(128)S(1)} %copy-done.9, bf16[1056,768]{1,0:T(8,128)(2,1)} %get-tuple-element.13.refs_1_, bf16[1056,1536]{1,0:T(8,128)(2,1)} %get-tuple-element.14.refs_2_, bf16[1536,768]{1,0:T(8,128)(2,1)S(1)} %assemble.2.refs_3_, ...), custom_call_target="tpu_custom_call", output_to_operand_aliasing={{1}: (3, {})} | custom-call | tf_op jit(solution)/shard_map/mix_first/pallas_call | solution.py:223
  117.4 3.3 %collective-permute-start.8 = (bf16[528,768]{1,0:T(8,128)(2,1)S(1)}, bf16[528,768]{1,0:T(8,128)(2,1)S(1)}, u32[]{:S(2)}, u32[]{:S(2)}) collective-permute-start(bf16[528,768]{1,0:T(8,128)(2,1)S(1)} %get-tuple-element.15.refs_1_), channel_id=1, source_target_pairs={{0,64},{64,0},{1,65},{65,1},{2,66},{66,2},{3,67},{67,3},{4,68},{68... | collective-permute-start | bytes 2433032 | tf_op jit(solution)/shard_map/ppermute | solution.py:360
  120.7 2.1 collective-permute-start.9
  122.8 3.4 %collective-permute-start.10 = (bf16[4,96,768]{2,1,0:T(8,128)(2,1)S(1)}, bf16[4,96,768]{2,1,0:T(8,128)(2,1)S(1)}, u32[]{:S(2)}, u32[]{:S(2)}) collective-permute-start(bf16[4,96,768]{2,1,0:T(8,128)(2,1)S(1)} %copy-done.2), channel_id=1, source_target_pairs={{0,432},{16,0},{32,16},{48,32},{128,48},{144,128},{160,144},{176,1... | collective-permute-start | bytes 1769480 | tf_op jit(solution)/shard_map/ppermute | solution.py:336
  126.2 11.5 %collective-permute-done.9.refs_2_ = bf16[4,96,768]{2,1,0:T(8,128)(2,1)S(1)} collective-permute-done((bf16[4,96,768]{2,1,0:T(8,128)(2,1)S(1)}, bf16[4,96,768]{2,1,0:T(8,128)(2,1)S(1)}, u32[]{:S(2)}, u32[]{:S(2)}) %collective-permute-start.9) | collective-permute-done | bytes 589856 | tf_op jit(solution)/shard_map/ppermute | solution.py:336
  137.6 2.4 %collective-permute-done.10.refs_3_ = bf16[4,96,768]{2,1,0:T(8,128)(2,1)S(1)} collective-permute-done((bf16[4,96,768]{2,1,0:T(8,128)(2,1)S(1)}, bf16[4,96,768]{2,1,0:T(8,128)(2,1)S(1)}, u32[]{:S(2)}, u32[]{:S(2)}) %collective-permute-start.10) | collective-permute-done | bytes 589856 | tf_op jit(solution)/shard_map/ppermute | solution.py:336
  140.0 4.3 %assemble.3.refs_4_.refs_3_ = bf16[1536,768]{1,0:T(8,128)(2,1)S(1)} custom-call(s32[19]{0:T(128)S(1)} %copy-done.9, bf16[4,96,768]{2,1,0:T(8,128)(2,1)S(1)} %copy-done.2, bf16[4,96,768]{2,1,0:T(8,128)(2,1)S(1)} %collective-permute-done.9.refs_2_, bf16[4,96,768]{2,1,0:T(8,128)(2,1)S(1)} %collective-permute-done.10.refs_3_, ...), custom_call_target="tpu_custom_call" | custom-call | tf_op jit(solution)/shard_map/assemble/pallas_call | solution.py:236
  144.3 5.0 %shard_map.64 = bf16[256,768]{1,0:T(8,128)(2,1)S(1)} custom-call(s32[19]{0:T(128)S(1)} %copy-done.9, bf16[528,768]{1,0:T(8,128)(2,1)S(1)} %get-tuple-element.15.refs_1_, bf16[528,768]{1,0:T(8,128)(2,1)S(1)} %collective-permute-done.8.refs_2_, f32[8,1536]{1,0:T(8,128)S(1)} %copy-done.3, bf16[1536,768]{1,0:T(8,128)(2,1)S(1)} %assemble.3.refs_4_.refs_3_), custom_call_target="tpu_custom_call" | custom-call | tf_op jit(solution)/shard_map/pallas_call | solution.py:248
  149.3 1.4 collective-permute-start.12
  150.7 1.3 collective-permute-start.13
  152.0 1.3 collective-permute-start.11
  153.3 6.9 %collective-permute-done.13 = bf16[12,768]{1,0:T(8,128)(2,1)S(1)} collective-permute-done((bf16[12,768]{1,0:T(8,128)(2,1)S(1)}, bf16[12,768]{1,0:T(8,128)(2,1)S(1)}, u32[]{:S(2)}, u32[]{:S(2)}) %collective-permute-start.13) | collective-permute-done | bytes 18464 | tf_op jit(solution)/shard_map/ppermute | solution.py:308
  160.2 4.3 %collective-permute-done.11 = bf16[12,768]{1,0:T(8,128)(2,1)S(1)} collective-permute-done((bf16[12,768]{1,0:T(8,128)(2,1)S(1)}, bf16[12,768]{1,0:T(8,128)(2,1)S(1)}, u32[]{:S(2)}, u32[]{:S(2)}) %collective-permute-start.11) | collective-permute-done | bytes 18464 | tf_op jit(solution)/shard_map/ppermute | solution.py:307
  164.7 4.2 %all-gather.1 = bf16[576,768]{1,0:T(8,128)(2,1)S(1)} all-gather(bf16[288,768]{1,0:T(8,128)(2,1)S(1)} %pad_maximum_fusion), channel_id=3, replica_groups=mesh['zh'=4,'co'=2,'zl'=4,'y'=4,'x'=4] {'co'}, dimensions={0}, use_global_device_ids=true | all-gather | bytes 1327104 | tf_op jit(solution)/shard_map/all_gather | solution.py:365
  168.9 3.1 %shard_map.65 = bf16[144,768]{1,0:T(8,128)(2,1)S(1)} custom-call(s32[19]{0:T(128)S(1)} %copy-done.9, bf16[2,288,768]{2,1,0:T(8,128)(2,1)S(1)} %bitcast.37, f32[8,1536]{1,0:T(8,128)S(1)} %copy-done.4, bf16[1536,768]{1,0:T(8,128)(2,1)S(1)} %get-tuple-element.16.refs_3_), custom_call_target="tpu_custom_call" | custom-call | tf_op jit(solution)/shard_map/pallas_call | solution.py:259
  172.0 2.3 %all-gather.2 = bf16[288,768]{1,0:T(8,128)(2,1)S(1)} all-gather(bf16[144,768]{1,0:T(8,128)(2,1)S(1)} %shard_map.65), channel_id=4, replica_groups=mesh['zh'=4,'co'=2,'zl'=4,'y'=4,'x'=4] {'co'}, dimensions={0}, use_global_device_ids=true | all-gather | bytes 663552 | tf_op jit(solution)/shard_map/all_gather | solution.py:367
  174.3 1.8 shard_map.66
  176.1 1.3 collective-permute-start.15
  177.4 1.3 collective-permute-start.16
  178.7 1.3 collective-permute-start.14
  180.0 0.9 collective-permute-done.14
  181.0 2.6 %all-gather.3 = bf16[192,768]{1,0:T(8,128)(2,1)S(1)} all-gather(bf16[96,768]{1,0:T(8,128)(2,1)S(1)} %pad_maximum_fusion.2), channel_id=5, replica_groups=mesh['zh'=4,'co'=2,'zl'=4,'y'=4,'x'=4] {'co'}, dimensions={0}, use_global_device_ids=true | all-gather | bytes 442368 | tf_op jit(solution)/shard_map/all_gather | solution.py:365
  183.6 1.6 shard_map.67
  185.2 1.9 all-gather.4
  187.1 1.3 shard_map.68
  188.4 0.7 collective-permute-start.18
  189.1 0.7 collective-permute-start.19
  189.8 0.7 collective-permute-start.17
  190.5 1.9 all-gather.5
  192.4 1.3 shard_map.69
  193.8 1.8 all-gather.6
  195.6 1.1 shard_map.70
  198.8 1.3 collective-permute-start.21
  200.1 22.2 %collective-permute-done.21 = bf16[2,768]{1,0:T(2,128)(2,1)S(1)} collective-permute-done((bf16[2,768]{1,0:T(2,128)(2,1)S(1)}, bf16[2,768]{1,0:T(2,128)(2,1)S(1)}, u32[]{:S(2)}, u32[]{:S(2)}) %collective-permute-start.21) | collective-permute-done | bytes 3104 | tf_op jit(solution)/shard_map/ppermute | solution.py:380
  222.3 1.8 all-gather.8
  (100 shorter events, 6.9 us)
Async XLA Ops:
  27.2 23.3 %collective-permute-start = (s32[512]{0:T(512)S(1)}, s32[512]{0:T(512)S(1)}, u32[]{:S(2)}, u32[]{:S(2)}) collective-permute-start(s32[512]{0:T(512)S(1)} %bitcast.52), channel_id=1, source_target_pairs={{3,4},{7,8},{11,12},{15,16},{19,20},{23,24},{27,28},{31,32},{35,36... | collective-permute-start | bytes 6152 | tf_op jit(solution)/shard_map/ppermute | solution.py:298
  27.8 22.6 %collective-permute-start.1 = (s32[512]{0:T(512)S(1)}, s32[512]{0:T(512)S(1)}, u32[]{:S(2)}, u32[]{:S(2)}) collective-permute-start(s32[512]{0:T(512)S(1)} %bitcast.53), channel_id=1, source_target_pairs={{0,0},{4,4},{8,8},{12,12},{16,16},{20,20},{24,24},{28,28},{32,32},... | collective-permute-start | bytes 6152 | tf_op jit(solution)/shard_map/ppermute | solution.py:298
  28.5 22.0 %collective-permute-start.2 = (s32[512]{0:T(512)S(1)}, s32[512]{0:T(512)S(1)}, u32[]{:S(2)}, u32[]{:S(2)}) collective-permute-start(s32[512]{0:T(512)S(1)} %bitcast.54), channel_id=1, source_target_pairs={{1,0},{5,4},{9,8},{13,12},{17,16},{21,20},{25,24},{29,28},{33,32},... | collective-permute-start | bytes 6152 | tf_op jit(solution)/shard_map/ppermute | solution.py:298
  31.3 19.2 %collective-permute-start.3 = (s32[512]{0:T(512)S(1)}, s32[512]{0:T(512)S(1)}, u32[]{:S(2)}, u32[]{:S(2)}) collective-permute-start(s32[512]{0:T(512)S(1)} %bitcast.55), channel_id=1, source_target_pairs={{2,0},{6,4},{10,8},{14,12},{18,16},{22,20},{26,24},{30,28},{34,32}... | collective-permute-start | bytes 6152 | tf_op jit(solution)/shard_map/ppermute | solution.py:298
  33.3 12.8 %copy-start.12 = (s32[4]{0:T(128)S(1)}, s32[4]{0:T(128)}, u32[]{:S(2)}) copy-start(s32[4]{0:T(128)} %constant.115) | copy-start | bytes 52
  33.3 13.0 %copy-start.11 = (bf16[15,4,1536]{2,1,0:T(4,128)(2,1)S(1)}, bf16[15,4,1536]{2,1,0:T(4,128)(2,1)}, u32[]{:S(2)}) copy-start(bf16[15,4,1536]{2,1,0:T(4,128)(2,1)} %param.7) | copy-start | bytes 552964
  33.3 29.5 %all-to-all-start = ((bf16[32,24,768]{2,1,0:T(8,128)(2,1)}), bf16[32,24,768]{2,1,0:T(8,128)(2,1)S(1)}, u32[]{:S(2)}, u32[]{:S(2)}) async-start(bf16[32,24,768]{2,1,0:T(8,128)(2,1)} %bitcast.10), calls=%async_computation | async-start | bytes 2359296 | tf_op jit(solution)/shard_map/all_to_all | solution.py:327
  62.8 8.7 %collective-permute-start.7 = (bf16[96,768]{1,0:T(8,128)(2,1)S(1)}, bf16[96,768]{1,0:T(8,128)(2,1)S(1)}, u32[]{:S(2)}, u32[]{:S(2)}) collective-permute-start(bf16[96,768]{1,0:T(8,128)(2,1)S(1)} %get-tuple-element.20), channel_id=1, source_target_pairs={{0,416},{16,432},{32,0},{48,16},{128,32},{144,48},{160,128},{176,1... | collective-permute-start | bytes 442376 | tf_op jit(solution)/shard_map/ppermute | solution.py:331
  66.5 12.9 %collective-permute-start.6 = (bf16[96,768]{1,0:T(8,128)(2,1)S(1)}, bf16[96,768]{1,0:T(8,128)(2,1)S(1)}, u32[]{:S(2)}, u32[]{:S(2)}) collective-permute-start(bf16[96,768]{1,0:T(8,128)(2,1)S(1)} %get-tuple-element.19), channel_id=1, source_target_pairs={{0,32},{16,48},{32,128},{48,144},{128,160},{144,176},{160,256},{17... | collective-permute-start | bytes 442376 | tf_op jit(solution)/shard_map/ppermute | solution.py:330
  80.5 30.2 %all-to-all-start.1 = ((bf16[4,2,96,768]{3,2,1,0:T(8,128)(2,1)}), bf16[4,2,96,768]{3,2,1,0:T(8,128)(2,1)S(1)}, u32[]{:S(2)}, u32[]{:S(2)}) async-start(bf16[4,2,96,768]{3,2,1,0:T(8,128)(2,1)} %broadcast_in_dim.8), calls=%async_computation.1 | async-start | bytes 2359296 | tf_op jit(solution)/shard_map/all_to_all | solution.py:275
  84.1 6.3 %copy-start.10 = (s32[60,1056]{0,1:T(8,128)S(1)}, s32[60,1056]{0,1:T(8,128)}, u32[]{:S(2)}) copy-start(s32[60,1056]{0,1:T(8,128)} %copy.15) | copy-start | bytes 760324
  85.0 16.4 %copy-start = (bf16[4,96,768]{2,1,0:T(8,128)(2,1)}, bf16[4,96,768]{2,1,0:T(8,128)(2,1)S(1)}, u32[]{:S(2)}) copy-start(bf16[4,96,768]{2,1,0:T(8,128)(2,1)S(1)} %get-tuple-element.18.refs_1_) | copy-start | bytes 1769476
  85.0 19.2 %copy-start.9 = (s32[19]{0:T(128)S(1)}, s32[19]{0:T(128)}, u32[]{:S(2)}) copy-start(s32[19]{0:T(128)} %pad_add_fusion.refs_0_) | copy-start | bytes 232
  85.0 16.4 %collective-permute-start.4 = (bf16[4,96,768]{2,1,0:T(8,128)(2,1)S(1)}, bf16[4,96,768]{2,1,0:T(8,128)(2,1)S(1)}, u32[]{:S(2)}, u32[]{:S(2)}) collective-permute-start(bf16[4,96,768]{2,1,0:T(8,128)(2,1)S(1)} %get-tuple-element.18.refs_1_), channel_id=1, source_target_pairs={{0,16},{16,32},{32,48},{48,128},{128,144},{144,160},{160,176},{176... | collective-permute-start | bytes 1769480 | tf_op jit(solution)/shard_map/ppermute | solution.py:336
  87.0 16.3 %collective-permute-start.5 = (bf16[4,96,768]{2,1,0:T(8,128)(2,1)S(1)}, bf16[4,96,768]{2,1,0:T(8,128)(2,1)S(1)}, u32[]{:S(2)}, u32[]{:S(2)}) collective-permute-start(bf16[4,96,768]{2,1,0:T(8,128)(2,1)S(1)} %get-tuple-element.18.refs_1_), channel_id=1, source_target_pairs={{0,432},{16,0},{32,16},{48,32},{128,48},{144,128},{160,144},{176,1... | collective-permute-start | bytes 1769480 | tf_op jit(solution)/shard_map/ppermute | solution.py:336
  101.4 0.9 copy-start.5
  103.3 0.9 copy-start.7
  104.2 1.1 copy-start.1
  105.2 1.1 copy-start.6
  106.3 1.1 copy-start.8
  110.7 10.0 %copy-start.2 = (bf16[4,96,768]{2,1,0:T(8,128)(2,1)S(1)}, bf16[4,96,768]{2,1,0:T(8,128)(2,1)}, u32[]{:S(2)}) copy-start(bf16[4,96,768]{2,1,0:T(8,128)(2,1)} %get-tuple-element.17.refs_1_) | copy-start | bytes 1769476
  117.4 26.8 %collective-permute-start.8 = (bf16[528,768]{1,0:T(8,128)(2,1)S(1)}, bf16[528,768]{1,0:T(8,128)(2,1)S(1)}, u32[]{:S(2)}, u32[]{:S(2)}) collective-permute-start(bf16[528,768]{1,0:T(8,128)(2,1)S(1)} %get-tuple-element.15.refs_1_), channel_id=1, source_target_pairs={{0,64},{64,0},{1,65},{65,1},{2,66},{66,2},{3,67},{67,3},{4,68},{68... | collective-permute-start | bytes 2433032 | tf_op jit(solution)/shard_map/ppermute | solution.py:360
  120.7 23.6 %copy-start.3 = (f32[8,1536]{1,0:T(8,128)S(1)}, f32[8,1536]{1,0:T(8,128)}, u32[]{:S(2)}) copy-start(f32[8,1536]{1,0:T(8,128)} %get-tuple-element.27.refs_3_.refs_2_) | copy-start | bytes 147460
  120.7 16.9 %collective-permute-start.9 = (bf16[4,96,768]{2,1,0:T(8,128)(2,1)S(1)}, bf16[4,96,768]{2,1,0:T(8,128)(2,1)S(1)}, u32[]{:S(2)}, u32[]{:S(2)}) collective-permute-start(bf16[4,96,768]{2,1,0:T(8,128)(2,1)S(1)} %copy-done.2), channel_id=1, source_target_pairs={{0,16},{16,32},{32,48},{48,128},{128,144},{144,160},{160,176},{176... | collective-permute-start | bytes 1769480 | tf_op jit(solution)/shard_map/ppermute | solution.py:336
  122.8 17.2 %collective-permute-start.10 = (bf16[4,96,768]{2,1,0:T(8,128)(2,1)S(1)}, bf16[4,96,768]{2,1,0:T(8,128)(2,1)S(1)}, u32[]{:S(2)}, u32[]{:S(2)}) collective-permute-start(bf16[4,96,768]{2,1,0:T(8,128)(2,1)S(1)} %copy-done.2), channel_id=1, source_target_pairs={{0,432},{16,0},{32,16},{48,32},{128,48},{144,128},{160,144},{176,1... | collective-permute-start | bytes 1769480 | tf_op jit(solution)/shard_map/ppermute | solution.py:336
  149.3 19.6 %copy-start.4 = (f32[8,1536]{1,0:T(8,128)S(1)}, f32[8,1536]{1,0:T(8,128)}, u32[]{:S(2)}) copy-start(f32[8,1536]{1,0:T(8,128)} %get-tuple-element.28.refs_3_.refs_2_) | copy-start | bytes 147460
  149.3 15.3 %collective-permute-start.12 = (bf16[256,768]{1,0:T(8,128)(2,1)S(1)}, bf16[256,768]{1,0:T(8,128)(2,1)S(1)}, u32[]{:S(2)}, u32[]{:S(2)}) collective-permute-start(bf16[256,768]{1,0:T(8,128)(2,1)S(1)} %shard_map.64), channel_id=1, source_target_pairs={{0,1},{4,5},{8,9},{12,13},{16,17},{20,21},{24,25},{28,29},{32,33},... | collective-permute-start | bytes 1179656 | tf_op jit(solution)/shard_map/ppermute | solution.py:309
  150.7 9.5 %collective-permute-start.13 = (bf16[12,768]{1,0:T(8,128)(2,1)S(1)}, bf16[12,768]{1,0:T(8,128)(2,1)S(1)}, u32[]{:S(2)}, u32[]{:S(2)}) collective-permute-start(bf16[12,768]{1,0:T(8,128)(2,1)S(1)} %get-tuple-element.22), channel_id=1, source_target_pairs={{128,1},{4,129},{132,5},{8,133},{136,9},{12,137},{140,13},{16,141}... | collective-permute-start | bytes 55304 | tf_op jit(solution)/shard_map/ppermute | solution.py:308
  152.0 12.5 %collective-permute-start.11 = (bf16[12,768]{1,0:T(8,128)(2,1)S(1)}, bf16[12,768]{1,0:T(8,128)(2,1)S(1)}, u32[]{:S(2)}, u32[]{:S(2)}) collective-permute-start(bf16[12,768]{1,0:T(8,128)(2,1)S(1)} %get-tuple-element.21), channel_id=1, source_target_pairs={{0,129},{128,5},{4,133},{132,9},{8,137},{136,13},{12,141},{140,17}... | collective-permute-start | bytes 55304 | tf_op jit(solution)/shard_map/ppermute | solution.py:307
  176.1 4.8 %collective-permute-start.15 = (bf16[64,768]{1,0:T(8,128)(2,1)S(1)}, bf16[64,768]{1,0:T(8,128)(2,1)S(1)}, u32[]{:S(2)}, u32[]{:S(2)}) collective-permute-start(bf16[64,768]{1,0:T(8,128)(2,1)S(1)} %shard_map.66), channel_id=1, source_target_pairs={{1,2},{5,6},{9,10},{13,14},{17,18},{21,22},{25,26},{29,30},{33,34}... | collective-permute-start | bytes 294920 | tf_op jit(solution)/shard_map/ppermute | solution.py:309
  177.4 2.6 %collective-permute-start.16 = (bf16[12,768]{1,0:T(8,128)(2,1)S(1)}, bf16[12,768]{1,0:T(8,128)(2,1)S(1)}, u32[]{:S(2)}, u32[]{:S(2)}) collective-permute-start(bf16[12,768]{1,0:T(8,128)(2,1)S(1)} %get-tuple-element.26), channel_id=1, source_target_pairs={{129,2},{5,130},{133,6},{9,134},{137,10},{13,138},{141,14},{17,142... | collective-permute-start | bytes 55304 | tf_op jit(solution)/shard_map/ppermute | solution.py:308
  178.7 2.2 collective-permute-start.14
  188.4 2.1 collective-permute-start.18
  189.1 1.3 collective-permute-start.19
  189.8 0.7 collective-permute-start.17
  196.8 3.3 %collective-permute-start.23 = (bf16[2,768]{1,0:T(2,128)(2,1)S(1)}, bf16[2,768]{1,0:T(2,128)(2,1)S(1)}, u32[]{:S(2)}, u32[]{:S(2)}) collective-permute-start(bf16[2,768]{1,0:T(2,128)(2,1)S(1)} %get-tuple-element.49), channel_id=1, source_target_pairs={{3,129},{67,385},{131,131},{195,387},{259,193},{323,449},{387,195}... | collective-permute-start | bytes 9224 | tf_op jit(solution)/shard_map/ppermute | solution.py:380
  197.4 2.7 %collective-permute-start.22 = (bf16[2,768]{1,0:T(2,128)(2,1)S(1)}, bf16[2,768]{1,0:T(2,128)(2,1)S(1)}, u32[]{:S(2)}, u32[]{:S(2)}) collective-permute-start(bf16[2,768]{1,0:T(2,128)(2,1)S(1)} %get-tuple-element.48), channel_id=1, source_target_pairs={{3,128},{67,384},{131,130},{195,386},{259,192},{323,448},{387,194}... | collective-permute-start | bytes 9224 | tf_op jit(solution)/shard_map/ppermute | solution.py:380
  198.1 2.0 collective-permute-start.20
  198.8 23.5 %collective-permute-start.21 = (bf16[2,768]{1,0:T(2,128)(2,1)S(1)}, bf16[2,768]{1,0:T(2,128)(2,1)S(1)}, u32[]{:S(2)}, u32[]{:S(2)}) collective-permute-start(bf16[2,768]{1,0:T(2,128)(2,1)S(1)} %get-tuple-element.49), channel_id=1, source_target_pairs={{3,1},{67,257},{131,3},{195,259},{259,65},{323,321},{387,67},{451,... | collective-permute-start | bytes 9224 | tf_op jit(solution)/shard_map/ppermute | solution.py:380
